TPU v7x, 32 devices: a whole 2x2x4 slice. The times are simulated.
32 devices in a mesh: echo: 2 (over y), gx: 4 (over z), gy: 2 (over x), gz: 2 (over core).
Axes of the slice: x: 2, y: 2, z: 4, core: 2. Of those that a mesh axis runs over, the one named last changes fastest.
Arguments:
- measured: bfloat16 [2, 32, 8, 16, 32], P(None, 'echo', 'gx', 'gy', 'gz'), parts along dimension 1, may hold values from -6 to 6
- sample_mask: int32 [16, 16, 32], P(('echo', 'gx'), 'gy', 'gz'), parts along dimension 0, may hold values 0 or 1
- kernel: bfloat16 [2, 5, 5, 5, 512], replicated, may hold values from -0.0625 to 0.0625
Outputs:
- spirit_kspace: bfloat16 [2, 32, 8, 16, 32], P(None, 'echo', 'gx', 'gy', 'gz'), parts along dimension 1
There are 2 independent parts, one for each index of `echo`. A program takes and returns all parts, laid end to end along the dimension named above; an argument that names none is the same for every part. Nothing has to cross between parts.
All inputs are finite; a program needn't handle non-finite values. No bound on the sum of `sample_mask` on one device may be relied on, other than what follows from the above.
Results may differ from a plain program's by a relative error of at most 0.0016.
Values may be sent and summed in bfloat16 or wider, within the bound.
No kernel may reach another device: no remote copies, remote signals or barrier semaphores. Data moves between devices by JAX's collectives and lax.ppermute only.
A program may use at most 128 MiB of HBM per device.

v0:
```python
import functools

import jax
import jax.numpy as jnp
from jax import lax
from jax.experimental import pallas as pl
from jax.experimental.pallas import tpu as pltpu
from jax.sharding import PartitionSpec as P

COILS = 16
KS = 5
ITERS = 2
SPACE = ("gx", "gy", "gz")
UNSAMPLED = 2.0 ** 100
LIMIT = 2.0 ** 99


def iota(shape, dim):
    return lax.broadcasted_iota(jnp.int32, shape, dim)


def one_hot(flags):
    return jnp.where(flags, 1.0, 0.0).astype(jnp.bfloat16)


def dot(a, b):
    return jnp.dot(a, b, preferred_element_type=jnp.float32)


def dot_nt(a, b):
    return lax.dot_general(a, b, (((1,), (1,)), ((), ())), preferred_element_type=jnp.float32)


def pack_kernel(measured_ref, mask_ref, packed_ref):
    parts, coils, size_x, size_y, size_z = measured_ref.shape
    lanes = size_y * size_z
    rows = parts * coils * size_y
    repeat = one_hot(iota((size_z, lanes), 1) % size_z == iota((size_z, lanes), 0))
    own_y = iota((rows, lanes), 1) // size_z == iota((rows, lanes), 0) % size_y
    gather = one_hot(iota((parts * coils, rows), 1) // size_y == iota((parts * coils, rows), 0))
    for x in range(size_x):
        values = measured_ref[:, :, x].astype(jnp.float32)
        sampled = (mask_ref[x] == 1)[None, None]
        coded = jnp.where(sampled, values, UNSAMPLED).reshape(rows, size_z).astype(jnp.bfloat16)
        spread = jnp.where(own_y, dot(coded, repeat), 0.0).astype(jnp.bfloat16)
        packed_ref[x * parts * coils : (x + 1) * parts * coils] = dot(gather, spread).astype(jnp.bfloat16)


def grid_kernel(sizes, blocks_ref, own_ref, taps_ref, place_ref, out_ref, flat, table, padded, coded):
    count_x, count_y, count_z = sizes
    parts, coils, local_x, local_y, local_z = out_ref.shape
    size_x, size_y, size_z = count_x * local_x, count_y * local_y, count_z * local_z
    channels = parts * coils
    width = size_x * channels
    reach = KS // 2
    taps = KS ** 3
    group = 128 // channels

    pair = 2 * coils
    per_tile = 128 // pair
    lane = iota((128, 256), 1)
    source = (lane // 128) * coils + lane % coils
    for c in range(coils):
        pick = one_hot(iota((128, 256), 0) == (c % per_tile) * pair + source)
        tile = (c // per_tile) * 128
        spread = dot(taps_ref[:, tile : tile + 128], pick)
        for half in range(2):
            rows_of_coil = pl.ds(c, taps_ref.shape[0], stride=coils)
            flat[half, rows_of_coil, :] = spread[:, half * 128 : half * 128 + 128]

    imaginary = iota((coils, 128), 1) // coils % 2 == 1
    lane_group = iota((channels, 128), 1) // channels

    def add_taps(step, carry):
        dy, dz = step // KS, step % KS
        for half in range(2):
            mats = []
            for dx in range(KS):
                tap = (dx * KS + dy) * KS + dz
                real_at = pl.multiple_of(tap * coils, coils)
                imag_at = pl.multiple_of((taps + tap) * coils, coils)
                real = flat[half, pl.ds(real_at, coils), :]
                imag = flat[half, pl.ds(imag_at, coils), :]
                if half == 0:
                    top = jnp.where(imaginary, -imag, real)
                    low = jnp.where(imaginary, real, imag)
                else:
                    top = jnp.where(imaginary, imag, real)
                    low = jnp.where(imaginary, -real, imag)
                mats.append(jnp.concatenate([top, low], axis=0).astype(jnp.bfloat16))
            known = {}
            zero = jnp.zeros((channels, 128), jnp.bfloat16)
            for x_out in range(size_x):
                for j in range(width // 128):
                    at = [j * group + g for g in range(group)]
                    if half == 1:
                        at = [size_x - 1 - a for a in at]
                    which = tuple(a - x_out + reach if 0 <= a - x_out + reach < KS else -1 for a in at)
                    if which not in known:
                        block = zero
                        for g, dx in enumerate(which):
                            if dx >= 0:
                                block = jnp.where(lane_group == g, mats[dx], block)
                        known[which] = block
                    start = pl.multiple_of(dz * 2 * width + half * width + j * 128, 128)
                    table[dy, x_out * channels : (x_out + 1) * channels, pl.ds(start, 128)] = known[which]
        return carry

    lax.fori_loop(0, KS * KS, add_taps, 0)

    half_rows = local_y * size_z
    row, col = iota((half_rows, half_rows), 0), iota((half_rows, half_rows), 1)
    block_size = local_y * local_z
    row_at = row // size_z * local_z + row % local_z + row % size_z // local_z * block_size
    order = one_hot(row_at == col)
    padded[: reach * size_z] = jnp.zeros((reach * size_z, padded.shape[1]), jnp.bfloat16)
    padded[(reach + size_y) * size_z :] = jnp.zeros((reach * size_z, padded.shape[1]), jnp.bfloat16)
    for gy in range(count_y):
        field = jnp.concatenate(
            [
                jnp.concatenate([blocks_ref[(gx * count_y + gy) * count_z + gz] for gz in range(count_z)], axis=1)
                for gx in range(count_x)
            ],
            axis=0,
        )
        coded[gy * half_rows : (gy + 1) * half_rows] = dot_nt(order, field)

    def spread(current):
        for dz in range(KS):
            shift = dz - reach
            inside = (row % size_z + shift >= 0) & (row % size_z + shift < size_z)
            direct = one_hot(inside & (col == row + shift))
            mirror = one_hot(inside & (half_rows - 1 - col == row + shift))
            for gy in range(count_y):
                values = current[gy]
                there = count_y - 1 - gy
                low = dz * 2 * width
                at = reach * size_z + gy * half_rows
                padded[at : at + half_rows, low : low + width] = dot(direct, values).astype(jnp.bfloat16)
                at = reach * size_z + there * half_rows
                padded[at : at + half_rows, low + width : low + 2 * width] = dot(mirror, values).astype(jnp.bfloat16)

    def known_values(gy):
        return coded[gy * half_rows : (gy + 1) * half_rows]

    current = []
    for gy in range(count_y):
        values = known_values(gy)
        current.append(jnp.where(values < LIMIT, values, 0.0).astype(jnp.bfloat16))
    for iteration in range(ITERS - 1):
        spread(current)
        total = jnp.zeros((size_y * size_z, width), jnp.float32)
        for dy in range(KS):
            total = total + dot_nt(padded[dy * size_z : (dy + size_y) * size_z], table[dy])
        current = []
        for gy in range(count_y):
            values = known_values(gy)
            part = total[gy * half_rows : (gy + 1) * half_rows]
            current.append(jnp.where(values < LIMIT, values, part).astype(jnp.bfloat16))
    spread(current)
    at_x, at_y, at_z = place_ref[0], place_ref[1], place_ref[2]
    own_rows = local_x * channels
    total = jnp.zeros((own_rows, local_y * local_z), jnp.float32)
    for dy in range(KS):
        pieces = []
        for y in range(local_y):
            start = pl.multiple_of((at_y * local_y + y + dy) * size_z + at_z * local_z, local_z)
            pieces.append(padded[pl.ds(start, local_z), :])
        window = jnp.concatenate(pieces, axis=0)
        weights = table[dy, pl.ds(pl.multiple_of(at_x * own_rows, own_rows), own_rows), :]
        total = total + dot_nt(weights, window)
    own = own_ref[...].astype(jnp.float32)
    result = jnp.where(own < LIMIT, own, total).astype(jnp.bfloat16)
    rows, lanes = channels * local_y, local_y * local_z
    unfold = one_hot(iota((rows, channels), 0) // local_y == iota((rows, channels), 1))
    own_y = iota((rows, lanes), 1) // local_z == iota((rows, lanes), 0) % local_y
    fold = one_hot(iota((lanes, local_z), 0) % local_z == iota((lanes, local_z), 1))
    for x in range(local_x):
        spread_out = dot(unfold, result[x * channels : (x + 1) * channels])
        spread_out = jnp.where(own_y, spread_out, 0.0).astype(jnp.bfloat16)
        values = dot(spread_out, fold).reshape(parts, coils, local_y, local_z)
        out_ref[:, :, x] = values.astype(jnp.bfloat16)


def gathered_body(measured, sample_mask, kernel):
    parts, coils, local_x, local_y, local_z = measured.shape
    sizes = tuple(lax.axis_size(axis) for axis in SPACE)
    devices = sizes[0] * sizes[1] * sizes[2]
    channels = parts * coils
    packed = pl.pallas_call(
        pack_kernel,
        out_shape=jax.ShapeDtypeStruct((local_x * channels, local_y * local_z), jnp.bfloat16),
        name="pack",
    )(measured, sample_mask)
    blocks = lax.all_to_all(jnp.broadcast_to(packed[None], (devices,) + packed.shape), SPACE, 0, 0)
    taps = kernel.reshape(parts * KS ** 3, coils * 2 * coils)
    taps = jnp.pad(taps, ((0, -taps.shape[0] % 16), (0, 0)))
    place = jnp.stack([lax.axis_index(axis) for axis in SPACE]).astype(jnp.int32)
    size_x, size_y, size_z = sizes[0] * local_x, sizes[1] * local_y, sizes[2] * local_z
    width = size_x * channels
    return pl.pallas_call(
        functools.partial(grid_kernel, sizes),
        out_shape=jax.ShapeDtypeStruct(measured.shape, jnp.bfloat16),
        in_specs=[pl.BlockSpec(memory_space=pltpu.VMEM)] * 3 + [pl.BlockSpec(memory_space=pltpu.SMEM)],
        out_specs=pl.BlockSpec(memory_space=pltpu.VMEM),
        scratch_shapes=[
            pltpu.VMEM((2, taps.shape[0] * coils, 128), jnp.float32),
            pltpu.VMEM((KS, width, 2 * KS * width), jnp.bfloat16),
            pltpu.VMEM(((size_y + 2 * (KS // 2)) * size_z, 2 * KS * width), jnp.bfloat16),
            pltpu.VMEM((size_y * size_z, width), jnp.float32),
        ],
        name="grid",
    )(blocks, packed, taps, place)


def partner(block, axis, bit):
    count = lax.axis_size(axis)
    route = []
    for low in range(count):
        high = low | 1 << bit
        if high != low and high < count:
            route += [(low, high), (high, low)]
    return lax.ppermute(block, axis, route)


def padded_2(shard, sides, width):
    for axis, dim in sides:
        size, length = (lax.axis_size(axis), shard.shape[dim])
        up = [(i, (i + 1) % size) for i in range(size - 1)]
        down = [(j, i) for i, j in up]
        last = lax.slice_in_dim(shard, length - width, length, axis=dim)
        leading = lax.slice_in_dim(shard, 0, width, axis=dim)
        before = lax.ppermute(last, axis, up)
        after = lax.ppermute(leading, axis, down)
        shard = jnp.concatenate([before, shard, after], axis=dim)
    return shard


def unpack_kernel(kernel):
    shaped = kernel.reshape(2, KS, KS, KS, COILS, 2 * COILS)
    return jnp.transpose(shaped, (0, 4, 5, 1, 2, 3))


def tap_matrix(kernel_part):
    real_part = kernel_part[0]
    imag_part = kernel_part[1]
    upper_rows = jnp.concatenate([real_part, -imag_part], axis=1)
    lower_rows = jnp.concatenate([imag_part, real_part], axis=1)
    blocks = jnp.concatenate([upper_rows, lower_rows], axis=0)
    return jnp.transpose(blocks, (2, 3, 0, 4, 1))


def conjugate(values):
    return jnp.concatenate([values[:1], -values[1:]], axis=0)


def convolve(padded, tap_table):
    extent = tap_table.shape[0]
    channel_count = padded.shape[0] * padded.shape[1]
    channels = padded.reshape((channel_count,) + padded.shape[2:])
    size_x = channels.shape[1] - extent + 1
    size_y = channels.shape[2] - extent + 1
    size_z = channels.shape[3] - extent + 1
    out_rows = tap_table.shape[2]
    running = jnp.zeros((out_rows, size_x * size_y * size_z), jnp.float32)
    for offset_x in range(extent):
        for offset_y in range(extent):
            pieces = [
                channels[
                    :,
                    offset_x : offset_x + size_x,
                    offset_y : offset_y + size_y,
                    offset_z : offset_z + size_z,
                ]
                for offset_z in range(extent)
            ]
            stacked = jnp.stack(pieces).reshape(extent * channel_count, size_x * size_y * size_z)
            weights = tap_table[offset_x, offset_y].reshape(out_rows, extent * channel_count)
            running = running + jnp.dot(weights, stacked, preferred_element_type=jnp.float32)
    return running.reshape(2, out_rows // 2, size_x, size_y, size_z)


def mirror_state(values):
    values = values[:, :, ::-1, ::-1, ::-1]
    for bit_place in range(lax.axis_size(("gx", "gy", "gz")).bit_length() - 1):
        values = partner(values, ("gx", "gy", "gz"), bit_place)
    return values


def halo_body(measured, sample_mask, kernel):
    kernel = unpack_kernel(kernel)
    reach = kernel.shape[-1] // 2
    sampled = (sample_mask == 1)[None, None]
    current = jnp.where(sampled, measured, jnp.zeros_like(measured))
    tap_table = tap_matrix(kernel)
    for iteration in range(ITERS):
        joined = jnp.concatenate([current, conjugate(mirror_state(current))], axis=1)
        padded = padded_2(joined, (("gx", 2), ("gy", 3), ("gz", 4)), reach)
        convolved = convolve(padded, tap_table)
        current = jnp.where(sampled, measured.astype(jnp.float32), convolved).astype(jnp.bfloat16)
    return current


def solution(mesh):
    grid = tuple(mesh.shape[axis] for axis in SPACE)
    spec = P(None, "echo", "gx", "gy", "gz")

    def body(measured, sample_mask, kernel):
        parts, coils, local_x, local_y, local_z = measured.shape
        width = grid[0] * local_x * parts * coils
        small = width == 256 and grid[1] == 2 and grid[1] * local_y * grid[2] * local_z <= 512
        if small:
            return gathered_body(measured, sample_mask, kernel)
        return halo_body(measured, sample_mask, kernel)

    return jax.shard_map(
        body,
        mesh=mesh,
        in_specs=(spec, P(("echo", "gx"), "gy", "gz"), P()),
        out_specs=spec,
        check_vma=False,
    )
```

profile of v0, /device:TPU:0, one launch (start us, length us, event | category | flops | bytes accessed | tf_op | source)
XLA Modules:
  0.0 36.7 jit_solution(10326259863473897604)
XLA Ops:
  0.0 1.9 %pack.1.own_ref = bf16[64,128]{1,0:T(8,128)(2,1)} custom-call(bf16[2,16,2,8,16]{4,3,2,1,0:T(8,128)(2,1)} %measured_ref.1, s32[2,8,16]{2,1,0:T(8,128)} %mask_ref.1), custom_call_target="tpu_custom_call" | custom-call | tf_op jit(solution)/shard_map/pack/pallas_call | solution.py:190
  1.9 1.5 %broadcast_in_dim.2 = bf16[16,64,128]{2,1,0:T(8,128)(2,1)} broadcast(bf16[64,128]{1,0:T(8,128)(2,1)} %pack.1.own_ref), dimensions={1,2} | broadcast | bytes 278528 | tf_op jit(solution)/shard_map/broadcast_in_dim | solution.py:195
  3.4 0.0 copy-start.1
  3.4 7.5 %all-to-all-start = ((bf16[16,64,128]{2,1,0:T(8,128)(2,1)}), bf16[16,64,128]{2,1,0:T(8,128)(2,1)S(1)}, u32[]{:S(2)}, u32[]{:S(2)}) async-start(bf16[16,64,128]{2,1,0:T(8,128)(2,1)} %broadcast_in_dim.2), calls=%async_computation | async-start | bytes 524288 | tf_op jit(solution)/shard_map/all_to_all | solution.py:195
  10.9 0.0 copy-done.1
  11.0 0.1 reshape.4
  11.1 0.7 %pad.4.taps_ref = bf16[256,512]{1,0:T(8,128)(2,1)} pad(bf16[250,512]{1,0:T(8,128)(2,1)S(1)} %reshape.4, bf16[]{:T(256)} %constant.10.clone.1), padding=0_6x0_0 | pad | bytes 518146 | tf_op jit(solution)/shard_map/jit(_pad)/pad | solution.py:197
  11.8 0.7 %pad_add_fusion.place_ref = s32[3]{0:T(128)} fusion(s32[1]{0:T(128)} %bitcast.2, s32[1]{0:T(128)} %bitcast.1, s32[1]{0:T(128)} %bitcast), kind=kLoop, calls=%fused_computation | loop fusion | flops 6 | bytes 24 | tf_op jit(solution)/shard_map/stack | solution.py:198
  12.5 8.5 %all-to-all-done.blocks_ref = bf16[16,64,128]{2,1,0:T(8,128)(2,1)S(1)} async-done(((bf16[16,64,128]{2,1,0:T(8,128)(2,1)}), bf16[16,64,128]{2,1,0:T(8,128)(2,1)S(1)}, u32[]{:S(2)}, u32[]{:S(2)}) %all-to-all-start) | async-done | bytes 262176 | tf_op jit(solution)/shard_map/all_to_all | solution.py:195
  20.9 0.0 copy-start
  20.9 0.7 %copy-done = bf16[16,64,128]{2,1,0:T(8,128)(2,1)} copy-done((bf16[16,64,128]{2,1,0:T(8,128)(2,1)}, bf16[16,64,128]{2,1,0:T(8,128)(2,1)S(1)}, u32[]{:S(2)}) %copy-start) | copy-done | bytes 262168
  21.6 15.1 %grid.1 = bf16[2,16,2,8,16]{4,3,2,1,0:T(8,128)(2,1)} custom-call(bf16[16,64,128]{2,1,0:T(8,128)(2,1)} %copy-done, bf16[64,128]{1,0:T(8,128)(2,1)} %pack.1.own_ref, bf16[256,512]{1,0:T(8,128)(2,1)} %pad.4.taps_ref, s32[3]{0:T(128)} %pad_add_fusion.place_ref), custom_call_target="tpu_custom_call" | custom-call | tf_op jit(solution)/shard_map/grid/pallas_call | solution.py:201
  (1 shorter events, 0.0 us)
Async XLA Ops:
  3.4 7.5 %copy-start.1 = (bf16[2,5,5,5,512]{4,0,3,2,1:T(2,128)(2,1)S(1)}, bf16[2,5,5,5,512]{4,0,3,2,1:T(2,128)(2,1)}, u32[]{:S(2)}) copy-start(bf16[2,5,5,5,512]{4,0,3,2,1:T(2,128)(2,1)} %param.5) | copy-start | bytes 768004
  3.4 17.5 %all-to-all-start = ((bf16[16,64,128]{2,1,0:T(8,128)(2,1)}), bf16[16,64,128]{2,1,0:T(8,128)(2,1)S(1)}, u32[]{:S(2)}, u32[]{:S(2)}) async-start(bf16[16,64,128]{2,1,0:T(8,128)(2,1)} %broadcast_in_dim.2), calls=%async_computation | async-start | bytes 524288 | tf_op jit(solution)/shard_map/all_to_all | solution.py:195
  20.9 0.7 %copy-start = (bf16[16,64,128]{2,1,0:T(8,128)(2,1)}, bf16[16,64,128]{2,1,0:T(8,128)(2,1)S(1)}, u32[]{:S(2)}) copy-start(bf16[16,64,128]{2,1,0:T(8,128)(2,1)S(1)} %all-to-all-done.blocks_ref) | copy-start | bytes 786436
where the time goes:
time: 37.1 us; the launch traced here: 36.7 us
  Pallas kernels  17 us (46%)
  waiting for transfers between devices  8.46 us (23%)
  starting transfers between devices  7.52 us (20%)
  local copies, waits for them, and re-layouts  3.02 us (8%)
  other arithmetic  0.65 us (2%)
    pallas_call x1, Pallas kernels, gathered_body(): pl.pallas_call(functools.partial(grid_kernel, sizes), out_shape=jax.Shape...  15.1 us
    all_to_all x1, waiting for transfers between devices, gathered_body(): lax.all_to_all(jnp.broadcast_to(packed[None], (devices,) + packed.shape),...  8.46 us
    all_to_all x1, starting transfers between devices, gathered_body(): lax.all_to_all(jnp.broadcast_to(packed[None], (devices,) + packed.shape),...  7.52 us
    pallas_call x1, Pallas kernels, gathered_body(): pl.pallas_call(pack_kernel, out_shape=jax.ShapeDtypeStruct((local_x * cha...  1.94 us
    broadcast_in_dim x1, local copies, waits for them, and re-layouts, gathered_body(): jnp.broadcast_to(packed[None], (devices,) + packed.shape)  1.46 us
  transfers between devices with their start and end apart: 1, of which 1 were waited for; matrix products, arithmetic and copies ran while one was open for 4% of the time, Pallas kernels for 0%

commit v1 on v0

v1 whole, which is shorter than its diff:
```python
import functools

import jax
import jax.numpy as jnp
from jax import lax
from jax.experimental import pallas as pl
from jax.experimental.pallas import tpu as pltpu
from jax.sharding import PartitionSpec as P

COILS = 16
KS = 5
REACH = KS // 2
ITERS = 2
SPACE = ("gx", "gy", "gz")
UNSAMPLED = 2.0 ** 100
LIMIT = 2.0 ** 99
VMEM_LIMIT = 16 * 2 ** 20


def iota(shape, dim):
    return lax.broadcasted_iota(jnp.int32, shape, dim)


def one_hot(flags):
    return jnp.where(flags, 1.0, 0.0).astype(jnp.bfloat16)


def dot(a, b):
    return jnp.dot(a, b, preferred_element_type=jnp.float32)


def dot_nt(a, b):
    return lax.dot_general(a, b, (((1,), (1,)), ((), ())), preferred_element_type=jnp.float32)


def pack_kernel(measured_hbm, mask_hbm, packed_ref, measured_ref, mask_ref, sems):
    copies = [
        pltpu.make_async_copy(measured_hbm, measured_ref, sems.at[0]),
        pltpu.make_async_copy(mask_hbm, mask_ref, sems.at[1]),
    ]
    for copy in copies:
        copy.start()
    parts, coils, size_x, size_y, size_z = measured_ref.shape
    lanes = size_y * size_z
    rows = parts * coils * size_y
    repeat = one_hot(iota((size_z, lanes), 1) % size_z == iota((size_z, lanes), 0))
    own_y = iota((rows, lanes), 1) // size_z == iota((rows, lanes), 0) % size_y
    gather = one_hot(iota((parts * coils, rows), 1) // size_y == iota((parts * coils, rows), 0))
    for copy in copies:
        copy.wait()
    for x in range(size_x):
        values = measured_ref[:, :, x].astype(jnp.float32)
        sampled = (mask_ref[x] == 1)[None, None]
        coded = jnp.where(sampled, values, UNSAMPLED).reshape(rows, size_z).astype(jnp.bfloat16)
        spread = jnp.where(own_y, dot(coded, repeat), 0.0).astype(jnp.bfloat16)
        packed_ref[x * parts * coils : (x + 1) * parts * coils] = dot(gather, spread).astype(jnp.bfloat16)


def flat_kernel(taps_ref, flat):
    coils = COILS
    pair = 2 * coils
    per_tile = 128 // pair
    lane = iota((128, 256), 1)
    source = (lane // 128) * coils + lane % coils
    for c in range(coils):
        pick = one_hot(iota((128, 256), 0) == (c % per_tile) * pair + source)
        tile = (c // per_tile) * 128
        spread = dot(taps_ref[:, tile : tile + 128], pick)
        for half in range(2):
            rows_of_coil = pl.ds(c, taps_ref.shape[0], stride=coils)
            flat[half, rows_of_coil, :] = spread[:, half * 128 : half * 128 + 128]


def table_kernel(first_dy, size_x, flat, table):
    coils = COILS
    channels = 2 * coils
    width = size_x * channels
    taps = KS ** 3
    group = 128 // channels
    imaginary = iota((coils, 128), 1) // coils % 2 == 1
    lane_group = iota((channels, 128), 1) // channels

    def add_taps(step, carry):
        dy, dz = step // KS, step % KS
        for half in range(2):
            mats = []
            for dx in range(KS):
                tap = (dx * KS + dy + first_dy) * KS + dz
                real_at = pl.multiple_of(tap * coils, coils)
                imag_at = pl.multiple_of((taps + tap) * coils, coils)
                real = flat[half, pl.ds(real_at, coils), :]
                imag = flat[half, pl.ds(imag_at, coils), :]
                if half == 0:
                    top = jnp.where(imaginary, -imag, real)
                    low = jnp.where(imaginary, real, imag)
                else:
                    top = jnp.where(imaginary, imag, real)
                    low = jnp.where(imaginary, -real, imag)
                mats.append(jnp.concatenate([top, low], axis=0).astype(jnp.bfloat16))
            known = {}
            zero = jnp.zeros((channels, 128), jnp.bfloat16)
            for x_out in range(size_x):
                for j in range(width // 128):
                    at = [j * group + g for g in range(group)]
                    if half == 1:
                        at = [size_x - 1 - a for a in at]
                    which = tuple(a - x_out + REACH if 0 <= a - x_out + REACH < KS else -1 for a in at)
                    if which not in known:
                        block = zero
                        for g, dx in enumerate(which):
                            if dx >= 0:
                                block = jnp.where(lane_group == g, mats[dx], block)
                        known[which] = block
                    lanes = slice(half * width + j * 128, half * width + j * 128 + 128)
                    table[dy, dz, x_out * channels : (x_out + 1) * channels, lanes] = known[which]
        return carry

    lax.fori_loop(0, table.shape[0] * KS, add_taps, 0)


def order_kernel(local_y, local_z, size_z, order):
    rows = local_y * size_z
    row, col = iota((rows, rows), 0), iota((rows, rows), 1)

    def block_order(at):
        return at // size_z * local_z + at % local_z + at % size_z // local_z * (local_y * local_z)

    order[:rows] = one_hot(block_order(row) == col)
    order[rows : 2 * rows] = one_hot(block_order(rows - 1 - row) == col)
    order[2 * rows :] = one_hot(rows - 1 - row == col)


def grid_kernel(sizes, blocks_ref, measured_ref, mask_ref, order_ref, place_ref, *refs):
    tables, (out_ref, padded, coded) = refs[:-3], refs[-3:]
    table = [(ref, dy) for ref in tables for dy in range(ref.shape[0])]
    count_x, count_y, count_z = sizes
    parts, coils, local_x, local_y, local_z = out_ref.shape
    size_x, size_y, size_z = count_x * local_x, count_y * local_y, count_z * local_z
    channels = parts * coils
    width = size_x * channels
    at_x, at_y, at_z = place_ref[0], place_ref[1], place_ref[2]
    half_rows = local_y * size_z
    top = REACH * size_z

    def rows_of(gy):
        return slice(top + gy * half_rows, top + (gy + 1) * half_rows)

    edge = jnp.zeros((top, 2 * width), jnp.bfloat16)
    padded[:top] = edge
    padded[top + size_y * size_z :] = edge
    for gy in range(count_y):
        field = jnp.concatenate(
            [
                jnp.concatenate(
                    [
                        blocks_ref[((at_z ^ gz) * count_y + (at_y ^ gy)) * count_x + (at_x ^ gx)]
                        for gz in range(count_z)
                    ],
                    axis=1,
                )
                for gx in range(count_x)
            ],
            axis=0,
        )
        both = dot_nt(order_ref[: 2 * half_rows], field)
        coded[gy * half_rows : (gy + 1) * half_rows] = both[:half_rows]
        both = jnp.where(both < LIMIT, both, 0.0).astype(jnp.bfloat16)
        padded[rows_of(gy), :width] = both[:half_rows]
        padded[rows_of(count_y - 1 - gy), width:] = both[half_rows:]

    z_at = iota((size_y * size_z, width), 0) % size_z
    for iteration in range(ITERS - 1):
        total = None
        for dz in range(KS):
            part = None
            for dy, (ref, at) in enumerate(table):
                term = dot_nt(padded[dy * size_z : (dy + size_y) * size_z], ref[at, dz])
                part = term if part is None else part + term
            shift = dz - REACH
            if shift != 0:
                part = pltpu.roll(part, -shift % part.shape[0], 0)
                part = jnp.where((z_at + shift >= 0) & (z_at + shift < size_z), part, 0.0)
            total = part if total is None else total + part
        for gy in range(count_y):
            values = coded[gy * half_rows : (gy + 1) * half_rows]
            part = total[gy * half_rows : (gy + 1) * half_rows]
            values = jnp.where(values < LIMIT, values, part).astype(jnp.bfloat16)
            padded[rows_of(gy), :width] = values
            padded[rows_of(count_y - 1 - gy), width:] = dot(order_ref[2 * half_rows :], values).astype(jnp.bfloat16)

    own_rows = local_x * channels
    start_x = pl.multiple_of(at_x * own_rows, own_rows)
    result = None
    for dy, (ref, at) in enumerate(table):
        weights = jnp.concatenate([ref[at, dz, pl.ds(start_x, own_rows), :] for dz in range(KS)], axis=0)
        start = pl.multiple_of((at_y * local_y + dy) * size_z, size_z)
        term = dot_nt(weights, padded[pl.ds(start, half_rows), :])
        result = term if result is None else result + term
    z_at = iota((own_rows, half_rows), 1) % size_z
    total = None
    for dz in range(KS):
        part = result[dz * own_rows : (dz + 1) * own_rows]
        shift = dz - REACH
        if shift != 0:
            part = pltpu.roll(part, -shift % half_rows, 1)
            part = jnp.where((z_at + shift >= 0) & (z_at + shift < size_z), part, 0.0)
        total = part if total is None else total + part
    total = total.astype(jnp.bfloat16)

    rows = channels * local_y
    unfold = one_hot(iota((rows, channels), 0) // local_y == iota((rows, channels), 1))
    own_y = iota((rows, half_rows), 1) // size_z == iota((rows, half_rows), 0) % local_y
    fold = one_hot(iota((half_rows, local_z), 0) % size_z == at_z * local_z + iota((half_rows, local_z), 1))
    for x in range(local_x):
        spread_out = dot(unfold, total[x * channels : (x + 1) * channels])
        spread_out = jnp.where(own_y, spread_out, 0.0).astype(jnp.bfloat16)
        values = dot(spread_out, fold).reshape(parts, coils, local_y, local_z)
        sampled = (mask_ref[x] == 1)[None, None]
        values = jnp.where(sampled, measured_ref[:, :, x].astype(jnp.float32), values)
        out_ref[:, :, x] = values.astype(jnp.bfloat16)


def swap(block, axis, bit):
    count = lax.axis_size(axis)
    return lax.ppermute(block, axis, [(i, i ^ bit) for i in range(count)])


def gathered_body(measured, sample_mask, kernel):
    parts, coils, local_x, local_y, local_z = measured.shape
    sizes = tuple(lax.axis_size(axis) for axis in SPACE)
    devices = sizes[0] * sizes[1] * sizes[2]
    channels = parts * coils
    size_x, size_y, size_z = sizes[0] * local_x, sizes[1] * local_y, sizes[2] * local_z
    width = size_x * channels
    half_rows = local_y * size_z
    in_vmem = pl.BlockSpec(memory_space=pltpu.VMEM)
    in_hbm = pl.BlockSpec(memory_space=pltpu.HBM)

    def call(kernel_fn, name, out_shape, in_specs, scratch=(), limit=VMEM_LIMIT, cost=2 ** 22):
        return pl.pallas_call(
            kernel_fn,
            out_shape=out_shape,
            in_specs=in_specs,
            out_specs=in_vmem,
            scratch_shapes=list(scratch),
            compiler_params=pltpu.CompilerParams(vmem_limit_bytes=limit),
            cost_estimate=pl.CostEstimate(flops=0, bytes_accessed=cost, transcendentals=0),
            name=name,
        )

    packed = call(
        pack_kernel,
        "pack",
        jax.ShapeDtypeStruct((local_x * channels, local_y * local_z), jnp.bfloat16),
        [in_hbm, in_hbm],
        [
            pltpu.VMEM(measured.shape, measured.dtype),
            pltpu.VMEM(sample_mask.shape, sample_mask.dtype),
            pltpu.SemaphoreType.DMA((2,)),
        ],
    )(*[pltpu.with_memory_space_constraint(a, pltpu.HBM) for a in (measured, sample_mask)])

    def after(arrived, *work):
        return lax.optimization_barrier((arrived,) + work)

    taps = kernel.reshape(parts * KS ** 3, coils * 2 * coils)
    taps = jnp.pad(taps, ((0, -taps.shape[0] % 16), (0, 0)))
    place = jnp.stack([lax.axis_index(axis) for axis in SPACE]).astype(jnp.int32)
    steps = [(axis, 1 << bit) for axis in SPACE for bit in range(lax.axis_size(axis).bit_length() - 1)]
    blocks = packed[None]
    tables, order = [], None
    for number, (axis, bit) in enumerate(steps):
        arrived = swap(blocks, axis, bit)
        if number == 0:
            arrived, taps, place = after(arrived, taps, place)
        elif number == 1:
            flat_shape = jax.ShapeDtypeStruct((2, taps.shape[0] * coils, 128), jnp.float32)
            arrived, flat = after(arrived, call(flat_kernel, "flat", flat_shape, [in_vmem])(taps))
        elif number == 2:
            table_shape = jax.ShapeDtypeStruct((KS, KS, width, 2 * width), jnp.bfloat16)
            table = call(functools.partial(table_kernel, 0, size_x), "table", table_shape, [in_vmem])(flat)
            order_shape = jax.ShapeDtypeStruct((3 * half_rows, half_rows), jnp.bfloat16)
            order = call(functools.partial(order_kernel, local_y, local_z, size_z), "order", order_shape, [])()
            arrived, table, order = after(arrived, table, order)
            tables.append(table)
        blocks = jnp.concatenate([blocks, arrived], axis=0)

    return call(
        functools.partial(grid_kernel, sizes),
        "grid",
        jax.ShapeDtypeStruct(measured.shape, jnp.bfloat16),
        [in_vmem] * 4 + [pl.BlockSpec(memory_space=pltpu.SMEM)] + [in_vmem] * len(tables),
        [
            pltpu.VMEM(((size_y + 2 * REACH) * size_z, 2 * width), jnp.bfloat16),
            pltpu.VMEM((size_y * size_z, width), jnp.float32),
        ],
    )(blocks, measured, sample_mask, order, place, *tables)


def partner(block, axis, bit):
    count = lax.axis_size(axis)
    route = []
    for low in range(count):
        high = low | 1 << bit
        if high != low and high < count:
            route += [(low, high), (high, low)]
    return lax.ppermute(block, axis, route)


def padded_2(shard, sides, width):
    for axis, dim in sides:
        size, length = (lax.axis_size(axis), shard.shape[dim])
        up = [(i, (i + 1) % size) for i in range(size - 1)]
        down = [(j, i) for i, j in up]
        last = lax.slice_in_dim(shard, length - width, length, axis=dim)
        leading = lax.slice_in_dim(shard, 0, width, axis=dim)
        before = lax.ppermute(last, axis, up)
        after = lax.ppermute(leading, axis, down)
        shard = jnp.concatenate([before, shard, after], axis=dim)
    return shard


def unpack_kernel(kernel):
    shaped = kernel.reshape(2, KS, KS, KS, COILS, 2 * COILS)
    return jnp.transpose(shaped, (0, 4, 5, 1, 2, 3))


def tap_matrix(kernel_part):
    real_part = kernel_part[0]
    imag_part = kernel_part[1]
    upper_rows = jnp.concatenate([real_part, -imag_part], axis=1)
    lower_rows = jnp.concatenate([imag_part, real_part], axis=1)
    blocks = jnp.concatenate([upper_rows, lower_rows], axis=0)
    return jnp.transpose(blocks, (2, 3, 0, 4, 1))


def conjugate(values):
    return jnp.concatenate([values[:1], -values[1:]], axis=0)


def convolve(padded, tap_table):
    extent = tap_table.shape[0]
    channel_count = padded.shape[0] * padded.shape[1]
    channels = padded.reshape((channel_count,) + padded.shape[2:])
    size_x = channels.shape[1] - extent + 1
    size_y = channels.shape[2] - extent + 1
    size_z = channels.shape[3] - extent + 1
    out_rows = tap_table.shape[2]
    running = jnp.zeros((out_rows, size_x * size_y * size_z), jnp.float32)
    for offset_x in range(extent):
        for offset_y in range(extent):
            pieces = [
                channels[
                    :,
                    offset_x : offset_x + size_x,
                    offset_y : offset_y + size_y,
                    offset_z : offset_z + size_z,
                ]
                for offset_z in range(extent)
            ]
            stacked = jnp.stack(pieces).reshape(extent * channel_count, size_x * size_y * size_z)
            weights = tap_table[offset_x, offset_y].reshape(out_rows, extent * channel_count)
            running = running + jnp.dot(weights, stacked, preferred_element_type=jnp.float32)
    return running.reshape(2, out_rows // 2, size_x, size_y, size_z)


def mirror_state(values):
    values = values[:, :, ::-1, ::-1, ::-1]
    for bit_place in range(lax.axis_size(("gx", "gy", "gz")).bit_length() - 1):
        values = partner(values, ("gx", "gy", "gz"), bit_place)
    return values


def halo_body(measured, sample_mask, kernel):
    kernel = unpack_kernel(kernel)
    reach = kernel.shape[-1] // 2
    sampled = (sample_mask == 1)[None, None]
    current = jnp.where(sampled, measured, jnp.zeros_like(measured))
    tap_table = tap_matrix(kernel)
    for iteration in range(ITERS):
        joined = jnp.concatenate([current, conjugate(mirror_state(current))], axis=1)
        padded = padded_2(joined, (("gx", 2), ("gy", 3), ("gz", 4)), reach)
        convolved = convolve(padded, tap_table)
        current = jnp.where(sampled, measured.astype(jnp.float32), convolved).astype(jnp.bfloat16)
    return current


def solution(mesh):
    grid = tuple(mesh.shape[axis] for axis in SPACE)
    spec = P(None, "echo", "gx", "gy", "gz")

    def body(measured, sample_mask, kernel):
        parts, coils, local_x, local_y, local_z = measured.shape
        width = grid[0] * local_x * parts * coils
        small = width == 256 and grid[1] == 2 and local_y * grid[2] * local_z == 256
        if small:
            return gathered_body(measured, sample_mask, kernel)
        return halo_body(measured, sample_mask, kernel)

    return jax.shard_map(
        body,
        mesh=mesh,
        in_specs=(spec, P(("echo", "gx"), "gy", "gz"), P()),
        out_specs=spec,
        check_vma=False,
    )
```

time: 37.1 us -> 24.6 us (0.66)
  waiting for transfers between devices: 8.46 us -> 3.15 us
  Pallas kernels: 17 us -> 12 us
  local copies, waits for them, and re-layouts: 3.02 us -> 1.19 us
  other arithmetic: 0.65 us -> 0.11 us
  starting transfers between devices: 7.52 us -> 7.95 us
    all_to_all x1 -> x0, waiting for transfers between devices: 8.46 us -> none  [gathered_body(): lax.all_to_all(jnp.broadcast_to(packed[None], (devices,) + packed.shape),...]
    ppermute x0 -> x4, starting transfers between devices: none -> 7.95 us  [swap(): return lax.ppermute(block, axis, [(i, i ^ bit) for i in range(count)])]
    all_to_all x1 -> x0, starting transfers between devices: 7.52 us -> none  [gathered_body(): lax.all_to_all(jnp.broadcast_to(packed[None], (devices,) + packed.shape),...]
    pallas_call x2 -> x5, Pallas kernels: 17 us -> 12 us  [the longest x1 7.35 us: gathered_body(): call(functools.partial(grid_kernel, sizes), 'grid', jax.ShapeDtypeStruct(...]
    ppermute x0 -> x4, waiting for transfers between devices: none -> 3.15 us  [swap(): return lax.ppermute(block, axis, [(i, i ^ bit) for i in range(count)])]
    broadcast_in_dim x1 -> x0, local copies, waits for them, and re-layouts: 1.46 us -> none  [gathered_body(): jnp.broadcast_to(packed[None], (devices,) + packed.shape)]
    pad x1, local copies, waits for them, and re-layouts: 0.71 us -> 0.02 us  [gathered_body(): taps = jnp.pad(taps, ((0, -taps.shape[0] % 16), (0, 0)))]
    another operation x1, other arithmetic: 0.65 us -> 0.08 us  [gathered_body(): jnp.stack([lax.axis_index(axis) for axis in SPACE]).astype(jnp.int32)]
  transfers between devices with their start and end apart: 1 -> 4, of which waited for: 1 -> 3; matrix products, arithmetic and copies ran while one was open for 4% -> 5% of each run, Pallas kernels for 0% -> 13%
where the time goes in v1:
time: 24.6 us; the launch traced here: 24.5 us
  Pallas kernels  12 us (49%)
  starting transfers between devices  7.95 us (32%)
  waiting for transfers between devices  3.15 us (13%)
  local copies, waits for them, and re-layouts  1.19 us (5%)
    ppermute x4, starting transfers between devices, swap(): return lax.ppermute(block, axis, [(i, i ^ bit) for i in range(count)])  7.95 us
    pallas_call x1, Pallas kernels, gathered_body(): call(functools.partial(grid_kernel, sizes), 'grid', jax.ShapeDtypeStruct(...  7.35 us
    ppermute x4, waiting for transfers between devices, swap(): return lax.ppermute(block, axis, [(i, i ^ bit) for i in range(count)])  3.15 us
    pallas_call x1, Pallas kernels, gathered_body(): call(flat_kernel, 'flat', flat_shape, [in_vmem])(taps)  1.85 us
    pallas_call x1, Pallas kernels, gathered_body(): call(pack_kernel, 'pack', jax.ShapeDtypeStruct((local_x * channels, local...  1.36 us
    pallas_call x1, Pallas kernels, gathered_body(): call(functools.partial(table_kernel, 0, size_x), 'table', table_shape, [i...  1.24 us
    unnamed x9, local copies, waits for them, and re-layouts  1.04 us
  transfers between devices with their start and end apart: 4, of which 3 were waited for; matrix products, arithmetic and copies ran while one was open for 5% of the time, Pallas kernels for 13%

profile of v1, /device:TPU:0, one launch (start us, length us, event | category | flops | bytes accessed | tf_op | source)
XLA Modules:
  0.0 24.5 jit_solution(16509087387189469377)
XLA Ops:
  0.0 1.4 %pack.1 = bf16[64,128]{1,0:T(8,128)(2,1)S(1)} custom-call(bf16[2,16,2,8,16]{4,3,2,1,0:T(8,128)(2,1)} %measured_ref.1, s32[2,8,16]{2,1,0:T(8,128)} %mask_ref.1), custom_call_target="tpu_custom_call" | custom-call | bytes 4194304 | tf_op jit(solution)/shard_map/pack/pallas_call | solution.py:251
  1.4 3.1 %collective-permute-start = (bf16[1,64,128]{2,1,0:T(8,128)(2,1)S(1)}, bf16[1,64,128]{2,1,0:T(8,128)(2,1)S(1)}, u32[]{:S(2)}, u32[]{:S(2)}) collective-permute-start(bf16[1,64,128]{2,1,0:T(8,128)(2,1)S(1)} %bitcast.5), channel_id=1, source_target_pairs={{0,4},{4,0},{8,12},{12,8},{1,5},{5,1},{9,13},{13,9},{2,6},{6,2},{1... | collective-permute-start | bytes 49160 | tf_op jit(solution)/shard_map/ppermute | solution.py:225
  4.5 0.1 pad_add_fusion.place_ref
  4.6 1.0 %copy.5 = bf16[2,5,5,5,512]{4,3,2,1,0:T(8,128)(2,1)S(1)} copy(bf16[2,5,5,5,512]{4,0,3,2,1:T(2,128)(2,1)} %param.5) | data formatting | bytes 512000 | tf_op args[2]
  5.6 0.1 reshape.3
  5.7 0.5 %collective-permute-done = bf16[1,64,128]{2,1,0:T(8,128)(2,1)S(1)} collective-permute-done((bf16[1,64,128]{2,1,0:T(8,128)(2,1)S(1)}, bf16[1,64,128]{2,1,0:T(8,128)(2,1)S(1)}, u32[]{:S(2)}, u32[]{:S(2)}) %collective-permute-start) | collective-permute-done | bytes 16416 | tf_op jit(solution)/shard_map/ppermute | solution.py:225
  6.2 3.0 %collective-permute-start.1 = (bf16[2,64,128]{2,1,0:T(8,128)(2,1)S(1)}, bf16[2,64,128]{2,1,0:T(8,128)(2,1)S(1)}, u32[]{:S(2)}, u32[]{:S(2)}) collective-permute-start(bf16[2,64,128]{2,1,0:T(8,128)(2,1)S(1)} %pad_maximum_fusion.2), channel_id=1, source_target_pairs={{0,8},{4,12},{8,0},{12,4},{1,9},{5,13},{9,1},{13,5},{2,10},{6,14},... | collective-permute-start | bytes 98312 | tf_op jit(solution)/shard_map/ppermute | solution.py:225
  9.2 0.2 order.1.order_ref
  9.4 1.9 %flat.1 = f32[2,4096,128]{2,1,0:T(8,128)S(1)} custom-call(bf16[256,512]{1,0:T(8,128)(2,1)S(1)} %pad.4.taps_ref), custom_call_target="tpu_custom_call" | custom-call | bytes 4194304 | tf_op jit(solution)/shard_map/flat/pallas_call | solution.py:278
  11.3 0.0 copy-start
  11.3 0.0 copy-start.1
  11.3 0.0 collective-permute-done.1
  11.3 1.7 %collective-permute-start.2 = (bf16[4,64,128]{2,1,0:T(8,128)(2,1)S(1)}, bf16[4,64,128]{2,1,0:T(8,128)(2,1)S(1)}, u32[]{:S(2)}, u32[]{:S(2)}) collective-permute-start(bf16[4,64,128]{2,1,0:T(8,128)(2,1)S(1)} %pad_maximum_fusion.1), channel_id=1, source_target_pairs={{0,2},{2,0},{1,3},{3,1},{4,6},{6,4},{5,7},{7,5},{8,10},{10,8},{9,1... | collective-permute-start | bytes 196616 | tf_op jit(solution)/shard_map/ppermute | solution.py:225
  13.0 1.2 %table.1.refs_0_ = bf16[5,5,256,512]{3,2,1,0:T(8,128)(2,1)S(1)} custom-call(f32[2,4096,128]{2,1,0:T(8,128)S(1)} %flat.1), custom_call_target="tpu_custom_call" | custom-call | bytes 4194304 | tf_op jit(solution)/shard_map/table/pallas_call | solution.py:281
  14.3 1.3 %collective-permute-done.2 = bf16[4,64,128]{2,1,0:T(8,128)(2,1)S(1)} collective-permute-done((bf16[4,64,128]{2,1,0:T(8,128)(2,1)S(1)}, bf16[4,64,128]{2,1,0:T(8,128)(2,1)S(1)}, u32[]{:S(2)}, u32[]{:S(2)}) %collective-permute-start.2) | collective-permute-done | bytes 65568 | tf_op jit(solution)/shard_map/ppermute | solution.py:225
  15.7 0.1 collective-permute-start.3
  15.8 1.3 %collective-permute-done.3 = bf16[8,64,128]{2,1,0:T(8,128)(2,1)S(1)} collective-permute-done((bf16[8,64,128]{2,1,0:T(8,128)(2,1)S(1)}, bf16[8,64,128]{2,1,0:T(8,128)(2,1)S(1)}, u32[]{:S(2)}, u32[]{:S(2)}) %collective-permute-start.3) | collective-permute-done | bytes 131104 | tf_op jit(solution)/shard_map/ppermute | solution.py:225
  17.1 0.0 copy-done
  17.1 0.0 copy-done.1
  17.1 7.3 %grid.1 = bf16[2,16,2,8,16]{4,3,2,1,0:T(8,128)(2,1)} custom-call(bf16[16,64,128]{2,1,0:T(8,128)(2,1)S(1)} %constant_dynamic-update-slice_fusion.blocks_ref, bf16[2,16,2,8,16]{4,3,2,1,0:T(8,128)(2,1)S(1)} %copy-done, s32[2,8,16]{2,1,0:T(8,128)S(1)} %copy-done.1, bf16[768,256]{1,0:T(8,128)(2,1)S(1)} %order.1.order_ref, s32[3]{0:T(128)S(1)} %pad_add_fusion.place_ref, ...), custom_call_target="tpu_custom_call" | custom-call | bytes 4194304 | tf_op jit(solution)/shard_map/grid/pallas_call | solution.py:288
  (9 shorter events, 0.1 us)
Async XLA Ops:
  1.4 4.8 %collective-permute-start = (bf16[1,64,128]{2,1,0:T(8,128)(2,1)S(1)}, bf16[1,64,128]{2,1,0:T(8,128)(2,1)S(1)}, u32[]{:S(2)}, u32[]{:S(2)}) collective-permute-start(bf16[1,64,128]{2,1,0:T(8,128)(2,1)S(1)} %bitcast.5), channel_id=1, source_target_pairs={{0,4},{4,0},{8,12},{12,8},{1,5},{5,1},{9,13},{13,9},{2,6},{6,2},{1... | collective-permute-start | bytes 49160 | tf_op jit(solution)/shard_map/ppermute | solution.py:225
  6.2 5.1 %collective-permute-start.1 = (bf16[2,64,128]{2,1,0:T(8,128)(2,1)S(1)}, bf16[2,64,128]{2,1,0:T(8,128)(2,1)S(1)}, u32[]{:S(2)}, u32[]{:S(2)}) collective-permute-start(bf16[2,64,128]{2,1,0:T(8,128)(2,1)S(1)} %pad_maximum_fusion.2), channel_id=1, source_target_pairs={{0,8},{4,12},{8,0},{12,4},{1,9},{5,13},{9,1},{13,5},{2,10},{6,14},... | collective-permute-start | bytes 98312 | tf_op jit(solution)/shard_map/ppermute | solution.py:225
  11.3 5.8 %copy-start = (bf16[2,16,2,8,16]{4,3,2,1,0:T(8,128)(2,1)S(1)}, bf16[2,16,2,8,16]{4,3,2,1,0:T(8,128)(2,1)}, u32[]{:S(2)}) copy-start(bf16[2,16,2,8,16]{4,3,2,1,0:T(8,128)(2,1)} %measured_ref.1) | copy-start | bytes 49156
  11.3 5.8 %copy-start.1 = (s32[2,8,16]{2,1,0:T(8,128)S(1)}, s32[2,8,16]{2,1,0:T(8,128)}, u32[]{:S(2)}) copy-start(s32[2,8,16]{2,1,0:T(8,128)} %mask_ref.1) | copy-start | bytes 3076
  11.3 4.3 %collective-permute-start.2 = (bf16[4,64,128]{2,1,0:T(8,128)(2,1)S(1)}, bf16[4,64,128]{2,1,0:T(8,128)(2,1)S(1)}, u32[]{:S(2)}, u32[]{:S(2)}) collective-permute-start(bf16[4,64,128]{2,1,0:T(8,128)(2,1)S(1)} %pad_maximum_fusion.1), channel_id=1, source_target_pairs={{0,2},{2,0},{1,3},{3,1},{4,6},{6,4},{5,7},{7,5},{8,10},{10,8},{9,1... | collective-permute-start | bytes 196616 | tf_op jit(solution)/shard_map/ppermute | solution.py:225
  15.7 1.4 %collective-permute-start.3 = (bf16[8,64,128]{2,1,0:T(8,128)(2,1)S(1)}, bf16[8,64,128]{2,1,0:T(8,128)(2,1)S(1)}, u32[]{:S(2)}, u32[]{:S(2)}) collective-permute-start(bf16[8,64,128]{2,1,0:T(8,128)(2,1)S(1)} %pad_maximum_fusion), channel_id=1, source_target_pairs={{0,1},{1,0},{2,3},{3,2},{4,5},{5,4},{6,7},{7,6},{8,9},{9,8},{10,11... | collective-permute-start | bytes 393224 | tf_op jit(solution)/shard_map/ppermute | solution.py:225

commit v2 on v1

--- a/solution.py
+++ b/solution.py
@@ -71,11 +71,18 @@
             flat[half, rows_of_coil, :] = spread[:, half * 128 : half * 128 + 128]
 
 
-def table_kernel(first_dy, size_x, flat, table):
+def write_orders(order):
+    rows = order.shape[1]
+    row, col = iota((rows, rows), 0), iota((rows, rows), 1)
+    order[:rows] = one_hot(row == col)
+    order[rows:] = one_hot(rows - 1 - row == col)
+
+
+def table_kernel(size_x, flat, table, order):
+    write_orders(order)
     coils = COILS
     channels = 2 * coils
     width = size_x * channels
-    taps = KS ** 3
     group = 128 // channels
     imaginary = iota((coils, 128), 1) // coils % 2 == 1
     lane_group = iota((channels, 128), 1) // channels
@@ -85,9 +92,9 @@
         for half in range(2):
             mats = []
             for dx in range(KS):
-                tap = (dx * KS + dy + first_dy) * KS + dz
-                real_at = pl.multiple_of(tap * coils, coils)
-                imag_at = pl.multiple_of((taps + tap) * coils, coils)
+                tap = (dx * KS + dy) * KS + dz
+                real_at = pl.multiple_of(2 * tap * coils, coils)
+                imag_at = pl.multiple_of((2 * tap + 1) * coils, coils)
                 real = flat[half, pl.ds(real_at, coils), :]
                 imag = flat[half, pl.ds(imag_at, coils), :]
                 if half == 0:
@@ -118,103 +125,108 @@
     lax.fori_loop(0, table.shape[0] * KS, add_taps, 0)
 
 
-def order_kernel(local_y, local_z, size_z, order):
-    rows = local_y * size_z
-    row, col = iota((rows, rows), 0), iota((rows, rows), 1)
-
-    def block_order(at):
-        return at // size_z * local_z + at % local_z + at % size_z // local_z * (local_y * local_z)
-
-    order[:rows] = one_hot(block_order(row) == col)
-    order[rows : 2 * rows] = one_hot(block_order(rows - 1 - row) == col)
-    order[2 * rows :] = one_hot(rows - 1 - row == col)
-
-
-def grid_kernel(sizes, blocks_ref, measured_ref, mask_ref, order_ref, place_ref, *refs):
-    tables, (out_ref, padded, coded) = refs[:-3], refs[-3:]
-    table = [(ref, dy) for ref in tables for dy in range(ref.shape[0])]
-    count_x, count_y, count_z = sizes
+def load_half(sizes, blocks_ref, order_ref, place_ref, local_z, coded, points, mirrored):
+    count_x, count_y, _ = sizes
+    rows = order_ref.shape[1]
+    edge = REACH * local_z
+    field = jnp.concatenate(
+        [
+            jnp.concatenate(
+                [blocks_ref[(place_ref[1] ^ gy) * count_x + (place_ref[0] ^ gx)] for gy in range(count_y)], axis=1
+            )
+            for gx in range(count_x)
+        ],
+        axis=0,
+    )
+    both = dot_nt(order_ref[...], field)
+    coded[...] = both[:rows]
+    both = jnp.where(both < LIMIT, both, 0.0).astype(jnp.bfloat16)
+    for ref, values in ((points, both[:rows]), (mirrored, both[rows:])):
+        ref[:edge] = jnp.zeros((edge, ref.shape[1]), jnp.bfloat16)
+        ref[edge + rows :] = jnp.zeros((edge, ref.shape[1]), jnp.bfloat16)
+        ref[edge : edge + rows] = values
+
+
+def y_taps(ref, rows, local_z, weights):
+    total = None
+    for dy in range(KS):
+        term = dot_nt(ref[dy * local_z : dy * local_z + rows], weights(dy))
+        total = term if total is None else total + term
+    return total
+
+
+def near_kernel(sizes, local_z, blocks_ref, order_ref, place_ref, table, partial, coded, points, mirrored):
+    rows, width = coded.shape
+    load_half(sizes, blocks_ref, order_ref, place_ref, local_z, coded, points, mirrored)
+    for dz in range(KS):
+        partial[0, dz] = y_taps(points, rows, local_z, lambda dy: table[dy, dz, :, :width])
+        partial[1, dz] = y_taps(mirrored, rows, local_z, lambda dy: table[dy, dz, :, width:])
+
+
+def shift_z(own, other, shift, local_z, dim, own_first):
+    length = own.shape[dim]
+    inside = iota(own.shape, dim) % local_z + shift
+    inside = (inside >= 0) & (inside < local_z)
+    across = pltpu.roll(other, (local_z - shift if shift > 0 else -local_z - shift) % length, dim)
+    keep = own_first if shift > 0 else 1.0 - own_first
+    return jnp.where(inside, pltpu.roll(own, -shift % length, dim), across * keep)
+
+
+def grid_kernel(
+    sizes, blocks_ref, measured_ref, mask_ref, order_ref, place_ref, table, partial, coded_near,
+    out_ref, coded_far, points, mirrored, near, far, lined,
+):
     parts, coils, local_x, local_y, local_z = out_ref.shape
-    size_x, size_y, size_z = count_x * local_x, count_y * local_y, count_z * local_z
     channels = parts * coils
-    width = size_x * channels
-    at_x, at_y, at_z = place_ref[0], place_ref[1], place_ref[2]
-    half_rows = local_y * size_z
-    top = REACH * size_z
-
-    def rows_of(gy):
-        return slice(top + gy * half_rows, top + (gy + 1) * half_rows)
-
-    edge = jnp.zeros((top, 2 * width), jnp.bfloat16)
-    padded[:top] = edge
-    padded[top + size_y * size_z :] = edge
-    for gy in range(count_y):
-        field = jnp.concatenate(
-            [
-                jnp.concatenate(
-                    [
-                        blocks_ref[((at_z ^ gz) * count_y + (at_y ^ gy)) * count_x + (at_x ^ gx)]
-                        for gz in range(count_z)
-                    ],
-                    axis=1,
+    rows, width = coded_far.shape
+    at_x, at_y = place_ref[0], place_ref[1]
+    own_first = (1 - place_ref[2]).astype(jnp.float32)
+    edge = REACH * local_z
+    load_half(sizes, blocks_ref, order_ref, place_ref, local_z, coded_far, points, mirrored)
+    for iteration in range(ITERS - 1):
+        totals = [None, None]
+        for dz in sorted(range(KS), key=lambda dz: dz == REACH):
+            shift = dz - REACH
+            own = partial[0, dz] + y_taps(mirrored, rows, local_z, lambda dy: table[dy, dz, :, width:])
+            other = partial[1, dz] + y_taps(points, rows, local_z, lambda dy: table[dy, dz, :, :width])
+            if shift != 0:
+                own, other = (
+                    shift_z(own, other, shift, local_z, 0, own_first),
+                    shift_z(other, own, shift, local_z, 0, 1.0 - own_first),
                 )
-                for gx in range(count_x)
-            ],
-            axis=0,
-        )
-        both = dot_nt(order_ref[: 2 * half_rows], field)
-        coded[gy * half_rows : (gy + 1) * half_rows] = both[:half_rows]
-        both = jnp.where(both < LIMIT, both, 0.0).astype(jnp.bfloat16)
-        padded[rows_of(gy), :width] = both[:half_rows]
-        padded[rows_of(count_y - 1 - gy), width:] = both[half_rows:]
-
-    z_at = iota((size_y * size_z, width), 0) % size_z
-    for iteration in range(ITERS - 1):
-        total = None
-        for dz in range(KS):
-            part = None
-            for dy, (ref, at) in enumerate(table):
-                term = dot_nt(padded[dy * size_z : (dy + size_y) * size_z], ref[at, dz])
-                part = term if part is None else part + term
-            shift = dz - REACH
-            if shift != 0:
-                part = pltpu.roll(part, -shift % part.shape[0], 0)
-                part = jnp.where((z_at + shift >= 0) & (z_at + shift < size_z), part, 0.0)
-            total = part if total is None else total + part
-        for gy in range(count_y):
-            values = coded[gy * half_rows : (gy + 1) * half_rows]
-            part = total[gy * half_rows : (gy + 1) * half_rows]
-            values = jnp.where(values < LIMIT, values, part).astype(jnp.bfloat16)
-            padded[rows_of(gy), :width] = values
-            padded[rows_of(count_y - 1 - gy), width:] = dot(order_ref[2 * half_rows :], values).astype(jnp.bfloat16)
+            totals = [part if total is None else total + part for total, part in zip(totals, (own, other))]
+        for ref, mirror_ref, coded, total in ((near, far, coded_near, totals[0]), (far, near, coded_far, totals[1])):
+            values = jnp.where(coded[...] < LIMIT, coded[...], total).astype(jnp.bfloat16)
+            ref[edge : edge + rows, :width] = values
+            mirror_ref[edge : edge + rows, width:] = dot(order_ref[rows:], values).astype(jnp.bfloat16)
+    for ref in (near, far):
+        ref[:edge] = jnp.zeros((edge, 2 * width), jnp.bfloat16)
+        ref[edge + rows :] = jnp.zeros((edge, 2 * width), jnp.bfloat16)
 
     own_rows = local_x * channels
+    own_points = local_y * local_z
     start_x = pl.multiple_of(at_x * own_rows, own_rows)
     result = None
-    for dy, (ref, at) in enumerate(table):
-        weights = jnp.concatenate([ref[at, dz, pl.ds(start_x, own_rows), :] for dz in range(KS)], axis=0)
-        start = pl.multiple_of((at_y * local_y + dy) * size_z, size_z)
-        term = dot_nt(weights, padded[pl.ds(start, half_rows), :])
+    for dy in range(KS):
+        weights = jnp.concatenate([table[dy, dz, pl.ds(start_x, own_rows), :] for dz in range(KS)], axis=0)
+        start = pl.multiple_of((at_y * local_y + dy) * local_z, local_z)
+        window = jnp.concatenate([near[pl.ds(start, own_points), :], far[pl.ds(start, own_points), :]], axis=0)
+        term = dot_nt(weights, window)
         result = term if result is None else result + term
-    z_at = iota((own_rows, half_rows), 1) % size_z
     total = None
     for dz in range(KS):
-        part = result[dz * own_rows : (dz + 1) * own_rows]
-        shift = dz - REACH
-        if shift != 0:
-            part = pltpu.roll(part, -shift % half_rows, 1)
-            part = jnp.where((z_at + shift >= 0) & (z_at + shift < size_z), part, 0.0)
-        total = part if total is None else total + part
-    total = total.astype(jnp.bfloat16)
-
-    rows = channels * local_y
-    unfold = one_hot(iota((rows, channels), 0) // local_y == iota((rows, channels), 1))
-    own_y = iota((rows, half_rows), 1) // size_z == iota((rows, half_rows), 0) % local_y
-    fold = one_hot(iota((half_rows, local_z), 0) % size_z == at_z * local_z + iota((half_rows, local_z), 1))
+        own = result[dz * own_rows : (dz + 1) * own_rows, :own_points]
+        other = result[dz * own_rows : (dz + 1) * own_rows, own_points:]
+        if dz != REACH:
+            own = shift_z(own, other, dz - REACH, local_z, 1, own_first)
+        total = own if total is None else total + own
+
+    for y in range(local_y):
+        piece = total if y == 0 else pltpu.roll(total, own_points - y * local_z, 1)
+        lined[pl.ds(y, own_rows, stride=local_y), :] = piece
     for x in range(local_x):
-        spread_out = dot(unfold, total[x * channels : (x + 1) * channels])
-        spread_out = jnp.where(own_y, spread_out, 0.0).astype(jnp.bfloat16)
-        values = dot(spread_out, fold).reshape(parts, coils, local_y, local_z)
+        values = lined[x * channels * local_y : (x + 1) * channels * local_y, :local_z]
+        values = values.reshape(parts, coils, local_y, local_z)
         sampled = (mask_ref[x] == 1)[None, None]
         values = jnp.where(sampled, measured_ref[:, :, x].astype(jnp.float32), values)
         out_ref[:, :, x] = values.astype(jnp.bfloat16)
@@ -232,18 +244,18 @@
     channels = parts * coils
     size_x, size_y, size_z = sizes[0] * local_x, sizes[1] * local_y, sizes[2] * local_z
     width = size_x * channels
-    half_rows = local_y * size_z
+    half_rows = size_y * local_z
     in_vmem = pl.BlockSpec(memory_space=pltpu.VMEM)
     in_hbm = pl.BlockSpec(memory_space=pltpu.HBM)
 
-    def call(kernel_fn, name, out_shape, in_specs, scratch=(), limit=VMEM_LIMIT, cost=2 ** 22):
+    def call(kernel_fn, name, out_shape, in_specs, scratch=(), outs=1, cost=2 ** 22):
         return pl.pallas_call(
             kernel_fn,
             out_shape=out_shape,
             in_specs=in_specs,
-            out_specs=in_vmem,
+            out_specs=in_vmem if outs == 1 else (in_vmem,) * outs,
             scratch_shapes=list(scratch),
-            compiler_params=pltpu.CompilerParams(vmem_limit_bytes=limit),
+            compiler_params=pltpu.CompilerParams(vmem_limit_bytes=VMEM_LIMIT),
             cost_estimate=pl.CostEstimate(flops=0, bytes_accessed=cost, transcendentals=0),
             name=name,
         )
@@ -263,12 +275,12 @@
     def after(arrived, *work):
         return lax.optimization_barrier((arrived,) + work)
 
-    taps = kernel.reshape(parts * KS ** 3, coils * 2 * coils)
+    taps = jnp.moveaxis(kernel, 0, 3).reshape(parts * KS ** 3, coils * 2 * coils)
     taps = jnp.pad(taps, ((0, -taps.shape[0] % 16), (0, 0)))
     place = jnp.stack([lax.axis_index(axis) for axis in SPACE]).astype(jnp.int32)
     steps = [(axis, 1 << bit) for axis in SPACE for bit in range(lax.axis_size(axis).bit_length() - 1)]
     blocks = packed[None]
-    tables, order = [], None
+    table, order = None, None
     for number, (axis, bit) in enumerate(steps):
         arrived = swap(blocks, axis, bit)
         if number == 0:
@@ -278,23 +290,43 @@
             arrived, flat = after(arrived, call(flat_kernel, "flat", flat_shape, [in_vmem])(taps))
         elif number == 2:
             table_shape = jax.ShapeDtypeStruct((KS, KS, width, 2 * width), jnp.bfloat16)
-            table = call(functools.partial(table_kernel, 0, size_x), "table", table_shape, [in_vmem])(flat)
-            order_shape = jax.ShapeDtypeStruct((3 * half_rows, half_rows), jnp.bfloat16)
-            order = call(functools.partial(order_kernel, local_y, local_z, size_z), "order", order_shape, [])()
+            order_shape = jax.ShapeDtypeStruct((2 * half_rows, half_rows), jnp.bfloat16)
+            table_fn = functools.partial(table_kernel, size_x)
+            table, order = call(table_fn, "table", (table_shape, order_shape), [in_vmem], outs=2)(flat)
             arrived, table, order = after(arrived, table, order)
-            tables.append(table)
+        elif number == len(steps) - 1:
+            in_smem = pl.BlockSpec(memory_space=pltpu.SMEM)
+            padded_rows = half_rows + 2 * REACH * local_z
+            padded = pltpu.VMEM((padded_rows, width), jnp.bfloat16)
+            partial_shape = jax.ShapeDtypeStruct((2, KS, half_rows, width), jnp.float32)
+            coded_shape = jax.ShapeDtypeStruct((half_rows, width), jnp.float32)
+            partial, coded = call(
+                functools.partial(near_kernel, sizes, local_z),
+                "near",
+                (partial_shape, coded_shape),
+                [in_vmem, in_vmem, in_smem, in_vmem],
+                [padded, padded],
+                outs=2,
+            )(blocks, order, place, table)
+            arrived, partial, coded = after(arrived, partial, coded)
+            break
         blocks = jnp.concatenate([blocks, arrived], axis=0)
 
+    both = pltpu.VMEM((padded_rows, 2 * width), jnp.bfloat16)
     return call(
         functools.partial(grid_kernel, sizes),
         "grid",
         jax.ShapeDtypeStruct(measured.shape, jnp.bfloat16),
-        [in_vmem] * 4 + [pl.BlockSpec(memory_space=pltpu.SMEM)] + [in_vmem] * len(tables),
+        [in_vmem] * 4 + [in_smem] + [in_vmem] * 3,
         [
-            pltpu.VMEM(((size_y + 2 * REACH) * size_z, 2 * width), jnp.bfloat16),
-            pltpu.VMEM((size_y * size_z, width), jnp.float32),
+            pltpu.VMEM((half_rows, width), jnp.float32),
+            padded,
+            padded,
+            both,
+            both,
+            pltpu.VMEM((local_x * channels * local_y, 128), jnp.float32),
         ],
-    )(blocks, measured, sample_mask, order, place, *tables)
+    )(arrived, measured, sample_mask, order, place, table, partial, coded)
 
 
 def partner(block, axis, bit):
@@ -392,7 +424,8 @@
     def body(measured, sample_mask, kernel):
         parts, coils, local_x, local_y, local_z = measured.shape
         width = grid[0] * local_x * parts * coils
-        small = width == 256 and grid[1] == 2 and local_y * grid[2] * local_z == 256
+        points = grid[1] * local_y * local_z
+        small = width == 256 and grid[1:] == (2, 2) and points == 256 and local_y * local_z == 128
         if small:
             return gathered_body(measured, sample_mask, kernel)
         return halo_body(measured, sample_mask, kernel)

time: 24.6 us -> 23 us (0.935)
  waiting for transfers between devices: 3.15 us -> 1.73 us
  Pallas kernels: 12 us -> 11.7 us
    pallas_call x1, Pallas kernels: 7.35 us -> 4.62 us  [gathered_body(): call(functools.partial(grid_kernel, sizes), 'grid', jax.ShapeDtypeStruct(...]
    pallas_call x2, Pallas kernels: 1.39 us -> 3.85 us  [the longest x1 2.57 us: gathered_body(): call(functools.partial(near_kernel, sizes, local_z), 'near', (partial_sha...]
    ppermute x4, waiting for transfers between devices: 3.15 us -> 1.73 us  [swap(): return lax.ppermute(block, axis, [(i, i ^ bit) for i in range(count)])]
    unnamed x9 -> x4, local copies, waits for them, and re-layouts: 1.04 us -> 0.01 us
    reshape x1, local copies, waits for them, and re-layouts: 0.11 us -> 1.05 us  [gathered_body(): jnp.moveaxis(kernel, 0, 3).reshape(parts * KS ** 3, coils * 2 * coils)]
  transfers between devices with their start and end apart: 4 -> 4, of which waited for: 3 -> 2; matrix products, arithmetic and copies ran while one was open for 5% -> 5% of each run, Pallas kernels for 13% -> 25%
where the time goes in v2:
time: 23 us; the launch traced here: 22.8 us
  Pallas kernels  11.7 us (51%)
  starting transfers between devices  8.11 us (35%)
  waiting for transfers between devices  1.73 us (8%)
  local copies, waits for them, and re-layouts  1.08 us (5%)
    ppermute x4, starting transfers between devices, swap(): return lax.ppermute(block, axis, [(i, i ^ bit) for i in range(count)])  8.11 us
    pallas_call x1, Pallas kernels, gathered_body(): call(functools.partial(grid_kernel, sizes), 'grid', jax.ShapeDtypeStruct(...  4.62 us
    pallas_call x1, Pallas kernels, gathered_body(): call(functools.partial(near_kernel, sizes, local_z), 'near', (partial_sha...  2.57 us
    pallas_call x1, Pallas kernels, gathered_body(): call(flat_kernel, 'flat', flat_shape, [in_vmem])(taps)  1.85 us
    ppermute x4, waiting for transfers between devices, swap(): return lax.ppermute(block, axis, [(i, i ^ bit) for i in range(count)])  1.73 us
    pallas_call x1, Pallas kernels, gathered_body(): call(pack_kernel, 'pack', jax.ShapeDtypeStruct((local_x * channels, local...  1.36 us
    pallas_call x1, Pallas kernels, gathered_body(): call(table_fn, 'table', (table_shape, order_shape), [in_vmem], outs=2)(flat)  1.28 us
    reshape x1, local copies, waits for them, and re-layouts, gathered_body(): jnp.moveaxis(kernel, 0, 3).reshape(parts * KS ** 3, coils * 2 * coils)  1.05 us
  transfers between devices with their start and end apart: 4, of which 2 were waited for; matrix products, arithmetic and copies ran while one was open for 5% of the time, Pallas kernels for 25%

profile of v2, /device:TPU:0, one launch (start us, length us, event | category | flops | bytes accessed | tf_op | source)
XLA Modules:
  0.0 22.8 jit_solution(13050222545244946222)
XLA Ops:
  0.0 1.4 %pack.1 = bf16[64,128]{1,0:T(8,128)(2,1)S(1)} custom-call(bf16[2,16,2,8,16]{4,3,2,1,0:T(8,128)(2,1)} %measured_ref.1, s32[2,8,16]{2,1,0:T(8,128)} %mask_ref.1), custom_call_target="tpu_custom_call" | custom-call | bytes 4194304 | tf_op jit(solution)/shard_map/pack/pallas_call | solution.py:263
  1.4 3.1 %collective-permute-start = (bf16[1,64,128]{2,1,0:T(8,128)(2,1)S(1)}, bf16[1,64,128]{2,1,0:T(8,128)(2,1)S(1)}, u32[]{:S(2)}, u32[]{:S(2)}) collective-permute-start(bf16[1,64,128]{2,1,0:T(8,128)(2,1)S(1)} %bitcast.5), channel_id=1, source_target_pairs={{0,4},{4,0},{8,12},{12,8},{1,5},{5,1},{9,13},{13,9},{2,6},{6,2},{1... | collective-permute-start | bytes 49160 | tf_op jit(solution)/shard_map/ppermute | solution.py:237
  4.5 0.1 pad_add_fusion.place_ref
  4.6 1.0 %reshape.3 = bf16[250,512]{1,0:T(8,128)(2,1)S(1)} reshape(bf16[5,5,5,2,512]{4,3,2,1,0:T(2,128)(2,1)} %bitcast.9) | data formatting | bytes 512000 | tf_op jit(solution)/shard_map/reshape | solution.py:278
  5.6 0.6 %collective-permute-done = bf16[1,64,128]{2,1,0:T(8,128)(2,1)S(1)} collective-permute-done((bf16[1,64,128]{2,1,0:T(8,128)(2,1)S(1)}, bf16[1,64,128]{2,1,0:T(8,128)(2,1)S(1)}, u32[]{:S(2)}, u32[]{:S(2)}) %collective-permute-start) | collective-permute-done | bytes 16416 | tf_op jit(solution)/shard_map/ppermute | solution.py:237
  6.2 3.0 %collective-permute-start.1 = (bf16[2,64,128]{2,1,0:T(8,128)(2,1)S(1)}, bf16[2,64,128]{2,1,0:T(8,128)(2,1)S(1)}, u32[]{:S(2)}, u32[]{:S(2)}) collective-permute-start(bf16[2,64,128]{2,1,0:T(8,128)(2,1)S(1)} %pad_maximum_fusion.2), channel_id=1, source_target_pairs={{0,8},{4,12},{8,0},{12,4},{1,9},{5,13},{9,1},{13,5},{2,10},{6,14},... | collective-permute-start | bytes 98312 | tf_op jit(solution)/shard_map/ppermute | solution.py:237
  9.2 1.9 %flat.1 = f32[2,4096,128]{2,1,0:T(8,128)S(1)} custom-call(bf16[256,512]{1,0:T(8,128)(2,1)S(1)} %pad.4.taps_ref), custom_call_target="tpu_custom_call" | custom-call | bytes 4194304 | tf_op jit(solution)/shard_map/flat/pallas_call | solution.py:290
  11.1 0.0 collective-permute-done.1
  11.2 1.9 %collective-permute-start.2 = (bf16[4,64,128]{2,1,0:T(8,128)(2,1)S(1)}, bf16[4,64,128]{2,1,0:T(8,128)(2,1)S(1)}, u32[]{:S(2)}, u32[]{:S(2)}) collective-permute-start(bf16[4,64,128]{2,1,0:T(8,128)(2,1)S(1)} %pad_maximum_fusion.1), channel_id=1, source_target_pairs={{0,2},{2,0},{1,3},{3,1},{4,6},{6,4},{5,7},{7,5},{8,10},{10,8},{9,1... | collective-permute-start | bytes 196616 | tf_op jit(solution)/shard_map/ppermute | solution.py:237
  13.0 1.3 %table.1 = (bf16[5,5,256,512]{3,2,1,0:T(8,128)(2,1)S(1)}, bf16[512,256]{1,0:T(8,128)(2,1)S(1)}) custom-call(f32[2,4096,128]{2,1,0:T(8,128)S(1)} %flat.1), custom_call_target="tpu_custom_call" | custom-call | bytes 4194304 | tf_op jit(solution)/shard_map/table/pallas_call | solution.py:295
  14.3 0.0 copy-start
  14.3 0.0 copy-start.1
  14.4 1.1 %collective-permute-done.2 = bf16[4,64,128]{2,1,0:T(8,128)(2,1)S(1)} collective-permute-done((bf16[4,64,128]{2,1,0:T(8,128)(2,1)S(1)}, bf16[4,64,128]{2,1,0:T(8,128)(2,1)S(1)}, u32[]{:S(2)}, u32[]{:S(2)}) %collective-permute-start.2) | collective-permute-done | bytes 65568 | tf_op jit(solution)/shard_map/ppermute | solution.py:237
  15.5 0.1 collective-permute-start.3
  15.6 2.6 %near.1 = (f32[2,5,256,256]{3,2,1,0:T(8,128)S(1)}, f32[256,256]{1,0:T(8,128)S(1)}) custom-call(bf16[8,64,128]{2,1,0:T(8,128)(2,1)S(1)} %pad_maximum_fusion.blocks_ref, bf16[512,256]{1,0:T(8,128)(2,1)S(1)} %get-tuple-element.27.order_ref, s32[3]{0:T(128)S(1)} %pad_add_fusion.place_ref, bf16[5,5,256,512]{3,2,1,0:T(8,128)(2,1)S(1)} %get-tuple-element.29.table), custom_call_target="tpu_custom_call" | custom-call | bytes 4194304 | tf_op jit(solution)/shard_map/near/pallas_call | solution.py:303
  18.2 0.0 collective-permute-done.3.blocks_ref
  18.2 0.0 copy-done
  18.2 0.0 copy-done.1
  18.2 4.6 %grid.1 = bf16[2,16,2,8,16]{4,3,2,1,0:T(8,128)(2,1)} custom-call(bf16[8,64,128]{2,1,0:T(8,128)(2,1)S(1)} %collective-permute-done.3.blocks_ref, bf16[2,16,2,8,16]{4,3,2,1,0:T(8,128)(2,1)S(1)} %copy-done, s32[2,8,16]{2,1,0:T(8,128)S(1)} %copy-done.1, bf16[512,256]{1,0:T(8,128)(2,1)S(1)} %get-tuple-element.27.order_ref, s32[3]{0:T(128)S(1)} %pad_add_fusion.place_ref, ...), custom_call_target="tpu_custom_call" | custom-call | bytes 4194304 | tf_op jit(solution)/shard_map/grid/pallas_call | solution.py:316
  (4 shorter events, 0.0 us)
Async XLA Ops:
  1.4 4.8 %collective-permute-start = (bf16[1,64,128]{2,1,0:T(8,128)(2,1)S(1)}, bf16[1,64,128]{2,1,0:T(8,128)(2,1)S(1)}, u32[]{:S(2)}, u32[]{:S(2)}) collective-permute-start(bf16[1,64,128]{2,1,0:T(8,128)(2,1)S(1)} %bitcast.5), channel_id=1, source_target_pairs={{0,4},{4,0},{8,12},{12,8},{1,5},{5,1},{9,13},{13,9},{2,6},{6,2},{1... | collective-permute-start | bytes 49160 | tf_op jit(solution)/shard_map/ppermute | solution.py:237
  6.2 4.9 %collective-permute-start.1 = (bf16[2,64,128]{2,1,0:T(8,128)(2,1)S(1)}, bf16[2,64,128]{2,1,0:T(8,128)(2,1)S(1)}, u32[]{:S(2)}, u32[]{:S(2)}) collective-permute-start(bf16[2,64,128]{2,1,0:T(8,128)(2,1)S(1)} %pad_maximum_fusion.2), channel_id=1, source_target_pairs={{0,8},{4,12},{8,0},{12,4},{1,9},{5,13},{9,1},{13,5},{2,10},{6,14},... | collective-permute-start | bytes 98312 | tf_op jit(solution)/shard_map/ppermute | solution.py:237
  11.2 4.3 %collective-permute-start.2 = (bf16[4,64,128]{2,1,0:T(8,128)(2,1)S(1)}, bf16[4,64,128]{2,1,0:T(8,128)(2,1)S(1)}, u32[]{:S(2)}, u32[]{:S(2)}) collective-permute-start(bf16[4,64,128]{2,1,0:T(8,128)(2,1)S(1)} %pad_maximum_fusion.1), channel_id=1, source_target_pairs={{0,2},{2,0},{1,3},{3,1},{4,6},{6,4},{5,7},{7,5},{8,10},{10,8},{9,1... | collective-permute-start | bytes 196616 | tf_op jit(solution)/shard_map/ppermute | solution.py:237
  14.3 3.8 %copy-start = (bf16[2,16,2,8,16]{4,3,2,1,0:T(8,128)(2,1)S(1)}, bf16[2,16,2,8,16]{4,3,2,1,0:T(8,128)(2,1)}, u32[]{:S(2)}) copy-start(bf16[2,16,2,8,16]{4,3,2,1,0:T(8,128)(2,1)} %measured_ref.1) | copy-start | bytes 49156
  14.3 3.8 %copy-start.1 = (s32[2,8,16]{2,1,0:T(8,128)S(1)}, s32[2,8,16]{2,1,0:T(8,128)}, u32[]{:S(2)}) copy-start(s32[2,8,16]{2,1,0:T(8,128)} %mask_ref.1) | copy-start | bytes 3076
  15.5 2.7 %collective-permute-start.3 = (bf16[8,64,128]{2,1,0:T(8,128)(2,1)S(1)}, bf16[8,64,128]{2,1,0:T(8,128)(2,1)S(1)}, u32[]{:S(2)}, u32[]{:S(2)}) collective-permute-start(bf16[8,64,128]{2,1,0:T(8,128)(2,1)S(1)} %pad_maximum_fusion.blocks_ref), channel_id=1, source_target_pairs={{0,1},{1,0},{2,3},{3,2},{4,5},{5,4},{6,7},{7,6},{8,9},{9,8},{10,11... | collective-permute-start | bytes 393224 | tf_op jit(solution)/shard_map/ppermute | solution.py:237

commit v3 on v2

--- a/solution.py
+++ b/solution.py
@@ -33,27 +33,31 @@
     return lax.dot_general(a, b, (((1,), (1,)), ((), ())), preferred_element_type=jnp.float32)
 
 
-def pack_kernel(measured_hbm, mask_hbm, packed_ref, measured_ref, mask_ref, sems):
+def pack_kernel(measured_hbm, mask_hbm, packed_ref, measured_ref, mask_ref, lined, sems):
     copies = [
         pltpu.make_async_copy(measured_hbm, measured_ref, sems.at[0]),
         pltpu.make_async_copy(mask_hbm, mask_ref, sems.at[1]),
     ]
     for copy in copies:
         copy.start()
-    parts, coils, size_x, size_y, size_z = measured_ref.shape
-    lanes = size_y * size_z
-    rows = parts * coils * size_y
-    repeat = one_hot(iota((size_z, lanes), 1) % size_z == iota((size_z, lanes), 0))
-    own_y = iota((rows, lanes), 1) // size_z == iota((rows, lanes), 0) % size_y
-    gather = one_hot(iota((parts * coils, rows), 1) // size_y == iota((parts * coils, rows), 0))
     for copy in copies:
         copy.wait()
+    parts, coils, size_x, size_y, size_z = measured_ref.shape
+    channels = parts * coils
+    rows = channels * size_y
     for x in range(size_x):
         values = measured_ref[:, :, x].astype(jnp.float32)
         sampled = (mask_ref[x] == 1)[None, None]
-        coded = jnp.where(sampled, values, UNSAMPLED).reshape(rows, size_z).astype(jnp.bfloat16)
-        spread = jnp.where(own_y, dot(coded, repeat), 0.0).astype(jnp.bfloat16)
-        packed_ref[x * parts * coils : (x + 1) * parts * coils] = dot(gather, spread).astype(jnp.bfloat16)
+        lined[x, :, :size_z] = jnp.where(sampled, values, UNSAMPLED).reshape(rows, size_z)
+    lane_y = iota((channels, size_y * size_z), 1) // size_z
+    for x in range(size_x):
+        packed = None
+        for y in range(size_y):
+            piece = lined[x, pl.ds(y, channels, stride=size_y), :]
+            if y > 0:
+                piece = jnp.where(lane_y == y, pltpu.roll(piece, y * size_z, 1), packed)
+            packed = piece
+        packed_ref[x * channels : (x + 1) * channels] = packed.astype(jnp.bfloat16)
 
 
 def flat_kernel(taps_ref, flat):
@@ -125,14 +129,15 @@
     lax.fori_loop(0, table.shape[0] * KS, add_taps, 0)
 
 
-def load_half(sizes, blocks_ref, order_ref, place_ref, local_z, coded, points, mirrored):
+def load_half(sizes, blocks_ref, order_ref, local_z, coded, points, mirrored):
     count_x, count_y, _ = sizes
+    at_x, at_y = lax.axis_index(SPACE[0]), lax.axis_index(SPACE[1])
     rows = order_ref.shape[1]
     edge = REACH * local_z
     field = jnp.concatenate(
         [
             jnp.concatenate(
-                [blocks_ref[(place_ref[1] ^ gy) * count_x + (place_ref[0] ^ gx)] for gy in range(count_y)], axis=1
+                [blocks_ref[(at_y ^ gy) * count_x + (at_x ^ gx)] for gy in range(count_y)], axis=1
             )
             for gx in range(count_x)
         ],
@@ -155,9 +160,9 @@
     return total
 
 
-def near_kernel(sizes, local_z, blocks_ref, order_ref, place_ref, table, partial, coded, points, mirrored):
+def near_kernel(sizes, local_z, blocks_ref, order_ref, table, partial, coded, points, mirrored):
     rows, width = coded.shape
-    load_half(sizes, blocks_ref, order_ref, place_ref, local_z, coded, points, mirrored)
+    load_half(sizes, blocks_ref, order_ref, local_z, coded, points, mirrored)
     for dz in range(KS):
         partial[0, dz] = y_taps(points, rows, local_z, lambda dy: table[dy, dz, :, :width])
         partial[1, dz] = y_taps(mirrored, rows, local_z, lambda dy: table[dy, dz, :, width:])
@@ -173,16 +178,16 @@
 
 
 def grid_kernel(
-    sizes, blocks_ref, measured_ref, mask_ref, order_ref, place_ref, table, partial, coded_near,
+    sizes, blocks_ref, measured_ref, mask_ref, order_ref, table, partial, coded_near,
     out_ref, coded_far, points, mirrored, near, far, lined,
 ):
     parts, coils, local_x, local_y, local_z = out_ref.shape
     channels = parts * coils
     rows, width = coded_far.shape
-    at_x, at_y = place_ref[0], place_ref[1]
-    own_first = (1 - place_ref[2]).astype(jnp.float32)
+    at_x, at_y = lax.axis_index(SPACE[0]), lax.axis_index(SPACE[1])
+    own_first = (1 - lax.axis_index(SPACE[2])).astype(jnp.float32)
     edge = REACH * local_z
-    load_half(sizes, blocks_ref, order_ref, place_ref, local_z, coded_far, points, mirrored)
+    load_half(sizes, blocks_ref, order_ref, local_z, coded_far, points, mirrored)
     for iteration in range(ITERS - 1):
         totals = [None, None]
         for dz in sorted(range(KS), key=lambda dz: dz == REACH):
@@ -268,6 +273,7 @@
         [
             pltpu.VMEM(measured.shape, measured.dtype),
             pltpu.VMEM(sample_mask.shape, sample_mask.dtype),
+            pltpu.VMEM((local_x, channels * local_y, local_y * local_z), jnp.float32),
             pltpu.SemaphoreType.DMA((2,)),
         ],
     )(*[pltpu.with_memory_space_constraint(a, pltpu.HBM) for a in (measured, sample_mask)])
@@ -277,14 +283,13 @@
 
     taps = jnp.moveaxis(kernel, 0, 3).reshape(parts * KS ** 3, coils * 2 * coils)
     taps = jnp.pad(taps, ((0, -taps.shape[0] % 16), (0, 0)))
-    place = jnp.stack([lax.axis_index(axis) for axis in SPACE]).astype(jnp.int32)
     steps = [(axis, 1 << bit) for axis in SPACE for bit in range(lax.axis_size(axis).bit_length() - 1)]
     blocks = packed[None]
     table, order = None, None
     for number, (axis, bit) in enumerate(steps):
         arrived = swap(blocks, axis, bit)
         if number == 0:
-            arrived, taps, place = after(arrived, taps, place)
+            arrived, taps = after(arrived, taps)
         elif number == 1:
             flat_shape = jax.ShapeDtypeStruct((2, taps.shape[0] * coils, 128), jnp.float32)
             arrived, flat = after(arrived, call(flat_kernel, "flat", flat_shape, [in_vmem])(taps))
@@ -295,7 +300,6 @@
             table, order = call(table_fn, "table", (table_shape, order_shape), [in_vmem], outs=2)(flat)
             arrived, table, order = after(arrived, table, order)
         elif number == len(steps) - 1:
-            in_smem = pl.BlockSpec(memory_space=pltpu.SMEM)
             padded_rows = half_rows + 2 * REACH * local_z
             padded = pltpu.VMEM((padded_rows, width), jnp.bfloat16)
             partial_shape = jax.ShapeDtypeStruct((2, KS, half_rows, width), jnp.float32)
@@ -304,10 +308,10 @@
                 functools.partial(near_kernel, sizes, local_z),
                 "near",
                 (partial_shape, coded_shape),
-                [in_vmem, in_vmem, in_smem, in_vmem],
+                [in_vmem] * 3,
                 [padded, padded],
                 outs=2,
-            )(blocks, order, place, table)
+            )(blocks, order, table)
             arrived, partial, coded = after(arrived, partial, coded)
             break
         blocks = jnp.concatenate([blocks, arrived], axis=0)
@@ -317,7 +321,7 @@
         functools.partial(grid_kernel, sizes),
         "grid",
         jax.ShapeDtypeStruct(measured.shape, jnp.bfloat16),
-        [in_vmem] * 4 + [in_smem] + [in_vmem] * 3,
+        [in_vmem] * 7,
         [
             pltpu.VMEM((half_rows, width), jnp.float32),
             padded,
@@ -326,7 +330,7 @@
             both,
             pltpu.VMEM((local_x * channels * local_y, 128), jnp.float32),
         ],
-    )(arrived, measured, sample_mask, order, place, table, partial, coded)
+    )(arrived, measured, sample_mask, order, table, partial, coded)
 
 
 def partner(block, axis, bit):

time: 23 us -> 21.6 us (0.939)
  Pallas kernels: 11.7 us -> 10.3 us
    pallas_call x1, Pallas kernels: 4.62 us -> 4.06 us  [gathered_body(): call(functools.partial(grid_kernel, sizes), 'grid', jax.ShapeDtypeStruct(...]
    pallas_call x1, Pallas kernels: 2.57 us -> 2.04 us  [gathered_body(): call(functools.partial(near_kernel, sizes, local_z), 'near', (partial_sha...]
    pallas_call x1, Pallas kernels: 1.36 us -> 1.05 us  [gathered_body(): call(pack_kernel, 'pack', jax.ShapeDtypeStruct((local_x * channels, local...]
  transfers between devices with their start and end apart: 4 -> 4, of which waited for: 2 -> 2; matrix products, arithmetic and copies ran while one was open for 5% -> 5% of each run, Pallas kernels for 25% -> 24%
where the time goes in v3:
time: 21.6 us; the launch traced here: 21.4 us
  Pallas kernels  10.3 us (48%)
  starting transfers between devices  8.11 us (38%)
  waiting for transfers between devices  1.8 us (8%)
  local copies, waits for them, and re-layouts  1.08 us (5%)
    ppermute x4, starting transfers between devices, swap(): return lax.ppermute(block, axis, [(i, i ^ bit) for i in range(count)])  8.11 us
    pallas_call x1, Pallas kernels, gathered_body(): call(functools.partial(grid_kernel, sizes), 'grid', jax.ShapeDtypeStruct(...  4.06 us
    pallas_call x1, Pallas kernels, gathered_body(): call(functools.partial(near_kernel, sizes, local_z), 'near', (partial_sha...  2.04 us
    pallas_call x1, Pallas kernels, gathered_body(): call(flat_kernel, 'flat', flat_shape, [in_vmem])(taps)  1.85 us
    ppermute x4, waiting for transfers between devices, swap(): return lax.ppermute(block, axis, [(i, i ^ bit) for i in range(count)])  1.8 us
    pallas_call x1, Pallas kernels, gathered_body(): call(table_fn, 'table', (table_shape, order_shape), [in_vmem], outs=2)(flat)  1.28 us
    pallas_call x1, Pallas kernels, gathered_body(): call(pack_kernel, 'pack', jax.ShapeDtypeStruct((local_x * channels, local...  1.05 us
    reshape x1, local copies, waits for them, and re-layouts, gathered_body(): jnp.moveaxis(kernel, 0, 3).reshape(parts * KS ** 3, coils * 2 * coils)  1.05 us
  transfers between devices with their start and end apart: 4, of which 2 were waited for; matrix products, arithmetic and copies ran while one was open for 5% of the time, Pallas kernels for 24%

profile of v3, /device:TPU:0, one launch (start us, length us, event | category | flops | bytes accessed | tf_op | source)
XLA Modules:
  0.0 21.4 jit_solution(1789832889664143389)
XLA Ops:
  0.0 1.1 %pack.1 = bf16[64,128]{1,0:T(8,128)(2,1)S(1)} custom-call(bf16[2,16,2,8,16]{4,3,2,1,0:T(8,128)(2,1)} %measured_ref.1, s32[2,8,16]{2,1,0:T(8,128)} %mask_ref.1), custom_call_target="tpu_custom_call" | custom-call | bytes 4194304 | tf_op jit(solution)/shard_map/pack/pallas_call | solution.py:268
  1.1 3.1 %collective-permute-start = (bf16[1,64,128]{2,1,0:T(8,128)(2,1)S(1)}, bf16[1,64,128]{2,1,0:T(8,128)(2,1)S(1)}, u32[]{:S(2)}, u32[]{:S(2)}) collective-permute-start(bf16[1,64,128]{2,1,0:T(8,128)(2,1)S(1)} %bitcast.2), channel_id=1, source_target_pairs={{0,4},{4,0},{8,12},{12,8},{1,5},{5,1},{9,13},{13,9},{2,6},{6,2},{1... | collective-permute-start | bytes 49160 | tf_op jit(solution)/shard_map/ppermute | solution.py:242
  4.2 1.0 %reshape.3 = bf16[250,512]{1,0:T(8,128)(2,1)S(1)} reshape(bf16[5,5,5,2,512]{4,3,2,1,0:T(2,128)(2,1)} %bitcast.6) | data formatting | bytes 512000 | tf_op jit(solution)/shard_map/reshape | solution.py:284
  5.3 0.6 %collective-permute-done = bf16[1,64,128]{2,1,0:T(8,128)(2,1)S(1)} collective-permute-done((bf16[1,64,128]{2,1,0:T(8,128)(2,1)S(1)}, bf16[1,64,128]{2,1,0:T(8,128)(2,1)S(1)}, u32[]{:S(2)}, u32[]{:S(2)}) %collective-permute-start) | collective-permute-done | bytes 16416 | tf_op jit(solution)/shard_map/ppermute | solution.py:242
  5.9 3.0 %collective-permute-start.1 = (bf16[2,64,128]{2,1,0:T(8,128)(2,1)S(1)}, bf16[2,64,128]{2,1,0:T(8,128)(2,1)S(1)}, u32[]{:S(2)}, u32[]{:S(2)}) collective-permute-start(bf16[2,64,128]{2,1,0:T(8,128)(2,1)S(1)} %pad_maximum_fusion.2), channel_id=1, source_target_pairs={{0,8},{4,12},{8,0},{12,4},{1,9},{5,13},{9,1},{13,5},{2,10},{6,14},... | collective-permute-start | bytes 98312 | tf_op jit(solution)/shard_map/ppermute | solution.py:242
  8.9 1.9 %flat.1 = f32[2,4096,128]{2,1,0:T(8,128)S(1)} custom-call(bf16[256,512]{1,0:T(8,128)(2,1)S(1)} %pad.4.taps_ref), custom_call_target="tpu_custom_call" | custom-call | bytes 4194304 | tf_op jit(solution)/shard_map/flat/pallas_call | solution.py:295
  10.8 0.0 collective-permute-done.1
  10.8 1.9 %collective-permute-start.2 = (bf16[4,64,128]{2,1,0:T(8,128)(2,1)S(1)}, bf16[4,64,128]{2,1,0:T(8,128)(2,1)S(1)}, u32[]{:S(2)}, u32[]{:S(2)}) collective-permute-start(bf16[4,64,128]{2,1,0:T(8,128)(2,1)S(1)} %pad_maximum_fusion.1), channel_id=1, source_target_pairs={{0,2},{2,0},{1,3},{3,1},{4,6},{6,4},{5,7},{7,5},{8,10},{10,8},{9,1... | collective-permute-start | bytes 196616 | tf_op jit(solution)/shard_map/ppermute | solution.py:242
  12.7 1.3 %table.1 = (bf16[5,5,256,512]{3,2,1,0:T(8,128)(2,1)S(1)}, bf16[512,256]{1,0:T(8,128)(2,1)S(1)}) custom-call(f32[2,4096,128]{2,1,0:T(8,128)S(1)} %flat.1), custom_call_target="tpu_custom_call" | custom-call | bytes 4194304 | tf_op jit(solution)/shard_map/table/pallas_call | solution.py:300
  14.0 0.0 copy-start
  14.0 0.0 copy-start.1
  14.0 1.1 %collective-permute-done.2 = bf16[4,64,128]{2,1,0:T(8,128)(2,1)S(1)} collective-permute-done((bf16[4,64,128]{2,1,0:T(8,128)(2,1)S(1)}, bf16[4,64,128]{2,1,0:T(8,128)(2,1)S(1)}, u32[]{:S(2)}, u32[]{:S(2)}) %collective-permute-start.2) | collective-permute-done | bytes 65568 | tf_op jit(solution)/shard_map/ppermute | solution.py:242
  15.2 0.1 collective-permute-start.3
  15.3 2.0 %near.1 = (f32[2,5,256,256]{3,2,1,0:T(8,128)S(1)}, f32[256,256]{1,0:T(8,128)S(1)}) custom-call(bf16[8,64,128]{2,1,0:T(8,128)(2,1)S(1)} %pad_maximum_fusion.blocks_ref, bf16[512,256]{1,0:T(8,128)(2,1)S(1)} %get-tuple-element.26.order_ref, bf16[5,5,256,512]{3,2,1,0:T(8,128)(2,1)S(1)} %get-tuple-element.27.table), custom_call_target="tpu_custom_call" | custom-call | bytes 4194304 | tf_op jit(solution)/shard_map/near/pallas_call | solution.py:307
  17.3 0.0 collective-permute-done.3.blocks_ref
  17.3 0.0 copy-done
  17.3 0.0 copy-done.1
  17.3 4.1 %grid.1 = bf16[2,16,2,8,16]{4,3,2,1,0:T(8,128)(2,1)} custom-call(bf16[8,64,128]{2,1,0:T(8,128)(2,1)S(1)} %collective-permute-done.3.blocks_ref, bf16[2,16,2,8,16]{4,3,2,1,0:T(8,128)(2,1)S(1)} %copy-done, s32[2,8,16]{2,1,0:T(8,128)S(1)} %copy-done.1, bf16[512,256]{1,0:T(8,128)(2,1)S(1)} %get-tuple-element.26.order_ref, ...), custom_call_target="tpu_custom_call" | custom-call | bytes 4194304 | tf_op jit(solution)/shard_map/grid/pallas_call | solution.py:320
  (4 shorter events, 0.1 us)
Async XLA Ops:
  1.1 4.8 %collective-permute-start = (bf16[1,64,128]{2,1,0:T(8,128)(2,1)S(1)}, bf16[1,64,128]{2,1,0:T(8,128)(2,1)S(1)}, u32[]{:S(2)}, u32[]{:S(2)}) collective-permute-start(bf16[1,64,128]{2,1,0:T(8,128)(2,1)S(1)} %bitcast.2), channel_id=1, source_target_pairs={{0,4},{4,0},{8,12},{12,8},{1,5},{5,1},{9,13},{13,9},{2,6},{6,2},{1... | collective-permute-start | bytes 49160 | tf_op jit(solution)/shard_map/ppermute | solution.py:242
  5.9 4.9 %collective-permute-start.1 = (bf16[2,64,128]{2,1,0:T(8,128)(2,1)S(1)}, bf16[2,64,128]{2,1,0:T(8,128)(2,1)S(1)}, u32[]{:S(2)}, u32[]{:S(2)}) collective-permute-start(bf16[2,64,128]{2,1,0:T(8,128)(2,1)S(1)} %pad_maximum_fusion.2), channel_id=1, source_target_pairs={{0,8},{4,12},{8,0},{12,4},{1,9},{5,13},{9,1},{13,5},{2,10},{6,14},... | collective-permute-start | bytes 98312 | tf_op jit(solution)/shard_map/ppermute | solution.py:242
  10.8 4.3 %collective-permute-start.2 = (bf16[4,64,128]{2,1,0:T(8,128)(2,1)S(1)}, bf16[4,64,128]{2,1,0:T(8,128)(2,1)S(1)}, u32[]{:S(2)}, u32[]{:S(2)}) collective-permute-start(bf16[4,64,128]{2,1,0:T(8,128)(2,1)S(1)} %pad_maximum_fusion.1), channel_id=1, source_target_pairs={{0,2},{2,0},{1,3},{3,1},{4,6},{6,4},{5,7},{7,5},{8,10},{10,8},{9,1... | collective-permute-start | bytes 196616 | tf_op jit(solution)/shard_map/ppermute | solution.py:242
  14.0 3.3 %copy-start = (bf16[2,16,2,8,16]{4,3,2,1,0:T(8,128)(2,1)S(1)}, bf16[2,16,2,8,16]{4,3,2,1,0:T(8,128)(2,1)}, u32[]{:S(2)}) copy-start(bf16[2,16,2,8,16]{4,3,2,1,0:T(8,128)(2,1)} %measured_ref.1) | copy-start | bytes 49156
  14.0 3.3 %copy-start.1 = (s32[2,8,16]{2,1,0:T(8,128)S(1)}, s32[2,8,16]{2,1,0:T(8,128)}, u32[]{:S(2)}) copy-start(s32[2,8,16]{2,1,0:T(8,128)} %mask_ref.1) | copy-start | bytes 3076
  15.2 2.1 %collective-permute-start.3 = (bf16[8,64,128]{2,1,0:T(8,128)(2,1)S(1)}, bf16[8,64,128]{2,1,0:T(8,128)(2,1)S(1)}, u32[]{:S(2)}, u32[]{:S(2)}) collective-permute-start(bf16[8,64,128]{2,1,0:T(8,128)(2,1)S(1)} %pad_maximum_fusion.blocks_ref), channel_id=1, source_target_pairs={{0,1},{1,0},{2,3},{3,2},{4,5},{5,4},{6,7},{7,6},{8,9},{9,8},{10,11... | collective-permute-start | bytes 393224 | tf_op jit(solution)/shard_map/ppermute | solution.py:242

commit v4 on v3

--- a/solution.py
+++ b/solution.py
@@ -82,8 +82,9 @@
     order[rows:] = one_hot(rows - 1 - row == col)
 
 
-def table_kernel(size_x, flat, table, order):
-    write_orders(order)
+def table_kernel(size_x, flat, table, mirror):
+    rows = mirror.shape[0]
+    mirror[...] = one_hot(rows - 1 - iota((rows, rows), 0) == iota((rows, rows), 1))
     coils = COILS
     channels = 2 * coils
     width = size_x * channels
@@ -129,27 +130,38 @@
     lax.fori_loop(0, table.shape[0] * KS, add_taps, 0)
 
 
-def load_half(sizes, blocks_ref, order_ref, local_z, coded, points, mirrored):
-    count_x, count_y, _ = sizes
-    at_x, at_y = lax.axis_index(SPACE[0]), lax.axis_index(SPACE[1])
-    rows = order_ref.shape[1]
+def turn(blocks_ref, order):
+    count_x = blocks_ref.shape[0]
+    at_x = lax.axis_index(SPACE[0])
+    field = jnp.concatenate([blocks_ref[at_x ^ gx] for gx in range(count_x)], axis=0)
+    return dot_nt(order, field).astype(jnp.bfloat16)
+
+
+def turn_kernel(blocks_ref, turned, order):
+    write_orders(order)
+    turned[...] = turn(blocks_ref, order[...])
+
+
+def join_kernel(blocks_ref, turned, order, half):
+    other = turn(blocks_ref, order[...])
+    quarter = order.shape[1]
+    rows = 2 * quarter
+    at_y = lax.axis_index(SPACE[1])
+    for values, place in ((turned[...], at_y), (other, 1 - at_y)):
+        start = pl.multiple_of(place * quarter, quarter)
+        half[pl.ds(start, quarter)] = values[:quarter]
+        start = pl.multiple_of(rows + (1 - place) * quarter, quarter)
+        half[pl.ds(start, quarter)] = values[quarter:]
+
+
+def load_half(half, local_z, points, mirrored):
+    rows, width = half.shape[0] // 2, half.shape[1]
     edge = REACH * local_z
-    field = jnp.concatenate(
-        [
-            jnp.concatenate(
-                [blocks_ref[(at_y ^ gy) * count_x + (at_x ^ gx)] for gy in range(count_y)], axis=1
-            )
-            for gx in range(count_x)
-        ],
-        axis=0,
-    )
-    both = dot_nt(order_ref[...], field)
-    coded[...] = both[:rows]
-    both = jnp.where(both < LIMIT, both, 0.0).astype(jnp.bfloat16)
-    for ref, values in ((points, both[:rows]), (mirrored, both[rows:])):
-        ref[:edge] = jnp.zeros((edge, ref.shape[1]), jnp.bfloat16)
-        ref[edge + rows :] = jnp.zeros((edge, ref.shape[1]), jnp.bfloat16)
-        ref[edge : edge + rows] = values
+    for number, ref in enumerate((points, mirrored)):
+        values = half[number * rows : (number + 1) * rows]
+        ref[:edge] = jnp.zeros((edge, width), jnp.bfloat16)
+        ref[edge + rows :] = jnp.zeros((edge, width), jnp.bfloat16)
+        ref[edge : edge + rows] = jnp.where(values < LIMIT, values, jnp.zeros_like(values))
 
 
 def y_taps(ref, rows, local_z, weights):
@@ -160,9 +172,9 @@
     return total
 
 
-def near_kernel(sizes, local_z, blocks_ref, order_ref, table, partial, coded, points, mirrored):
-    rows, width = coded.shape
-    load_half(sizes, blocks_ref, order_ref, local_z, coded, points, mirrored)
+def near_kernel(local_z, half, table, partial, points, mirrored):
+    rows, width = half.shape[0] // 2, half.shape[1]
+    load_half(half, local_z, points, mirrored)
     for dz in range(KS):
         partial[0, dz] = y_taps(points, rows, local_z, lambda dy: table[dy, dz, :, :width])
         partial[1, dz] = y_taps(mirrored, rows, local_z, lambda dy: table[dy, dz, :, width:])
@@ -178,16 +190,16 @@
 
 
 def grid_kernel(
-    sizes, blocks_ref, measured_ref, mask_ref, order_ref, table, partial, coded_near,
-    out_ref, coded_far, points, mirrored, near, far, lined,
+    half_near, half_far, measured_ref, mask_ref, mirror, table, partial,
+    out_ref, points, mirrored, near, far, lined,
 ):
     parts, coils, local_x, local_y, local_z = out_ref.shape
     channels = parts * coils
-    rows, width = coded_far.shape
+    rows, width = half_near.shape[0] // 2, half_near.shape[1]
     at_x, at_y = lax.axis_index(SPACE[0]), lax.axis_index(SPACE[1])
     own_first = (1 - lax.axis_index(SPACE[2])).astype(jnp.float32)
     edge = REACH * local_z
-    load_half(sizes, blocks_ref, order_ref, local_z, coded_far, points, mirrored)
+    load_half(half_far, local_z, points, mirrored)
     for iteration in range(ITERS - 1):
         totals = [None, None]
         for dz in sorted(range(KS), key=lambda dz: dz == REACH):
@@ -200,10 +212,11 @@
                     shift_z(other, own, shift, local_z, 0, 1.0 - own_first),
                 )
             totals = [part if total is None else total + part for total, part in zip(totals, (own, other))]
-        for ref, mirror_ref, coded, total in ((near, far, coded_near, totals[0]), (far, near, coded_far, totals[1])):
-            values = jnp.where(coded[...] < LIMIT, coded[...], total).astype(jnp.bfloat16)
+        for ref, mirror_ref, coded, total in ((near, far, half_near, totals[0]), (far, near, half_far, totals[1])):
+            coded = coded[:rows]
+            values = jnp.where(coded < LIMIT, coded, total.astype(jnp.bfloat16))
             ref[edge : edge + rows, :width] = values
-            mirror_ref[edge : edge + rows, width:] = dot(order_ref[rows:], values).astype(jnp.bfloat16)
+            mirror_ref[edge : edge + rows, width:] = dot(mirror[...], values).astype(jnp.bfloat16)
     for ref in (near, far):
         ref[:edge] = jnp.zeros((edge, 2 * width), jnp.bfloat16)
         ref[edge + rows :] = jnp.zeros((edge, 2 * width), jnp.bfloat16)
@@ -285,7 +298,6 @@
     taps = jnp.pad(taps, ((0, -taps.shape[0] % 16), (0, 0)))
     steps = [(axis, 1 << bit) for axis in SPACE for bit in range(lax.axis_size(axis).bit_length() - 1)]
     blocks = packed[None]
-    table, order = None, None
     for number, (axis, bit) in enumerate(steps):
         arrived = swap(blocks, axis, bit)
         if number == 0:
@@ -295,42 +307,35 @@
             arrived, flat = after(arrived, call(flat_kernel, "flat", flat_shape, [in_vmem])(taps))
         elif number == 2:
             table_shape = jax.ShapeDtypeStruct((KS, KS, width, 2 * width), jnp.bfloat16)
-            order_shape = jax.ShapeDtypeStruct((2 * half_rows, half_rows), jnp.bfloat16)
+            mirror_shape = jax.ShapeDtypeStruct((half_rows, half_rows), jnp.bfloat16)
             table_fn = functools.partial(table_kernel, size_x)
-            table, order = call(table_fn, "table", (table_shape, order_shape), [in_vmem], outs=2)(flat)
-            arrived, table, order = after(arrived, table, order)
+            table, mirror = call(table_fn, "table", (table_shape, mirror_shape), [in_vmem], outs=2)(flat)
+            turned_shape = jax.ShapeDtypeStruct((half_rows, width), jnp.bfloat16)
+            order_shape = jax.ShapeDtypeStruct((half_rows, half_rows // 2), jnp.bfloat16)
+            turned, order = call(turn_kernel, "turn", (turned_shape, order_shape), [in_vmem], outs=2)(blocks)
+            arrived, table, mirror, turned, order = after(arrived, table, mirror, turned, order)
+            half_shape = jax.ShapeDtypeStruct((2 * half_rows, width), jnp.bfloat16)
+            blocks = call(join_kernel, "join", half_shape, [in_vmem] * 3)(arrived, turned, order)
+            continue
         elif number == len(steps) - 1:
             padded_rows = half_rows + 2 * REACH * local_z
             padded = pltpu.VMEM((padded_rows, width), jnp.bfloat16)
             partial_shape = jax.ShapeDtypeStruct((2, KS, half_rows, width), jnp.float32)
-            coded_shape = jax.ShapeDtypeStruct((half_rows, width), jnp.float32)
-            partial, coded = call(
-                functools.partial(near_kernel, sizes, local_z),
-                "near",
-                (partial_shape, coded_shape),
-                [in_vmem] * 3,
-                [padded, padded],
-                outs=2,
-            )(blocks, order, table)
-            arrived, partial, coded = after(arrived, partial, coded)
+            near_fn = functools.partial(near_kernel, local_z)
+            partial = call(near_fn, "near", partial_shape, [in_vmem] * 2, [padded, padded])(blocks, table)
+            arrived, partial = after(arrived, partial)
             break
         blocks = jnp.concatenate([blocks, arrived], axis=0)
 
     both = pltpu.VMEM((padded_rows, 2 * width), jnp.bfloat16)
+    lined = pltpu.VMEM((local_x * channels * local_y, 128), jnp.float32)
     return call(
-        functools.partial(grid_kernel, sizes),
+        grid_kernel,
         "grid",
         jax.ShapeDtypeStruct(measured.shape, jnp.bfloat16),
         [in_vmem] * 7,
-        [
-            pltpu.VMEM((half_rows, width), jnp.float32),
-            padded,
-            padded,
-            both,
-            both,
-            pltpu.VMEM((local_x * channels * local_y, 128), jnp.float32),
-        ],
-    )(arrived, measured, sample_mask, order, table, partial, coded)
+        [padded, padded, both, both, lined],
+    )(blocks, arrived, measured, sample_mask, mirror, table, partial)
 
 
 def partner(block, axis, bit):

time: 21.6 us -> 21.4 us (level)
    pallas_call x3 -> x5, Pallas kernels: 7.38 us -> 7.34 us  [the longest x1 3.79 us: gathered_body(): call(grid_kernel, 'grid', jax.ShapeDtypeStruct(measured.shape, jnp.bfloat...]
  transfers between devices with their start and end apart: 4 -> 4, of which waited for: 2 -> 2; matrix products, arithmetic and copies ran while one was open for 5% -> 5% of each run, Pallas kernels for 24% -> 25%
where the time goes in v4:
time: 21.4 us; the launch traced here: 21.2 us
  Pallas kernels  10.2 us (48%)
  starting transfers between devices  8.11 us (38%)
  waiting for transfers between devices  1.63 us (8%)
  local copies, waits for them, and re-layouts  1.08 us (5%)
    ppermute x4, starting transfers between devices, swap(): return lax.ppermute(block, axis, [(i, i ^ bit) for i in range(count)])  8.11 us
    pallas_call x1, Pallas kernels, gathered_body(): call(grid_kernel, 'grid', jax.ShapeDtypeStruct(measured.shape, jnp.bfloat...  3.79 us
    pallas_call x1, Pallas kernels, gathered_body(): call(near_fn, 'near', partial_shape, [in_vmem] * 2, [padded, padded])  1.88 us
    pallas_call x1, Pallas kernels, gathered_body(): call(flat_kernel, 'flat', flat_shape, [in_vmem])(taps)  1.85 us
    ppermute x4, waiting for transfers between devices, swap(): return lax.ppermute(block, axis, [(i, i ^ bit) for i in range(count)])  1.63 us
    pallas_call x1, Pallas kernels, gathered_body(): call(table_fn, 'table', (table_shape, mirror_shape), [in_vmem], outs=2)  1.27 us
    pallas_call x1, Pallas kernels, gathered_body(): call(pack_kernel, 'pack', jax.ShapeDtypeStruct((local_x * channels, local...  1.05 us
    reshape x1, local copies, waits for them, and re-layouts, gathered_body(): jnp.moveaxis(kernel, 0, 3).reshape(parts * KS ** 3, coils * 2 * coils)  1.05 us
  transfers between devices with their start and end apart: 4, of which 2 were waited for; matrix products, arithmetic and copies ran while one was open for 5% of the time, Pallas kernels for 25%

profile of v4, /device:TPU:0, one launch (start us, length us, event | category | flops | bytes accessed | tf_op | source)
XLA Modules:
  0.0 21.2 jit_solution(646739093723355582)
XLA Ops:
  0.0 1.1 %pack.1 = bf16[64,128]{1,0:T(8,128)(2,1)S(1)} custom-call(bf16[2,16,2,8,16]{4,3,2,1,0:T(8,128)(2,1)} %measured_ref.1, s32[2,8,16]{2,1,0:T(8,128)} %mask_ref.1), custom_call_target="tpu_custom_call" | custom-call | bytes 4194304 | tf_op jit(solution)/shard_map/pack/pallas_call | solution.py:281
  1.1 3.1 %collective-permute-start = (bf16[1,64,128]{2,1,0:T(8,128)(2,1)S(1)}, bf16[1,64,128]{2,1,0:T(8,128)(2,1)S(1)}, u32[]{:S(2)}, u32[]{:S(2)}) collective-permute-start(bf16[1,64,128]{2,1,0:T(8,128)(2,1)S(1)} %bitcast.2), channel_id=1, source_target_pairs={{0,4},{4,0},{8,12},{12,8},{1,5},{5,1},{9,13},{13,9},{2,6},{6,2},{1... | collective-permute-start | bytes 49160 | tf_op jit(solution)/shard_map/ppermute | solution.py:255
  4.2 1.0 %reshape.3 = bf16[250,512]{1,0:T(8,128)(2,1)S(1)} reshape(bf16[5,5,5,2,512]{4,3,2,1,0:T(2,128)(2,1)} %bitcast.5) | data formatting | bytes 512000 | tf_op jit(solution)/shard_map/reshape | solution.py:297
  5.3 0.6 %collective-permute-done = bf16[1,64,128]{2,1,0:T(8,128)(2,1)S(1)} collective-permute-done((bf16[1,64,128]{2,1,0:T(8,128)(2,1)S(1)}, bf16[1,64,128]{2,1,0:T(8,128)(2,1)S(1)}, u32[]{:S(2)}, u32[]{:S(2)}) %collective-permute-start) | collective-permute-done | bytes 16416 | tf_op jit(solution)/shard_map/ppermute | solution.py:255
  5.9 3.0 %collective-permute-start.1 = (bf16[2,64,128]{2,1,0:T(8,128)(2,1)S(1)}, bf16[2,64,128]{2,1,0:T(8,128)(2,1)S(1)}, u32[]{:S(2)}, u32[]{:S(2)}) collective-permute-start(bf16[2,64,128]{2,1,0:T(8,128)(2,1)S(1)} %pad_maximum_fusion.1), channel_id=1, source_target_pairs={{0,8},{4,12},{8,0},{12,4},{1,9},{5,13},{9,1},{13,5},{2,10},{6,14},... | collective-permute-start | bytes 98312 | tf_op jit(solution)/shard_map/ppermute | solution.py:255
  8.9 1.9 %flat.1 = f32[2,4096,128]{2,1,0:T(8,128)S(1)} custom-call(bf16[256,512]{1,0:T(8,128)(2,1)S(1)} %pad.4.taps_ref), custom_call_target="tpu_custom_call" | custom-call | bytes 4194304 | tf_op jit(solution)/shard_map/flat/pallas_call | solution.py:307
  10.8 0.0 collective-permute-done.1
  10.8 1.9 %collective-permute-start.2 = (bf16[4,64,128]{2,1,0:T(8,128)(2,1)S(1)}, bf16[4,64,128]{2,1,0:T(8,128)(2,1)S(1)}, u32[]{:S(2)}, u32[]{:S(2)}) collective-permute-start(bf16[4,64,128]{2,1,0:T(8,128)(2,1)S(1)} %pad_maximum_fusion.blocks_ref), channel_id=1, source_target_pairs={{0,2},{2,0},{1,3},{3,1},{4,6},{6,4},{5,7},{7,5},{8,10},{10,8},{9,1... | collective-permute-start | bytes 196616 | tf_op jit(solution)/shard_map/ppermute | solution.py:255
  12.7 0.2 turn.1
  12.9 1.3 %table.1 = (bf16[5,5,256,512]{3,2,1,0:T(8,128)(2,1)S(1)}, bf16[256,256]{1,0:T(8,128)(2,1)S(1)}) custom-call(f32[2,4096,128]{2,1,0:T(8,128)S(1)} %flat.1), custom_call_target="tpu_custom_call" | custom-call | bytes 4194304 | tf_op jit(solution)/shard_map/table/pallas_call | solution.py:312
  14.2 1.0 %collective-permute-done.2.blocks_ref = bf16[4,64,128]{2,1,0:T(8,128)(2,1)S(1)} collective-permute-done((bf16[4,64,128]{2,1,0:T(8,128)(2,1)S(1)}, bf16[4,64,128]{2,1,0:T(8,128)(2,1)S(1)}, u32[]{:S(2)}, u32[]{:S(2)}) %collective-permute-start.2) | collective-permute-done | bytes 65568 | tf_op jit(solution)/shard_map/ppermute | solution.py:255
  15.2 0.2 join.1.half.half_near
  15.4 0.0 copy-start
  15.4 0.0 copy-start.1
  15.4 0.1 collective-permute-start.3
  15.5 1.9 %near.1.partial = f32[2,5,256,256]{3,2,1,0:T(8,128)S(1)} custom-call(bf16[512,256]{1,0:T(8,128)(2,1)S(1)} %join.1.half.half_near, bf16[5,5,256,512]{3,2,1,0:T(8,128)(2,1)S(1)} %get-tuple-element.31.table), custom_call_target="tpu_custom_call" | custom-call | bytes 4194304 | tf_op jit(solution)/shard_map/near/pallas_call | solution.py:325
  17.4 0.0 collective-permute-done.3.half_far
  17.4 0.0 copy-done
  17.4 0.0 copy-done.1
  17.4 3.8 %grid.1 = bf16[2,16,2,8,16]{4,3,2,1,0:T(8,128)(2,1)} custom-call(bf16[512,256]{1,0:T(8,128)(2,1)S(1)} %join.1.half.half_near, bf16[512,256]{1,0:T(8,128)(2,1)S(1)} %collective-permute-done.3.half_far, bf16[2,16,2,8,16]{4,3,2,1,0:T(8,128)(2,1)S(1)} %copy-done, s32[2,8,16]{2,1,0:T(8,128)S(1)} %copy-done.1, bf16[256,256]{1,0:T(8,128)(2,1)S(1)} %get-tuple-element.33.mirror, ...), custom_call_target="tpu_custom_call" | custom-call | bytes 4194304 | tf_op jit(solution)/shard_map/grid/pallas_call | solution.py:332
  (3 shorter events, 0.0 us)
Async XLA Ops:
  1.1 4.8 %collective-permute-start = (bf16[1,64,128]{2,1,0:T(8,128)(2,1)S(1)}, bf16[1,64,128]{2,1,0:T(8,128)(2,1)S(1)}, u32[]{:S(2)}, u32[]{:S(2)}) collective-permute-start(bf16[1,64,128]{2,1,0:T(8,128)(2,1)S(1)} %bitcast.2), channel_id=1, source_target_pairs={{0,4},{4,0},{8,12},{12,8},{1,5},{5,1},{9,13},{13,9},{2,6},{6,2},{1... | collective-permute-start | bytes 49160 | tf_op jit(solution)/shard_map/ppermute | solution.py:255
  5.9 4.9 %collective-permute-start.1 = (bf16[2,64,128]{2,1,0:T(8,128)(2,1)S(1)}, bf16[2,64,128]{2,1,0:T(8,128)(2,1)S(1)}, u32[]{:S(2)}, u32[]{:S(2)}) collective-permute-start(bf16[2,64,128]{2,1,0:T(8,128)(2,1)S(1)} %pad_maximum_fusion.1), channel_id=1, source_target_pairs={{0,8},{4,12},{8,0},{12,4},{1,9},{5,13},{9,1},{13,5},{2,10},{6,14},... | collective-permute-start | bytes 98312 | tf_op jit(solution)/shard_map/ppermute | solution.py:255
  10.8 4.3 %collective-permute-start.2 = (bf16[4,64,128]{2,1,0:T(8,128)(2,1)S(1)}, bf16[4,64,128]{2,1,0:T(8,128)(2,1)S(1)}, u32[]{:S(2)}, u32[]{:S(2)}) collective-permute-start(bf16[4,64,128]{2,1,0:T(8,128)(2,1)S(1)} %pad_maximum_fusion.blocks_ref), channel_id=1, source_target_pairs={{0,2},{2,0},{1,3},{3,1},{4,6},{6,4},{5,7},{7,5},{8,10},{10,8},{9,1... | collective-permute-start | bytes 196616 | tf_op jit(solution)/shard_map/ppermute | solution.py:255
  15.4 2.0 %copy-start = (bf16[2,16,2,8,16]{4,3,2,1,0:T(8,128)(2,1)S(1)}, bf16[2,16,2,8,16]{4,3,2,1,0:T(8,128)(2,1)}, u32[]{:S(2)}) copy-start(bf16[2,16,2,8,16]{4,3,2,1,0:T(8,128)(2,1)} %measured_ref.1) | copy-start | bytes 49156
  15.4 2.0 %copy-start.1 = (s32[2,8,16]{2,1,0:T(8,128)S(1)}, s32[2,8,16]{2,1,0:T(8,128)}, u32[]{:S(2)}) copy-start(s32[2,8,16]{2,1,0:T(8,128)} %mask_ref.1) | copy-start | bytes 3076
  15.4 2.0 %collective-permute-start.3 = (bf16[512,256]{1,0:T(8,128)(2,1)S(1)}, bf16[512,256]{1,0:T(8,128)(2,1)S(1)}, u32[]{:S(2)}, u32[]{:S(2)}) collective-permute-start(bf16[512,256]{1,0:T(8,128)(2,1)S(1)} %join.1.half.half_near), channel_id=1, source_target_pairs={{0,1},{1,0},{2,3},{3,2},{4,5},{5,4},{6,7},{7,6},{8,9},{9,8},{10,11... | collective-permute-start | bytes 786440 | tf_op jit(solution)/shard_map/ppermute | solution.py:255

commit v5 on v4

--- a/solution.py
+++ b/solution.py
@@ -9,6 +9,7 @@
 
 COILS = 16
 KS = 5
+NEAR = 3
 REACH = KS // 2
 ITERS = 2
 SPACE = ("gx", "gy", "gz")
@@ -82,9 +83,8 @@
     order[rows:] = one_hot(rows - 1 - row == col)
 
 
-def table_kernel(size_x, flat, table, mirror):
-    rows = mirror.shape[0]
-    mirror[...] = one_hot(rows - 1 - iota((rows, rows), 0) == iota((rows, rows), 1))
+def table_kernel(order_x, flat, table):
+    size_x = len(order_x)
     coils = COILS
     channels = 2 * coils
     width = size_x * channels
@@ -111,9 +111,9 @@
                 mats.append(jnp.concatenate([top, low], axis=0).astype(jnp.bfloat16))
             known = {}
             zero = jnp.zeros((channels, 128), jnp.bfloat16)
-            for x_out in range(size_x):
+            for row, x_out in enumerate(order_x):
                 for j in range(width // 128):
-                    at = [j * group + g for g in range(group)]
+                    at = order_x[j * group : (j + 1) * group]
                     if half == 1:
                         at = [size_x - 1 - a for a in at]
                     which = tuple(a - x_out + REACH if 0 <= a - x_out + REACH < KS else -1 for a in at)
@@ -124,34 +124,34 @@
                                 block = jnp.where(lane_group == g, mats[dx], block)
                         known[which] = block
                     lanes = slice(half * width + j * 128, half * width + j * 128 + 128)
-                    table[dy, dz, x_out * channels : (x_out + 1) * channels, lanes] = known[which]
+                    table[dy, dz, row * channels : (row + 1) * channels, lanes] = known[which]
         return carry
 
     lax.fori_loop(0, table.shape[0] * KS, add_taps, 0)
 
 
-def turn(blocks_ref, order):
-    count_x = blocks_ref.shape[0]
-    at_x = lax.axis_index(SPACE[0])
-    field = jnp.concatenate([blocks_ref[at_x ^ gx] for gx in range(count_x)], axis=0)
+def turn(blocks_ref, order, count_x, count_y):
+    at_x, at_y = lax.axis_index(SPACE[0]) // 2, lax.axis_index(SPACE[1])
+    field = jnp.concatenate(
+        [
+            jnp.concatenate([blocks_ref[(at_y ^ gy) * count_x + (at_x ^ gx)] for gy in range(count_y)], axis=1)
+            for gx in range(count_x)
+        ],
+        axis=0,
+    )
     return dot_nt(order, field).astype(jnp.bfloat16)
 
 
-def turn_kernel(blocks_ref, turned, order):
-    write_orders(order)
-    turned[...] = turn(blocks_ref, order[...])
-
-
-def join_kernel(blocks_ref, turned, order, half):
-    other = turn(blocks_ref, order[...])
-    quarter = order.shape[1]
-    rows = 2 * quarter
-    at_y = lax.axis_index(SPACE[1])
-    for values, place in ((turned[...], at_y), (other, 1 - at_y)):
-        start = pl.multiple_of(place * quarter, quarter)
-        half[pl.ds(start, quarter)] = values[:quarter]
-        start = pl.multiple_of(rows + (1 - place) * quarter, quarter)
-        half[pl.ds(start, quarter)] = values[quarter:]
+def turn_kernel(count_x, count_y, blocks_ref, order, turned):
+    turned[...] = turn(blocks_ref, order[...], count_x, count_y)
+
+
+def join_kernel(count_x, count_y, blocks_ref, turned, order, half):
+    other = turn(blocks_ref, order[...], count_x, count_y)
+    width = turned.shape[1]
+    own_part = lax.axis_index(SPACE[0]) % 2
+    for values, part in ((turned[...], own_part), (other, 1 - own_part)):
+        half[:, pl.ds(pl.multiple_of(part * width, width), width)] = values
 
 
 def load_half(half, local_z, points, mirrored):
@@ -172,12 +172,41 @@
     return total
 
 
-def near_kernel(local_z, half, table, partial, points, mirrored):
+def pair_taps(ref, rows, local_z, weights):
+    total = None
+    for dy in range(0, KS, 2):
+        both = range(dy, min(dy + 2, KS))
+        values = jnp.concatenate([ref[d * local_z : d * local_z + rows] for d in both], axis=1)
+        term = dot_nt(values, jnp.concatenate([weights(d) for d in both], axis=1))
+        total = term if total is None else total + term
+    return total
+
+
+def near_kernel(count_x, local_z, turned, table, partial, points, mirrored):
+    rows, width = turned.shape[0] // 2, turned.shape[1]
+    load_half(turned, local_z, points, mirrored)
+    first = lax.axis_index(SPACE[0]) % 2 * width
+    for number, ref in enumerate((points, mirrored)):
+        lanes = pl.ds(pl.multiple_of(number * table.shape[3] // 2 + first, width), width)
+        for dz in range(NEAR):
+            partial[number, dz] = pair_taps(ref, rows, local_z, lambda dy: table[dy, dz, :, lanes])
+
+
+def rest_kernel(count_x, local_z, half, table, before, partial, points, mirrored, points_x, mirrored_x):
     rows, width = half.shape[0] // 2, half.shape[1]
+    part = width // 2
+    first = pl.multiple_of((1 - lax.axis_index(SPACE[0]) % 2) * part, part)
     load_half(half, local_z, points, mirrored)
-    for dz in range(KS):
-        partial[0, dz] = y_taps(points, rows, local_z, lambda dy: table[dy, dz, :, :width])
-        partial[1, dz] = y_taps(mirrored, rows, local_z, lambda dy: table[dy, dz, :, width:])
+    load_half(half.at[:, pl.ds(first, part)], local_z, points_x, mirrored_x)
+    for number, (ref, ref_x) in enumerate(((points, points_x), (mirrored, mirrored_x))):
+        every = slice(number * width, (number + 1) * width)
+        lanes = pl.ds(pl.multiple_of(number * width + first, part), part)
+        for dz in range(NEAR):
+            partial[number, dz] = before[number, dz] + pair_taps(
+                ref_x, rows, local_z, lambda dy: table[dy, dz, :, lanes]
+            )
+        for dz in range(NEAR, KS):
+            partial[number, dz] = y_taps(ref, rows, local_z, lambda dy: table[dy, dz, :, every])
 
 
 def shift_z(own, other, shift, local_z, dim, own_first):
@@ -190,16 +219,20 @@
 
 
 def grid_kernel(
-    half_near, half_far, measured_ref, mask_ref, mirror, table, partial,
-    out_ref, points, mirrored, near, far, lined,
+    half_near, half_far, measured_ref, mask_ref, order, table, partial,
+    out_ref, points, mirrored, near, far, near_mirrored, far_mirrored, lined,
 ):
     parts, coils, local_x, local_y, local_z = out_ref.shape
     channels = parts * coils
     rows, width = half_near.shape[0] // 2, half_near.shape[1]
     at_x, at_y = lax.axis_index(SPACE[0]), lax.axis_index(SPACE[1])
+    at_x = at_x % 2 * (lax.axis_size(SPACE[0]) // 2) + at_x // 2
     own_first = (1 - lax.axis_index(SPACE[2])).astype(jnp.float32)
     edge = REACH * local_z
     load_half(half_far, local_z, points, mirrored)
+    for ref in (near, far, near_mirrored, far_mirrored):
+        ref[:edge] = jnp.zeros((edge, width), jnp.bfloat16)
+        ref[edge + rows :] = jnp.zeros((edge, width), jnp.bfloat16)
     for iteration in range(ITERS - 1):
         totals = [None, None]
         for dz in sorted(range(KS), key=lambda dz: dz == REACH):
@@ -212,25 +245,24 @@
                     shift_z(other, own, shift, local_z, 0, 1.0 - own_first),
                 )
             totals = [part if total is None else total + part for total, part in zip(totals, (own, other))]
-        for ref, mirror_ref, coded, total in ((near, far, half_near, totals[0]), (far, near, half_far, totals[1])):
+        halves = ((near, far_mirrored, half_near, totals[0]), (far, near_mirrored, half_far, totals[1]))
+        for ref, mirror_ref, coded, total in halves:
             coded = coded[:rows]
             values = jnp.where(coded < LIMIT, coded, total.astype(jnp.bfloat16))
-            ref[edge : edge + rows, :width] = values
-            mirror_ref[edge : edge + rows, width:] = dot(mirror[...], values).astype(jnp.bfloat16)
-    for ref in (near, far):
-        ref[:edge] = jnp.zeros((edge, 2 * width), jnp.bfloat16)
-        ref[edge + rows :] = jnp.zeros((edge, 2 * width), jnp.bfloat16)
+            ref[edge : edge + rows] = values
+            mirror_ref[edge : edge + rows] = dot(order[rows:], values).astype(jnp.bfloat16)
 
     own_rows = local_x * channels
     own_points = local_y * local_z
     start_x = pl.multiple_of(at_x * own_rows, own_rows)
     result = None
-    for dy in range(KS):
-        weights = jnp.concatenate([table[dy, dz, pl.ds(start_x, own_rows), :] for dz in range(KS)], axis=0)
-        start = pl.multiple_of((at_y * local_y + dy) * local_z, local_z)
-        window = jnp.concatenate([near[pl.ds(start, own_points), :], far[pl.ds(start, own_points), :]], axis=0)
-        term = dot_nt(weights, window)
-        result = term if result is None else result + term
+    for first, refs in ((0, (near, far)), (width, (near_mirrored, far_mirrored))):
+        for dy in range(KS):
+            taps = [table[dy, dz, pl.ds(start_x, own_rows), first : first + width] for dz in range(KS)]
+            start = pl.multiple_of((at_y * local_y + dy) * local_z, local_z)
+            window = jnp.concatenate([ref[pl.ds(start, own_points), :] for ref in refs], axis=0)
+            term = dot_nt(jnp.concatenate(taps, axis=0), window)
+            result = term if result is None else result + term
     total = None
     for dz in range(KS):
         own = result[dz * own_rows : (dz + 1) * own_rows, :own_points]
@@ -296,7 +328,16 @@
 
     taps = jnp.moveaxis(kernel, 0, 3).reshape(parts * KS ** 3, coils * 2 * coils)
     taps = jnp.pad(taps, ((0, -taps.shape[0] % 16), (0, 0)))
-    steps = [(axis, 1 << bit) for axis in SPACE for bit in range(lax.axis_size(axis).bit_length() - 1)]
+    bits = [[(axis, 1 << bit) for bit in range(lax.axis_size(axis).bit_length() - 1)] for axis in SPACE]
+    steps = bits[0][1:] + bits[1] + bits[0][:1] + bits[2]
+    order_x = [gx * local_x + x for odd in range(2) for gx in range(odd, sizes[0], 2) for x in range(local_x)]
+    half_x = sizes[0] // 2
+    padded_rows = half_rows + 2 * REACH * local_z
+    padded_part = pltpu.VMEM((padded_rows, width // 2), jnp.bfloat16)
+    padded = pltpu.VMEM((padded_rows, width), jnp.bfloat16)
+    partial_shape = jax.ShapeDtypeStruct((2, KS, half_rows, width), jnp.float32)
+    near_shape = jax.ShapeDtypeStruct((2, NEAR, half_rows, width), jnp.float32)
+    scratch = [padded, padded, padded_part, padded_part]
     blocks = packed[None]
     for number, (axis, bit) in enumerate(steps):
         arrived = swap(blocks, axis, bit)
@@ -304,38 +345,38 @@
             arrived, taps = after(arrived, taps)
         elif number == 1:
             flat_shape = jax.ShapeDtypeStruct((2, taps.shape[0] * coils, 128), jnp.float32)
-            arrived, flat = after(arrived, call(flat_kernel, "flat", flat_shape, [in_vmem])(taps))
+            order_shape = jax.ShapeDtypeStruct((2 * half_rows, half_rows), jnp.bfloat16)
+            order = call(write_orders, "order", order_shape, [])()
+            flat = call(flat_kernel, "flat", flat_shape, [in_vmem])(taps)
+            arrived, flat, order = after(arrived, flat, order)
         elif number == 2:
             table_shape = jax.ShapeDtypeStruct((KS, KS, width, 2 * width), jnp.bfloat16)
-            mirror_shape = jax.ShapeDtypeStruct((half_rows, half_rows), jnp.bfloat16)
-            table_fn = functools.partial(table_kernel, size_x)
-            table, mirror = call(table_fn, "table", (table_shape, mirror_shape), [in_vmem], outs=2)(flat)
-            turned_shape = jax.ShapeDtypeStruct((half_rows, width), jnp.bfloat16)
-            order_shape = jax.ShapeDtypeStruct((half_rows, half_rows // 2), jnp.bfloat16)
-            turned, order = call(turn_kernel, "turn", (turned_shape, order_shape), [in_vmem], outs=2)(blocks)
-            arrived, table, mirror, turned, order = after(arrived, table, mirror, turned, order)
+            table = call(functools.partial(table_kernel, order_x), "table", table_shape, [in_vmem])(flat)
+            turned_shape = jax.ShapeDtypeStruct((2 * half_rows, width // 2), jnp.bfloat16)
+            turn_fn = functools.partial(turn_kernel, half_x, sizes[1])
+            turned = call(turn_fn, "turn", turned_shape, [in_vmem] * 2)(blocks, order)
+            near_fn = functools.partial(near_kernel, half_x, local_z)
+            partial = call(near_fn, "near", near_shape, [in_vmem] * 2, [padded_part] * 2)(turned, table)
+            arrived, table, turned, partial = after(arrived, table, turned, partial)
             half_shape = jax.ShapeDtypeStruct((2 * half_rows, width), jnp.bfloat16)
-            blocks = call(join_kernel, "join", half_shape, [in_vmem] * 3)(arrived, turned, order)
+            join_fn = functools.partial(join_kernel, half_x, sizes[1])
+            blocks = call(join_fn, "join", half_shape, [in_vmem] * 3)(arrived, turned, order)
             continue
-        elif number == len(steps) - 1:
-            padded_rows = half_rows + 2 * REACH * local_z
-            padded = pltpu.VMEM((padded_rows, width), jnp.bfloat16)
-            partial_shape = jax.ShapeDtypeStruct((2, KS, half_rows, width), jnp.float32)
-            near_fn = functools.partial(near_kernel, local_z)
-            partial = call(near_fn, "near", partial_shape, [in_vmem] * 2, [padded, padded])(blocks, table)
+        elif number == 3:
+            rest_fn = functools.partial(rest_kernel, half_x, local_z)
+            partial = call(rest_fn, "rest", partial_shape, [in_vmem] * 3, scratch)(blocks, table, partial)
             arrived, partial = after(arrived, partial)
             break
         blocks = jnp.concatenate([blocks, arrived], axis=0)
 
-    both = pltpu.VMEM((padded_rows, 2 * width), jnp.bfloat16)
     lined = pltpu.VMEM((local_x * channels * local_y, 128), jnp.float32)
     return call(
         grid_kernel,
         "grid",
         jax.ShapeDtypeStruct(measured.shape, jnp.bfloat16),
         [in_vmem] * 7,
-        [padded, padded, both, both, lined],
-    )(blocks, arrived, measured, sample_mask, mirror, table, partial)
+        [padded] * 6 + [lined],
+    )(blocks, arrived, measured, sample_mask, order, table, partial)
 
 
 def partner(block, axis, bit):
@@ -434,7 +475,7 @@
         parts, coils, local_x, local_y, local_z = measured.shape
         width = grid[0] * local_x * parts * coils
         points = grid[1] * local_y * local_z
-        small = width == 256 and grid[1:] == (2, 2) and points == 256 and local_y * local_z == 128
+        small = width == 256 and grid == (4, 2, 2) and points == 256 and local_y * local_z == 128
         if small:
             return gathered_body(measured, sample_mask, kernel)
         return halo_body(measured, sample_mask, kernel)

time: 21.4 us -> 21 us (0.981)
  waiting for transfers between devices: 1.63 us -> 0.78 us
  Pallas kernels: 10.2 us -> 10.8 us
    ppermute x4, waiting for transfers between devices: 1.63 us -> 0.78 us  [swap(): return lax.ppermute(block, axis, [(i, i ^ bit) for i in range(count)])]
    pallas_call x5 -> x7, Pallas kernels: 5.4 us -> 6.05 us  [the longest x1 1.85 us: gathered_body(): flat = call(flat_kernel, 'flat', flat_shape, [in_vmem])(taps)]
  transfers between devices with their start and end apart: 4 -> 4, of which waited for: 2 -> 2; matrix products, arithmetic and copies ran while one was open for 5% -> 5% of each run, Pallas kernels for 25% -> 28%
where the time goes in v5:
time: 21 us; the launch traced here: 20.9 us
  Pallas kernels  10.8 us (51%)
  starting transfers between devices  8.05 us (38%)
  local copies, waits for them, and re-layouts  1.08 us (5%)
  waiting for transfers between devices  0.78 us (4%)
    ppermute x4, starting transfers between devices, swap(): return lax.ppermute(block, axis, [(i, i ^ bit) for i in range(count)])  8.05 us
    pallas_call x1, Pallas kernels, gathered_body(): call(grid_kernel, 'grid', jax.ShapeDtypeStruct(measured.shape, jnp.bfloat...  3.73 us
    pallas_call x1, Pallas kernels, gathered_body(): flat = call(flat_kernel, 'flat', flat_shape, [in_vmem])(taps)  1.85 us
    pallas_call x1, Pallas kernels, gathered_body(): call(rest_fn, 'rest', partial_shape, [in_vmem] * 3, scratch)  1.52 us
    pallas_call x1, Pallas kernels, gathered_body(): call(functools.partial(table_kernel, order_x), 'table', table_shape, [in_...  1.33 us
    pallas_call x1, Pallas kernels, gathered_body(): call(pack_kernel, 'pack', jax.ShapeDtypeStruct((local_x * channels, local...  1.05 us
    reshape x1, local copies, waits for them, and re-layouts, gathered_body(): jnp.moveaxis(kernel, 0, 3).reshape(parts * KS ** 3, coils * 2 * coils)  1.05 us
    pallas_call x1, Pallas kernels, gathered_body(): call(near_fn, 'near', near_shape, [in_vmem] * 2, [padded_part] * 2)  0.83 us
  transfers between devices with their start and end apart: 4, of which 2 were waited for; matrix products, arithmetic and copies ran while one was open for 5% of the time, Pallas kernels for 28%

profile of v5, /device:TPU:0, one launch (start us, length us, event | category | flops | bytes accessed | tf_op | source)
XLA Modules:
  0.0 20.9 jit_solution(1685910364829664009)
XLA Ops:
  0.0 1.1 %pack.1 = bf16[64,128]{1,0:T(8,128)(2,1)S(1)} custom-call(bf16[2,16,2,8,16]{4,3,2,1,0:T(8,128)(2,1)} %measured_ref.1, s32[2,8,16]{2,1,0:T(8,128)} %mask_ref.1), custom_call_target="tpu_custom_call" | custom-call | bytes 4194304 | tf_op jit(solution)/shard_map/pack/pallas_call | solution.py:313
  1.1 4.1 %collective-permute-start = (bf16[1,64,128]{2,1,0:T(8,128)(2,1)S(1)}, bf16[1,64,128]{2,1,0:T(8,128)(2,1)S(1)}, u32[]{:S(2)}, u32[]{:S(2)}) collective-permute-start(bf16[1,64,128]{2,1,0:T(8,128)(2,1)S(1)} %bitcast.2), channel_id=1, source_target_pairs={{0,8},{4,12},{8,0},{12,4},{1,9},{5,13},{9,1},{13,5},{2,10},{6,14},... | collective-permute-start | bytes 49160 | tf_op jit(solution)/shard_map/ppermute | solution.py:287
  5.2 1.0 %reshape.3 = bf16[250,512]{1,0:T(8,128)(2,1)S(1)} reshape(bf16[5,5,5,2,512]{4,3,2,1,0:T(2,128)(2,1)} %bitcast.5) | data formatting | bytes 512000 | tf_op jit(solution)/shard_map/reshape | solution.py:329
  6.3 0.6 %collective-permute-done = bf16[1,64,128]{2,1,0:T(8,128)(2,1)S(1)} collective-permute-done((bf16[1,64,128]{2,1,0:T(8,128)(2,1)S(1)}, bf16[1,64,128]{2,1,0:T(8,128)(2,1)S(1)}, u32[]{:S(2)}, u32[]{:S(2)}) %collective-permute-start) | collective-permute-done | bytes 16416 | tf_op jit(solution)/shard_map/ppermute | solution.py:287
  6.9 1.9 %collective-permute-start.1 = (bf16[2,64,128]{2,1,0:T(8,128)(2,1)S(1)}, bf16[2,64,128]{2,1,0:T(8,128)(2,1)S(1)}, u32[]{:S(2)}, u32[]{:S(2)}) collective-permute-start(bf16[2,64,128]{2,1,0:T(8,128)(2,1)S(1)} %pad_maximum_fusion.1), channel_id=1, source_target_pairs={{0,2},{2,0},{1,3},{3,1},{4,6},{6,4},{5,7},{7,5},{8,10},{10,8},{9,1... | collective-permute-start | bytes 98312 | tf_op jit(solution)/shard_map/ppermute | solution.py:287
  8.8 1.9 %flat.1 = f32[2,4096,128]{2,1,0:T(8,128)S(1)} custom-call(bf16[256,512]{1,0:T(8,128)(2,1)S(1)} %pad.4.taps_ref), custom_call_target="tpu_custom_call" | custom-call | bytes 4194304 | tf_op jit(solution)/shard_map/flat/pallas_call | solution.py:350
  10.7 0.1 collective-permute-done.1
  10.8 2.0 %collective-permute-start.2 = (bf16[4,64,128]{2,1,0:T(8,128)(2,1)S(1)}, bf16[4,64,128]{2,1,0:T(8,128)(2,1)S(1)}, u32[]{:S(2)}, u32[]{:S(2)}) collective-permute-start(bf16[4,64,128]{2,1,0:T(8,128)(2,1)S(1)} %pad_maximum_fusion.blocks_ref), channel_id=1, source_target_pairs={{0,4},{4,0},{8,12},{12,8},{1,5},{5,1},{9,13},{13,9},{2,6},{6,2},{1... | collective-permute-start | bytes 196616 | tf_op jit(solution)/shard_map/ppermute | solution.py:287
  12.8 0.2 %turn.1.turned = bf16[512,128]{1,0:T(8,128)(2,1)S(1)} custom-call(bf16[4,64,128]{2,1,0:T(8,128)(2,1)S(1)} %pad_maximum_fusion.blocks_ref, bf16[512,256]{1,0:T(8,128)(2,1)S(1)} %order.1), custom_call_target="tpu_custom_call" | custom-call | bytes 4194304 | tf_op jit(solution)/shard_map/turn/pallas_call | solution.py:357
  13.1 1.3 %table.1 = bf16[5,5,256,512]{3,2,1,0:T(8,128)(2,1)S(1)} custom-call(f32[2,4096,128]{2,1,0:T(8,128)S(1)} %flat.1), custom_call_target="tpu_custom_call" | custom-call | bytes 4194304 | tf_op jit(solution)/shard_map/table/pallas_call | solution.py:354
  14.4 0.8 %near.1.before = f32[2,3,256,256]{3,2,1,0:T(8,128)S(1)} custom-call(bf16[512,128]{1,0:T(8,128)(2,1)S(1)} %turn.1.turned, bf16[5,5,256,512]{3,2,1,0:T(8,128)(2,1)S(1)} %table.1), custom_call_target="tpu_custom_call" | custom-call | bytes 4194304 | tf_op jit(solution)/shard_map/near/pallas_call | solution.py:359
  15.2 0.0 collective-permute-done.2.blocks_ref
  15.2 0.2 %join.1.half.half_near = bf16[512,256]{1,0:T(8,128)(2,1)S(1)} custom-call(bf16[4,64,128]{2,1,0:T(8,128)(2,1)S(1)} %collective-permute-done.2.blocks_ref, bf16[512,128]{1,0:T(8,128)(2,1)S(1)} %turn.1.turned, bf16[512,256]{1,0:T(8,128)(2,1)S(1)} %order.1), custom_call_target="tpu_custom_call" | custom-call | bytes 4194304 | tf_op jit(solution)/shard_map/join/pallas_call | solution.py:363
  15.5 0.0 copy-start
  15.5 0.0 copy-start.1
  15.5 0.1 collective-permute-start.3
  15.6 1.5 %rest.1.partial = f32[2,5,256,256]{3,2,1,0:T(8,128)S(1)} custom-call(bf16[512,256]{1,0:T(8,128)(2,1)S(1)} %join.1.half.half_near, bf16[5,5,256,512]{3,2,1,0:T(8,128)(2,1)S(1)} %table.1, f32[2,3,256,256]{3,2,1,0:T(8,128)S(1)} %near.1.before), custom_call_target="tpu_custom_call" | custom-call | bytes 4194304 | tf_op jit(solution)/shard_map/rest/pallas_call | solution.py:367
  17.1 0.0 collective-permute-done.3.half_far
  17.1 0.0 copy-done
  17.1 0.0 copy-done.1
  17.1 3.7 %grid.1 = bf16[2,16,2,8,16]{4,3,2,1,0:T(8,128)(2,1)} custom-call(bf16[512,256]{1,0:T(8,128)(2,1)S(1)} %join.1.half.half_near, bf16[512,256]{1,0:T(8,128)(2,1)S(1)} %collective-permute-done.3.half_far, bf16[2,16,2,8,16]{4,3,2,1,0:T(8,128)(2,1)S(1)} %copy-done, s32[2,8,16]{2,1,0:T(8,128)S(1)} %copy-done.1, bf16[512,256]{1,0:T(8,128)(2,1)S(1)} %order.1, ...), custom_call_target="tpu_custom_call" | custom-call | bytes 4194304 | tf_op jit(solution)/shard_map/grid/pallas_call | solution.py:373
  (4 shorter events, 0.1 us)
Async XLA Ops:
  1.1 5.8 %collective-permute-start = (bf16[1,64,128]{2,1,0:T(8,128)(2,1)S(1)}, bf16[1,64,128]{2,1,0:T(8,128)(2,1)S(1)}, u32[]{:S(2)}, u32[]{:S(2)}) collective-permute-start(bf16[1,64,128]{2,1,0:T(8,128)(2,1)S(1)} %bitcast.2), channel_id=1, source_target_pairs={{0,8},{4,12},{8,0},{12,4},{1,9},{5,13},{9,1},{13,5},{2,10},{6,14},... | collective-permute-start | bytes 49160 | tf_op jit(solution)/shard_map/ppermute | solution.py:287
  6.9 3.9 %collective-permute-start.1 = (bf16[2,64,128]{2,1,0:T(8,128)(2,1)S(1)}, bf16[2,64,128]{2,1,0:T(8,128)(2,1)S(1)}, u32[]{:S(2)}, u32[]{:S(2)}) collective-permute-start(bf16[2,64,128]{2,1,0:T(8,128)(2,1)S(1)} %pad_maximum_fusion.1), channel_id=1, source_target_pairs={{0,2},{2,0},{1,3},{3,1},{4,6},{6,4},{5,7},{7,5},{8,10},{10,8},{9,1... | collective-permute-start | bytes 98312 | tf_op jit(solution)/shard_map/ppermute | solution.py:287
  10.8 4.4 %collective-permute-start.2 = (bf16[4,64,128]{2,1,0:T(8,128)(2,1)S(1)}, bf16[4,64,128]{2,1,0:T(8,128)(2,1)S(1)}, u32[]{:S(2)}, u32[]{:S(2)}) collective-permute-start(bf16[4,64,128]{2,1,0:T(8,128)(2,1)S(1)} %pad_maximum_fusion.blocks_ref), channel_id=1, source_target_pairs={{0,4},{4,0},{8,12},{12,8},{1,5},{5,1},{9,13},{13,9},{2,6},{6,2},{1... | collective-permute-start | bytes 196616 | tf_op jit(solution)/shard_map/ppermute | solution.py:287
  15.5 1.6 %copy-start = (bf16[2,16,2,8,16]{4,3,2,1,0:T(8,128)(2,1)S(1)}, bf16[2,16,2,8,16]{4,3,2,1,0:T(8,128)(2,1)}, u32[]{:S(2)}) copy-start(bf16[2,16,2,8,16]{4,3,2,1,0:T(8,128)(2,1)} %measured_ref.1) | copy-start | bytes 49156
  15.5 1.6 %copy-start.1 = (s32[2,8,16]{2,1,0:T(8,128)S(1)}, s32[2,8,16]{2,1,0:T(8,128)}, u32[]{:S(2)}) copy-start(s32[2,8,16]{2,1,0:T(8,128)} %mask_ref.1) | copy-start | bytes 3076
  15.5 1.6 %collective-permute-start.3 = (bf16[512,256]{1,0:T(8,128)(2,1)S(1)}, bf16[512,256]{1,0:T(8,128)(2,1)S(1)}, u32[]{:S(2)}, u32[]{:S(2)}) collective-permute-start(bf16[512,256]{1,0:T(8,128)(2,1)S(1)} %join.1.half.half_near), channel_id=1, source_target_pairs={{0,1},{1,0},{2,3},{3,2},{4,5},{5,4},{6,7},{7,6},{8,9},{9,8},{10,11... | collective-permute-start | bytes 786440 | tf_op jit(solution)/shard_map/ppermute | solution.py:287

commit v6 on v5

--- a/solution.py
+++ b/solution.py
@@ -9,7 +9,7 @@
 
 COILS = 16
 KS = 5
-NEAR = 3
+STRIDE = COILS + 1
 REACH = KS // 2
 ITERS = 2
 SPACE = ("gx", "gy", "gz")
@@ -45,16 +45,17 @@
         copy.wait()
     parts, coils, size_x, size_y, size_z = measured_ref.shape
     channels = parts * coils
-    rows = channels * size_y
     for x in range(size_x):
         values = measured_ref[:, :, x].astype(jnp.float32)
         sampled = (mask_ref[x] == 1)[None, None]
-        lined[x, :, :size_z] = jnp.where(sampled, values, UNSAMPLED).reshape(rows, size_z)
+        coded = jnp.where(sampled, values, UNSAMPLED).reshape(channels, size_y, size_z)
+        for row in range(channels):
+            lined[x, row * (size_y + 1) : row * (size_y + 1) + size_y, :size_z] = coded[row]
     lane_y = iota((channels, size_y * size_z), 1) // size_z
     for x in range(size_x):
         packed = None
         for y in range(size_y):
-            piece = lined[x, pl.ds(y, channels, stride=size_y), :]
+            piece = lined[x, pl.ds(y, channels, stride=size_y + 1), :]
             if y > 0:
                 piece = jnp.where(lane_y == y, pltpu.roll(piece, y * size_z, 1), packed)
             packed = piece
@@ -72,7 +73,7 @@
         tile = (c // per_tile) * 128
         spread = dot(taps_ref[:, tile : tile + 128], pick)
         for half in range(2):
-            rows_of_coil = pl.ds(c, taps_ref.shape[0], stride=coils)
+            rows_of_coil = pl.ds(c, taps_ref.shape[0], stride=STRIDE)
             flat[half, rows_of_coil, :] = spread[:, half * 128 : half * 128 + 128]
 
 
@@ -98,10 +99,8 @@
             mats = []
             for dx in range(KS):
                 tap = (dx * KS + dy) * KS + dz
-                real_at = pl.multiple_of(2 * tap * coils, coils)
-                imag_at = pl.multiple_of((2 * tap + 1) * coils, coils)
-                real = flat[half, pl.ds(real_at, coils), :]
-                imag = flat[half, pl.ds(imag_at, coils), :]
+                real = flat[half, pl.ds(2 * tap * STRIDE, coils), :]
+                imag = flat[half, pl.ds((2 * tap + 1) * STRIDE, coils), :]
                 if half == 0:
                     top = jnp.where(imaginary, -imag, real)
                     low = jnp.where(imaginary, real, imag)
@@ -130,7 +129,7 @@
     lax.fori_loop(0, table.shape[0] * KS, add_taps, 0)
 
 
-def turn(blocks_ref, order, count_x, count_y):
+def turn_kernel(count_x, count_y, blocks_ref, order, turned):
     at_x, at_y = lax.axis_index(SPACE[0]) // 2, lax.axis_index(SPACE[1])
     field = jnp.concatenate(
         [
@@ -139,19 +138,7 @@
         ],
         axis=0,
     )
-    return dot_nt(order, field).astype(jnp.bfloat16)
-
-
-def turn_kernel(count_x, count_y, blocks_ref, order, turned):
-    turned[...] = turn(blocks_ref, order[...], count_x, count_y)
-
-
-def join_kernel(count_x, count_y, blocks_ref, turned, order, half):
-    other = turn(blocks_ref, order[...], count_x, count_y)
-    width = turned.shape[1]
-    own_part = lax.axis_index(SPACE[0]) % 2
-    for values, part in ((turned[...], own_part), (other, 1 - own_part)):
-        half[:, pl.ds(pl.multiple_of(part * width, width), width)] = values
+    turned[...] = dot_nt(order[...], field).astype(jnp.bfloat16)
 
 
 def load_half(half, local_z, points, mirrored):
@@ -164,14 +151,6 @@
         ref[edge : edge + rows] = jnp.where(values < LIMIT, values, jnp.zeros_like(values))
 
 
-def y_taps(ref, rows, local_z, weights):
-    total = None
-    for dy in range(KS):
-        term = dot_nt(ref[dy * local_z : dy * local_z + rows], weights(dy))
-        total = term if total is None else total + term
-    return total
-
-
 def pair_taps(ref, rows, local_z, weights):
     total = None
     for dy in range(0, KS, 2):
@@ -182,31 +161,37 @@
     return total
 
 
-def near_kernel(count_x, local_z, turned, table, partial, points, mirrored):
-    rows, width = turned.shape[0] // 2, turned.shape[1]
-    load_half(turned, local_z, points, mirrored)
-    first = lax.axis_index(SPACE[0]) % 2 * width
-    for number, ref in enumerate((points, mirrored)):
+def own_lanes(width, own_parity):
+    parity = lax.axis_index(SPACE[0]) % 2
+    return pl.multiple_of((parity if own_parity else 1 - parity) * width, width)
+
+
+def give(half, local_z, own_z, own_parity, table, points, mirrored):
+    rows, width = half.shape[0] // 2, half.shape[1]
+    load_half(half, local_z, points, mirrored)
+    first = own_lanes(width, own_parity)
+
+    def given(target, dz):
+        number = target if own_z else 1 - target
         lanes = pl.ds(pl.multiple_of(number * table.shape[3] // 2 + first, width), width)
-        for dz in range(NEAR):
-            partial[number, dz] = pair_taps(ref, rows, local_z, lambda dy: table[dy, dz, :, lanes])
-
-
-def rest_kernel(count_x, local_z, half, table, before, partial, points, mirrored, points_x, mirrored_x):
-    rows, width = half.shape[0] // 2, half.shape[1]
-    part = width // 2
-    first = pl.multiple_of((1 - lax.axis_index(SPACE[0]) % 2) * part, part)
-    load_half(half, local_z, points, mirrored)
-    load_half(half.at[:, pl.ds(first, part)], local_z, points_x, mirrored_x)
-    for number, (ref, ref_x) in enumerate(((points, points_x), (mirrored, mirrored_x))):
-        every = slice(number * width, (number + 1) * width)
-        lanes = pl.ds(pl.multiple_of(number * width + first, part), part)
-        for dz in range(NEAR):
-            partial[number, dz] = before[number, dz] + pair_taps(
-                ref_x, rows, local_z, lambda dy: table[dy, dz, :, lanes]
-            )
-        for dz in range(NEAR, KS):
-            partial[number, dz] = y_taps(ref, rows, local_z, lambda dy: table[dy, dz, :, every])
+        ref = mirrored if number else points
+        return pair_taps(ref, rows, local_z, lambda dy: table[dy, dz, :, lanes])
+
+    return given
+
+
+def near_kernel(local_z, half, table, partial, points, mirrored):
+    given = give(half, local_z, True, True, table, points, mirrored)
+    for target in range(2):
+        for dz in range(KS):
+            partial[target, dz] = given(target, dz)
+
+
+def more_kernel(local_z, own_z, own_parity, half, table, before, partial, points, mirrored):
+    given = give(half, local_z, own_z, own_parity, table, points, mirrored)
+    for target in range(2):
+        for dz in range(KS):
+            partial[target, dz] = before[target, dz] + given(target, dz)
 
 
 def shift_z(own, other, shift, local_z, dim, own_first):
@@ -219,17 +204,20 @@
 
 
 def grid_kernel(
-    half_near, half_far, measured_ref, mask_ref, order, table, partial,
-    out_ref, points, mirrored, near, far, near_mirrored, far_mirrored, lined,
+    near_own, near_other, far_own, far_other, measured_ref, mask_ref, order, table, partial,
+    out_ref, points, mirrored, coded_ref, near, far, near_mirrored, far_mirrored, lined,
 ):
     parts, coils, local_x, local_y, local_z = out_ref.shape
     channels = parts * coils
-    rows, width = half_near.shape[0] // 2, half_near.shape[1]
+    rows, width = near_own.shape[0] // 2, 2 * near_own.shape[1]
     at_x, at_y = lax.axis_index(SPACE[0]), lax.axis_index(SPACE[1])
     at_x = at_x % 2 * (lax.axis_size(SPACE[0]) // 2) + at_x // 2
     own_first = (1 - lax.axis_index(SPACE[2])).astype(jnp.float32)
     edge = REACH * local_z
-    load_half(half_far, local_z, points, mirrored)
+    given = give(far_other, local_z, False, False, table, points, mirrored)
+    for number, halves in enumerate(((near_own, near_other), (far_own, far_other))):
+        for half, own_parity in zip(halves, (True, False)):
+            coded_ref[number, :, pl.ds(own_lanes(width // 2, own_parity), width // 2)] = half[:rows]
     for ref in (near, far, near_mirrored, far_mirrored):
         ref[:edge] = jnp.zeros((edge, width), jnp.bfloat16)
         ref[edge + rows :] = jnp.zeros((edge, width), jnp.bfloat16)
@@ -237,17 +225,16 @@
         totals = [None, None]
         for dz in sorted(range(KS), key=lambda dz: dz == REACH):
             shift = dz - REACH
-            own = partial[0, dz] + y_taps(mirrored, rows, local_z, lambda dy: table[dy, dz, :, width:])
-            other = partial[1, dz] + y_taps(points, rows, local_z, lambda dy: table[dy, dz, :, :width])
+            own, other = (partial[target, dz] + given(target, dz) for target in range(2))
             if shift != 0:
                 own, other = (
                     shift_z(own, other, shift, local_z, 0, own_first),
                     shift_z(other, own, shift, local_z, 0, 1.0 - own_first),
                 )
             totals = [part if total is None else total + part for total, part in zip(totals, (own, other))]
-        halves = ((near, far_mirrored, half_near, totals[0]), (far, near_mirrored, half_far, totals[1]))
+        halves = ((near, far_mirrored, coded_ref.at[0], totals[0]), (far, near_mirrored, coded_ref.at[1], totals[1]))
         for ref, mirror_ref, coded, total in halves:
-            coded = coded[:rows]
+            coded = coded[...]
             values = jnp.where(coded < LIMIT, coded, total.astype(jnp.bfloat16))
             ref[edge : edge + rows] = values
             mirror_ref[edge : edge + rows] = dot(order[rows:], values).astype(jnp.bfloat16)
@@ -273,9 +260,10 @@
 
     for y in range(local_y):
         piece = total if y == 0 else pltpu.roll(total, own_points - y * local_z, 1)
-        lined[pl.ds(y, own_rows, stride=local_y), :] = piece
+        lined[pl.ds(y, own_rows, stride=local_y + 1), :] = piece
     for x in range(local_x):
-        values = lined[x * channels * local_y : (x + 1) * channels * local_y, :local_z]
+        starts = [row * (local_y + 1) for row in range(x * channels, (x + 1) * channels)]
+        values = jnp.stack([lined[start : start + local_y, :local_z] for start in starts])
         values = values.reshape(parts, coils, local_y, local_z)
         sampled = (mask_ref[x] == 1)[None, None]
         values = jnp.where(sampled, measured_ref[:, :, x].astype(jnp.float32), values)
@@ -318,7 +306,7 @@
         [
             pltpu.VMEM(measured.shape, measured.dtype),
             pltpu.VMEM(sample_mask.shape, sample_mask.dtype),
-            pltpu.VMEM((local_x, channels * local_y, local_y * local_z), jnp.float32),
+            pltpu.VMEM((local_x, channels * (local_y + 1), local_y * local_z), jnp.float32),
             pltpu.SemaphoreType.DMA((2,)),
         ],
     )(*[pltpu.with_memory_space_constraint(a, pltpu.HBM) for a in (measured, sample_mask)])
@@ -336,47 +324,50 @@
     padded_part = pltpu.VMEM((padded_rows, width // 2), jnp.bfloat16)
     padded = pltpu.VMEM((padded_rows, width), jnp.bfloat16)
     partial_shape = jax.ShapeDtypeStruct((2, KS, half_rows, width), jnp.float32)
-    near_shape = jax.ShapeDtypeStruct((2, NEAR, half_rows, width), jnp.float32)
-    scratch = [padded, padded, padded_part, padded_part]
+    scratch = [padded_part, padded_part]
+
+    def more(own_z, own_parity, half, table, before):
+        more_fn = functools.partial(more_kernel, local_z, own_z, own_parity)
+        return call(more_fn, "more", partial_shape, [in_vmem] * 3, scratch)(half, table, before)
+
     blocks = packed[None]
     for number, (axis, bit) in enumerate(steps):
         arrived = swap(blocks, axis, bit)
         if number == 0:
-            arrived, taps = after(arrived, taps)
+            flat_shape = jax.ShapeDtypeStruct((2, taps.shape[0] * STRIDE, 128), jnp.float32)
+            arrived, flat = after(arrived, call(flat_kernel, "flat", flat_shape, [in_vmem])(taps))
         elif number == 1:
-            flat_shape = jax.ShapeDtypeStruct((2, taps.shape[0] * coils, 128), jnp.float32)
             order_shape = jax.ShapeDtypeStruct((2 * half_rows, half_rows), jnp.bfloat16)
             order = call(write_orders, "order", order_shape, [])()
-            flat = call(flat_kernel, "flat", flat_shape, [in_vmem])(taps)
-            arrived, flat, order = after(arrived, flat, order)
-        elif number == 2:
             table_shape = jax.ShapeDtypeStruct((KS, KS, width, 2 * width), jnp.bfloat16)
             table = call(functools.partial(table_kernel, order_x), "table", table_shape, [in_vmem])(flat)
+            arrived, table, order = after(arrived, table, order)
+        elif number == 2:
             turned_shape = jax.ShapeDtypeStruct((2 * half_rows, width // 2), jnp.bfloat16)
             turn_fn = functools.partial(turn_kernel, half_x, sizes[1])
             turned = call(turn_fn, "turn", turned_shape, [in_vmem] * 2)(blocks, order)
-            near_fn = functools.partial(near_kernel, half_x, local_z)
-            partial = call(near_fn, "near", near_shape, [in_vmem] * 2, [padded_part] * 2)(turned, table)
-            arrived, table, turned, partial = after(arrived, table, turned, partial)
-            half_shape = jax.ShapeDtypeStruct((2 * half_rows, width), jnp.bfloat16)
-            join_fn = functools.partial(join_kernel, half_x, sizes[1])
-            blocks = call(join_fn, "join", half_shape, [in_vmem] * 3)(arrived, turned, order)
+            turned_far = swap(turned, SPACE[2], 1)
+            near_fn = functools.partial(near_kernel, local_z)
+            partial = call(near_fn, "near", partial_shape, [in_vmem] * 2, scratch)(turned, table)
+            turned_far, partial = after(turned_far, partial)
+            partial = more(False, True, turned_far, table, partial)
+            arrived, turned, turned_far, partial = after(arrived, turned, turned_far, partial)
+            blocks = call(turn_fn, "turn_other", turned_shape, [in_vmem] * 2)(arrived, order)
             continue
         elif number == 3:
-            rest_fn = functools.partial(rest_kernel, half_x, local_z)
-            partial = call(rest_fn, "rest", partial_shape, [in_vmem] * 3, scratch)(blocks, table, partial)
+            partial = more(True, False, blocks, table, partial)
             arrived, partial = after(arrived, partial)
             break
         blocks = jnp.concatenate([blocks, arrived], axis=0)
 
-    lined = pltpu.VMEM((local_x * channels * local_y, 128), jnp.float32)
+    lined = pltpu.VMEM((local_x * channels * (local_y + 1), 128), jnp.float32)
     return call(
         grid_kernel,
         "grid",
         jax.ShapeDtypeStruct(measured.shape, jnp.bfloat16),
-        [in_vmem] * 7,
-        [padded] * 6 + [lined],
-    )(blocks, arrived, measured, sample_mask, order, table, partial)
+        [in_vmem] * 9,
+        scratch + [pltpu.VMEM((2, half_rows, width), jnp.bfloat16)] + [padded] * 4 + [lined],
+    )(turned, blocks, turned_far, arrived, measured, sample_mask, order, table, partial)
 
 
 def partner(block, axis, bit):

time: 21 us -> 20.8 us (level)
  Pallas kernels: 10.8 us -> 10.5 us
  waiting for transfers between devices: 0.78 us -> 1.01 us
    pallas_call x1, Pallas kernels: 3.73 us -> 3.12 us  [gathered_body(): call(grid_kernel, 'grid', jax.ShapeDtypeStruct(measured.shape, jnp.bfloat...]
    pallas_call x4 -> x5, Pallas kernels: 4.45 us -> 4.71 us  [the longest x2 2.54 us: more(): call(more_fn, 'more', partial_shape, [in_vmem] * 3, scratch)]
    ppermute x4 -> x5, waiting for transfers between devices: 0.78 us -> 1.01 us  [swap(): return lax.ppermute(block, axis, [(i, i ^ bit) for i in range(count)])]
    ppermute x4 -> x5, starting transfers between devices: 8.05 us -> 7.89 us  [swap(): return lax.ppermute(block, axis, [(i, i ^ bit) for i in range(count)])]
  transfers between devices with their start and end apart: 4 -> 5, of which waited for: 2 -> 2; matrix products, arithmetic and copies ran while one was open for 5% -> 5% of each run, Pallas kernels for 28% -> 28%
where the time goes in v6:
time: 20.8 us; the launch traced here: 20.6 us
  Pallas kernels  10.5 us (50%)
  starting transfers between devices  7.89 us (38%)
  local copies, waits for them, and re-layouts  1.08 us (5%)
  waiting for transfers between devices  1.01 us (5%)
    ppermute x5, starting transfers between devices, swap(): return lax.ppermute(block, axis, [(i, i ^ bit) for i in range(count)])  7.89 us
    pallas_call x1, Pallas kernels, gathered_body(): call(grid_kernel, 'grid', jax.ShapeDtypeStruct(measured.shape, jnp.bfloat...  3.12 us
    pallas_call x2, Pallas kernels, more(): call(more_fn, 'more', partial_shape, [in_vmem] * 3, scratch)  2.54 us
    pallas_call x1, Pallas kernels, gathered_body(): call(functools.partial(table_kernel, order_x), 'table', table_shape, [in_...  1.34 us
    pallas_call x1, Pallas kernels, gathered_body(): call(near_fn, 'near', partial_shape, [in_vmem] * 2, scratch)(turned, table)  1.24 us
    reshape x1, local copies, waits for them, and re-layouts, gathered_body(): jnp.moveaxis(kernel, 0, 3).reshape(parts * KS ** 3, coils * 2 * coils)  1.05 us
    pallas_call x1, Pallas kernels, gathered_body(): call(pack_kernel, 'pack', jax.ShapeDtypeStruct((local_x * channels, local...  1.04 us
    ppermute x5, waiting for transfers between devices, swap(): return lax.ppermute(block, axis, [(i, i ^ bit) for i in range(count)])  1.01 us
  transfers between devices with their start and end apart: 5, of which 2 were waited for; matrix products, arithmetic and copies ran while one was open for 5% of the time, Pallas kernels for 28%

profile of v6, /device:TPU:0, one launch (start us, length us, event | category | flops | bytes accessed | tf_op | source)
XLA Modules:
  0.0 20.6 jit_solution(16424213614388006736)
XLA Ops:
  0.0 1.0 %pack.1 = bf16[64,128]{1,0:T(8,128)(2,1)S(1)} custom-call(bf16[2,16,2,8,16]{4,3,2,1,0:T(8,128)(2,1)} %measured_ref.1, s32[2,8,16]{2,1,0:T(8,128)} %mask_ref.1), custom_call_target="tpu_custom_call" | custom-call | bytes 4194304 | tf_op jit(solution)/shard_map/pack/pallas_call | solution.py:301
  1.1 4.1 %collective-permute-start = (bf16[1,64,128]{2,1,0:T(8,128)(2,1)S(1)}, bf16[1,64,128]{2,1,0:T(8,128)(2,1)S(1)}, u32[]{:S(2)}, u32[]{:S(2)}) collective-permute-start(bf16[1,64,128]{2,1,0:T(8,128)(2,1)S(1)} %bitcast.2), channel_id=1, source_target_pairs={{0,8},{4,12},{8,0},{12,4},{1,9},{5,13},{9,1},{13,5},{2,10},{6,14},... | collective-permute-start | bytes 49160 | tf_op jit(solution)/shard_map/ppermute | solution.py:275
  5.2 1.0 %reshape.3 = bf16[250,512]{1,0:T(8,128)(2,1)S(1)} reshape(bf16[5,5,5,2,512]{4,3,2,1,0:T(2,128)(2,1)} %bitcast.5) | data formatting | bytes 512000 | tf_op jit(solution)/shard_map/reshape | solution.py:317
  6.3 0.7 %flat.1 = f32[2,4352,128]{2,1,0:T(8,128)S(1)} custom-call(bf16[256,512]{1,0:T(8,128)(2,1)S(1)} %pad.4.taps_ref), custom_call_target="tpu_custom_call" | custom-call | bytes 4194304 | tf_op jit(solution)/shard_map/flat/pallas_call | solution.py:338
  7.0 0.0 collective-permute-done
  7.0 1.8 %collective-permute-start.1 = (bf16[2,64,128]{2,1,0:T(8,128)(2,1)S(1)}, bf16[2,64,128]{2,1,0:T(8,128)(2,1)S(1)}, u32[]{:S(2)}, u32[]{:S(2)}) collective-permute-start(bf16[2,64,128]{2,1,0:T(8,128)(2,1)S(1)} %pad_maximum_fusion.1), channel_id=1, source_target_pairs={{0,2},{2,0},{1,3},{3,1},{4,6},{6,4},{5,7},{7,5},{8,10},{10,8},{9,1... | collective-permute-start | bytes 98312 | tf_op jit(solution)/shard_map/ppermute | solution.py:275
  8.8 1.3 %table.1 = bf16[5,5,256,512]{3,2,1,0:T(8,128)(2,1)S(1)} custom-call(f32[2,4352,128]{2,1,0:T(8,128)S(1)} %flat.1), custom_call_target="tpu_custom_call" | custom-call | bytes 4194304 | tf_op jit(solution)/shard_map/table/pallas_call | solution.py:343
  10.2 0.8 %collective-permute-done.1 = bf16[2,64,128]{2,1,0:T(8,128)(2,1)S(1)} collective-permute-done((bf16[2,64,128]{2,1,0:T(8,128)(2,1)S(1)}, bf16[2,64,128]{2,1,0:T(8,128)(2,1)S(1)}, u32[]{:S(2)}, u32[]{:S(2)}) %collective-permute-start.1) | collective-permute-done | bytes 32800 | tf_op jit(solution)/shard_map/ppermute | solution.py:275
  11.0 0.2 %turn.1.half.near_own = bf16[512,128]{1,0:T(8,128)(2,1)S(1)} custom-call(bf16[4,64,128]{2,1,0:T(8,128)(2,1)S(1)} %pad_maximum_fusion.blocks_ref, bf16[512,256]{1,0:T(8,128)(2,1)S(1)} %order.1), custom_call_target="tpu_custom_call" | custom-call | bytes 4194304 | tf_op jit(solution)/shard_map/turn/pallas_call | solution.py:348
  11.2 0.1 collective-permute-start.3
  11.3 1.8 %collective-permute-start.2 = (bf16[4,64,128]{2,1,0:T(8,128)(2,1)S(1)}, bf16[4,64,128]{2,1,0:T(8,128)(2,1)S(1)}, u32[]{:S(2)}, u32[]{:S(2)}) collective-permute-start(bf16[4,64,128]{2,1,0:T(8,128)(2,1)S(1)} %pad_maximum_fusion.blocks_ref), channel_id=1, source_target_pairs={{0,4},{4,0},{8,12},{12,8},{1,5},{5,1},{9,13},{13,9},{2,6},{6,2},{1... | collective-permute-start | bytes 196616 | tf_op jit(solution)/shard_map/ppermute | solution.py:275
  13.1 1.2 %near.1.before = f32[2,5,256,256]{3,2,1,0:T(8,128)S(1)} custom-call(bf16[512,128]{1,0:T(8,128)(2,1)S(1)} %turn.1.half.near_own, bf16[5,5,256,512]{3,2,1,0:T(8,128)(2,1)S(1)} %table.1), custom_call_target="tpu_custom_call" | custom-call | bytes 4194304 | tf_op jit(solution)/shard_map/near/pallas_call | solution.py:351
  14.4 0.0 collective-permute-done.3.half.far_own
  14.4 1.3 %more.2.before = f32[2,5,256,256]{3,2,1,0:T(8,128)S(1)} custom-call(bf16[512,128]{1,0:T(8,128)(2,1)S(1)} %collective-permute-done.3.half.far_own, bf16[5,5,256,512]{3,2,1,0:T(8,128)(2,1)S(1)} %table.1, f32[2,5,256,256]{3,2,1,0:T(8,128)S(1)} %near.1.before), custom_call_target="tpu_custom_call" | custom-call | bytes 4194304 | tf_op jit(solution)/shard_map/more/pallas_call | solution.py:331
  15.7 0.2 collective-permute-done.2.blocks_ref
  15.8 0.2 %turn_other.1.half.near_other = bf16[512,128]{1,0:T(8,128)(2,1)S(1)} custom-call(bf16[4,64,128]{2,1,0:T(8,128)(2,1)S(1)} %collective-permute-done.2.blocks_ref, bf16[512,256]{1,0:T(8,128)(2,1)S(1)} %order.1), custom_call_target="tpu_custom_call" | custom-call | bytes 4194304 | tf_op jit(solution)/shard_map/turn_other/pallas_call | solution.py:355
  16.1 0.0 copy-start
  16.1 0.0 copy-start.1
  16.1 0.1 collective-permute-start.4
  16.2 1.3 %more.3.partial = f32[2,5,256,256]{3,2,1,0:T(8,128)S(1)} custom-call(bf16[512,128]{1,0:T(8,128)(2,1)S(1)} %turn_other.1.half.near_other, bf16[5,5,256,512]{3,2,1,0:T(8,128)(2,1)S(1)} %table.1, f32[2,5,256,256]{3,2,1,0:T(8,128)S(1)} %more.2.before), custom_call_target="tpu_custom_call" | custom-call | bytes 4194304 | tf_op jit(solution)/shard_map/more/pallas_call | solution.py:331
  17.5 0.0 collective-permute-done.4.far_other
  17.5 0.0 copy-done
  17.5 0.0 copy-done.1
  17.5 3.1 %grid.1 = bf16[2,16,2,8,16]{4,3,2,1,0:T(8,128)(2,1)} custom-call(bf16[512,128]{1,0:T(8,128)(2,1)S(1)} %turn.1.half.near_own, bf16[512,128]{1,0:T(8,128)(2,1)S(1)} %turn_other.1.half.near_other, bf16[512,128]{1,0:T(8,128)(2,1)S(1)} %collective-permute-done.3.half.far_own, bf16[512,128]{1,0:T(8,128)(2,1)S(1)} %collective-permute-done.4.far_other, ...), custom_call_target="tpu_custom_call" | custom-call | bytes 4194304 | tf_op jit(solution)/shard_map/grid/pallas_call | solution.py:364
  (4 shorter events, 0.1 us)
Async XLA Ops:
  1.1 5.9 %collective-permute-start = (bf16[1,64,128]{2,1,0:T(8,128)(2,1)S(1)}, bf16[1,64,128]{2,1,0:T(8,128)(2,1)S(1)}, u32[]{:S(2)}, u32[]{:S(2)}) collective-permute-start(bf16[1,64,128]{2,1,0:T(8,128)(2,1)S(1)} %bitcast.2), channel_id=1, source_target_pairs={{0,8},{4,12},{8,0},{12,4},{1,9},{5,13},{9,1},{13,5},{2,10},{6,14},... | collective-permute-start | bytes 49160 | tf_op jit(solution)/shard_map/ppermute | solution.py:275
  7.0 4.0 %collective-permute-start.1 = (bf16[2,64,128]{2,1,0:T(8,128)(2,1)S(1)}, bf16[2,64,128]{2,1,0:T(8,128)(2,1)S(1)}, u32[]{:S(2)}, u32[]{:S(2)}) collective-permute-start(bf16[2,64,128]{2,1,0:T(8,128)(2,1)S(1)} %pad_maximum_fusion.1), channel_id=1, source_target_pairs={{0,2},{2,0},{1,3},{3,1},{4,6},{6,4},{5,7},{7,5},{8,10},{10,8},{9,1... | collective-permute-start | bytes 98312 | tf_op jit(solution)/shard_map/ppermute | solution.py:275
  11.2 3.2 %collective-permute-start.3 = (bf16[512,128]{1,0:T(8,128)(2,1)S(1)}, bf16[512,128]{1,0:T(8,128)(2,1)S(1)}, u32[]{:S(2)}, u32[]{:S(2)}) collective-permute-start(bf16[512,128]{1,0:T(8,128)(2,1)S(1)} %turn.1.half.near_own), channel_id=1, source_target_pairs={{0,1},{1,0},{2,3},{3,2},{4,5},{5,4},{6,7},{7,6},{8,9},{9,8},{10,11... | collective-permute-start | bytes 393224 | tf_op jit(solution)/shard_map/ppermute | solution.py:275
  11.3 4.5 %collective-permute-start.2 = (bf16[4,64,128]{2,1,0:T(8,128)(2,1)S(1)}, bf16[4,64,128]{2,1,0:T(8,128)(2,1)S(1)}, u32[]{:S(2)}, u32[]{:S(2)}) collective-permute-start(bf16[4,64,128]{2,1,0:T(8,128)(2,1)S(1)} %pad_maximum_fusion.blocks_ref), channel_id=1, source_target_pairs={{0,4},{4,0},{8,12},{12,8},{1,5},{5,1},{9,13},{13,9},{2,6},{6,2},{1... | collective-permute-start | bytes 196616 | tf_op jit(solution)/shard_map/ppermute | solution.py:275
  16.1 1.4 %copy-start = (bf16[2,16,2,8,16]{4,3,2,1,0:T(8,128)(2,1)S(1)}, bf16[2,16,2,8,16]{4,3,2,1,0:T(8,128)(2,1)}, u32[]{:S(2)}) copy-start(bf16[2,16,2,8,16]{4,3,2,1,0:T(8,128)(2,1)} %measured_ref.1) | copy-start | bytes 49156
  16.1 1.4 %copy-start.1 = (s32[2,8,16]{2,1,0:T(8,128)S(1)}, s32[2,8,16]{2,1,0:T(8,128)}, u32[]{:S(2)}) copy-start(s32[2,8,16]{2,1,0:T(8,128)} %mask_ref.1) | copy-start | bytes 3076
  16.1 1.4 %collective-permute-start.4 = (bf16[512,128]{1,0:T(8,128)(2,1)S(1)}, bf16[512,128]{1,0:T(8,128)(2,1)S(1)}, u32[]{:S(2)}, u32[]{:S(2)}) collective-permute-start(bf16[512,128]{1,0:T(8,128)(2,1)S(1)} %turn_other.1.half.near_other), channel_id=1, source_target_pairs={{0,1},{1,0},{2,3},{3,2},{4,5},{5,4},{6,7},{7,6},{8,9},{9,8},{10,11... | collective-permute-start | bytes 393224 | tf_op jit(solution)/shard_map/ppermute | solution.py:275

commit v7 on v6

--- a/solution.py
+++ b/solution.py
@@ -6,6 +6,7 @@
 from jax.experimental import pallas as pl
 from jax.experimental.pallas import tpu as pltpu
 from jax.sharding import PartitionSpec as P
+
 
 COILS = 16
 KS = 5
@@ -151,10 +152,10 @@
         ref[edge : edge + rows] = jnp.where(values < LIMIT, values, jnp.zeros_like(values))
 
 
-def pair_taps(ref, rows, local_z, weights):
+def pair_taps(ref, rows, local_z, weights, count):
     total = None
-    for dy in range(0, KS, 2):
-        both = range(dy, min(dy + 2, KS))
+    for dy in range(0, count, 2):
+        both = range(dy, min(dy + 2, count))
         values = jnp.concatenate([ref[d * local_z : d * local_z + rows] for d in both], axis=1)
         term = dot_nt(values, jnp.concatenate([weights(d) for d in both], axis=1))
         total = term if total is None else total + term
@@ -166,7 +167,7 @@
     return pl.multiple_of((parity if own_parity else 1 - parity) * width, width)
 
 
-def give(half, local_z, own_z, own_parity, table, points, mirrored):
+def give(half, local_z, own_z, own_parity, table, points, mirrored, count=KS):
     rows, width = half.shape[0] // 2, half.shape[1]
     load_half(half, local_z, points, mirrored)
     first = own_lanes(width, own_parity)
@@ -175,7 +176,7 @@
         number = target if own_z else 1 - target
         lanes = pl.ds(pl.multiple_of(number * table.shape[3] // 2 + first, width), width)
         ref = mirrored if number else points
-        return pair_taps(ref, rows, local_z, lambda dy: table[dy, dz, :, lanes])
+        return pair_taps(ref, rows, local_z, lambda dy: table[dy, dz, :, lanes], count)
 
     return given
 
@@ -188,7 +189,7 @@
 
 
 def more_kernel(local_z, own_z, own_parity, half, table, before, partial, points, mirrored):
-    given = give(half, local_z, own_z, own_parity, table, points, mirrored)
+    given = give(half, local_z, own_z, own_parity, table, points, mirrored, KS if own_z else KS - 1)
     for target in range(2):
         for dz in range(KS):
             partial[target, dz] = before[target, dz] + given(target, dz)
@@ -205,7 +206,7 @@
 
 def grid_kernel(
     near_own, near_other, far_own, far_other, measured_ref, mask_ref, order, table, partial,
-    out_ref, points, mirrored, coded_ref, near, far, near_mirrored, far_mirrored, lined,
+    out_ref, points, mirrored, points_own, mirrored_own, coded_ref, near, far, near_mirrored, far_mirrored, lined,
 ):
     parts, coils, local_x, local_y, local_z = out_ref.shape
     channels = parts * coils
@@ -214,18 +215,31 @@
     at_x = at_x % 2 * (lax.axis_size(SPACE[0]) // 2) + at_x // 2
     own_first = (1 - lax.axis_index(SPACE[2])).astype(jnp.float32)
     edge = REACH * local_z
-    given = give(far_other, local_z, False, False, table, points, mirrored)
+    given = give(far_other, local_z, False, False, table, points, mirrored, KS - 1)
+    load_half(far_own, local_z, points_own, mirrored_own)
+    last = slice((KS - 1) * local_z, (KS - 1) * local_z + rows)
+    pairs = ((mirrored_own, mirrored), (points_own, points))
+    last_values = [jnp.concatenate([ref[last] for ref in pair], axis=1) for pair in pairs]
+
+    def last_given(target, dz):
+        part = width // 2
+        lanes = [(1 - target) * width + own_lanes(part, own_parity) for own_parity in (True, False)]
+        weights = [table[KS - 1, dz, :, pl.ds(pl.multiple_of(at, part), part)] for at in lanes]
+        return dot_nt(last_values[target], jnp.concatenate(weights, axis=1))
+
     for number, halves in enumerate(((near_own, near_other), (far_own, far_other))):
         for half, own_parity in zip(halves, (True, False)):
             coded_ref[number, :, pl.ds(own_lanes(width // 2, own_parity), width // 2)] = half[:rows]
     for ref in (near, far, near_mirrored, far_mirrored):
         ref[:edge] = jnp.zeros((edge, width), jnp.bfloat16)
         ref[edge + rows :] = jnp.zeros((edge, width), jnp.bfloat16)
-    for iteration in range(ITERS - 1):
+    for _ in range(ITERS - 1):
         totals = [None, None]
         for dz in sorted(range(KS), key=lambda dz: dz == REACH):
             shift = dz - REACH
-            own, other = (partial[target, dz] + given(target, dz) for target in range(2))
+            own, other = (
+                partial[target, dz] + given(target, dz) + last_given(target, dz) for target in range(2)
+            )
             if shift != 0:
                 own, other = (
                     shift_z(own, other, shift, local_z, 0, own_first),
@@ -278,15 +292,14 @@
 def gathered_body(measured, sample_mask, kernel):
     parts, coils, local_x, local_y, local_z = measured.shape
     sizes = tuple(lax.axis_size(axis) for axis in SPACE)
-    devices = sizes[0] * sizes[1] * sizes[2]
     channels = parts * coils
-    size_x, size_y, size_z = sizes[0] * local_x, sizes[1] * local_y, sizes[2] * local_z
+    size_x, size_y = sizes[0] * local_x, sizes[1] * local_y
     width = size_x * channels
     half_rows = size_y * local_z
     in_vmem = pl.BlockSpec(memory_space=pltpu.VMEM)
     in_hbm = pl.BlockSpec(memory_space=pltpu.HBM)
 
-    def call(kernel_fn, name, out_shape, in_specs, scratch=(), outs=1, cost=2 ** 22):
+    def call(kernel_fn, out_shape, in_specs, scratch=(), outs=1, cost=2 ** 22):
         return pl.pallas_call(
             kernel_fn,
             out_shape=out_shape,
@@ -295,12 +308,10 @@
             scratch_shapes=list(scratch),
             compiler_params=pltpu.CompilerParams(vmem_limit_bytes=VMEM_LIMIT),
             cost_estimate=pl.CostEstimate(flops=0, bytes_accessed=cost, transcendentals=0),
-            name=name,
         )
 
     packed = call(
         pack_kernel,
-        "pack",
         jax.ShapeDtypeStruct((local_x * channels, local_y * local_z), jnp.bfloat16),
         [in_hbm, in_hbm],
         [
@@ -328,31 +339,31 @@
 
     def more(own_z, own_parity, half, table, before):
         more_fn = functools.partial(more_kernel, local_z, own_z, own_parity)
-        return call(more_fn, "more", partial_shape, [in_vmem] * 3, scratch)(half, table, before)
+        return call(more_fn, partial_shape, [in_vmem] * 3, scratch)(half, table, before)
 
     blocks = packed[None]
     for number, (axis, bit) in enumerate(steps):
         arrived = swap(blocks, axis, bit)
         if number == 0:
             flat_shape = jax.ShapeDtypeStruct((2, taps.shape[0] * STRIDE, 128), jnp.float32)
-            arrived, flat = after(arrived, call(flat_kernel, "flat", flat_shape, [in_vmem])(taps))
+            arrived, flat = after(arrived, call(flat_kernel, flat_shape, [in_vmem])(taps))
         elif number == 1:
             order_shape = jax.ShapeDtypeStruct((2 * half_rows, half_rows), jnp.bfloat16)
-            order = call(write_orders, "order", order_shape, [])()
+            order = call(write_orders, order_shape, [])()
             table_shape = jax.ShapeDtypeStruct((KS, KS, width, 2 * width), jnp.bfloat16)
-            table = call(functools.partial(table_kernel, order_x), "table", table_shape, [in_vmem])(flat)
+            table = call(functools.partial(table_kernel, order_x), table_shape, [in_vmem])(flat)
             arrived, table, order = after(arrived, table, order)
         elif number == 2:
             turned_shape = jax.ShapeDtypeStruct((2 * half_rows, width // 2), jnp.bfloat16)
             turn_fn = functools.partial(turn_kernel, half_x, sizes[1])
-            turned = call(turn_fn, "turn", turned_shape, [in_vmem] * 2)(blocks, order)
+            turned = call(turn_fn, turned_shape, [in_vmem] * 2)(blocks, order)
             turned_far = swap(turned, SPACE[2], 1)
             near_fn = functools.partial(near_kernel, local_z)
-            partial = call(near_fn, "near", partial_shape, [in_vmem] * 2, scratch)(turned, table)
+            partial = call(near_fn, partial_shape, [in_vmem] * 2, scratch)(turned, table)
             turned_far, partial = after(turned_far, partial)
             partial = more(False, True, turned_far, table, partial)
             arrived, turned, turned_far, partial = after(arrived, turned, turned_far, partial)
-            blocks = call(turn_fn, "turn_other", turned_shape, [in_vmem] * 2)(arrived, order)
+            blocks = call(turn_fn, turned_shape, [in_vmem] * 2)(arrived, order)
             continue
         elif number == 3:
             partial = more(True, False, blocks, table, partial)
@@ -363,10 +374,9 @@
     lined = pltpu.VMEM((local_x * channels * (local_y + 1), 128), jnp.float32)
     return call(
         grid_kernel,
-        "grid",
         jax.ShapeDtypeStruct(measured.shape, jnp.bfloat16),
         [in_vmem] * 9,
-        scratch + [pltpu.VMEM((2, half_rows, width), jnp.bfloat16)] + [padded] * 4 + [lined],
+        scratch * 2 + [pltpu.VMEM((2, half_rows, width), jnp.bfloat16)] + [padded] * 4 + [lined],
     )(turned, blocks, turned_far, arrived, measured, sample_mask, order, table, partial)
 
 
@@ -450,7 +460,7 @@
     sampled = (sample_mask == 1)[None, None]
     current = jnp.where(sampled, measured, jnp.zeros_like(measured))
     tap_table = tap_matrix(kernel)
-    for iteration in range(ITERS):
+    for _ in range(ITERS):
         joined = jnp.concatenate([current, conjugate(mirror_state(current))], axis=1)
         padded = padded_2(joined, (("gx", 2), ("gy", 3), ("gz", 4)), reach)
         convolved = convolve(padded, tap_table)

time: 20.8 us -> 20.8 us (level)
  waiting for transfers between devices: 1.01 us -> 1.36 us
  Pallas kernels: 10.5 us -> 10.2 us
    ppermute x5, waiting for transfers between devices: 1.01 us -> 1.36 us  [swap(): return lax.ppermute(block, axis, [(i, i ^ bit) for i in range(count)])]
    pallas_call x10, Pallas kernels: 10.5 us -> 10.2 us  [the longest x1 3.16 us: gathered_body(): call(grid_kernel, jax.ShapeDtypeStruct(measured.shape, jnp.bfloat16), [in...]
  transfers between devices with their start and end apart: 5 -> 5, of which waited for: 2 -> 2; matrix products, arithmetic and copies ran while one was open for 5% -> 5% of each run, Pallas kernels for 28% -> 27%
where the time goes in v7:
time: 20.8 us; the launch traced here: 20.7 us
  Pallas kernels  10.2 us (49%)
  starting transfers between devices  7.89 us (38%)
  waiting for transfers between devices  1.36 us (7%)
  local copies, waits for them, and re-layouts  1.08 us (5%)
    ppermute x5, starting transfers between devices, swap(): return lax.ppermute(block, axis, [(i, i ^ bit) for i in range(count)])  7.89 us
    pallas_call x1, Pallas kernels, gathered_body(): call(grid_kernel, jax.ShapeDtypeStruct(measured.shape, jnp.bfloat16), [in...  3.16 us
    pallas_call x2, Pallas kernels, more(): call(more_fn, partial_shape, [in_vmem] * 3, scratch)(half, table, before)  2.19 us
    ppermute x5, waiting for transfers between devices, swap(): return lax.ppermute(block, axis, [(i, i ^ bit) for i in range(count)])  1.36 us
    pallas_call x1, Pallas kernels, gathered_body(): call(functools.partial(table_kernel, order_x), table_shape, [in_vmem])(flat)  1.34 us
    pallas_call x1, Pallas kernels, gathered_body(): call(near_fn, partial_shape, [in_vmem] * 2, scratch)(turned, table)  1.24 us
    reshape x1, local copies, waits for them, and re-layouts, gathered_body(): jnp.moveaxis(kernel, 0, 3).reshape(parts * KS ** 3, coils * 2 * coils)  1.05 us
    pallas_call x1, Pallas kernels, gathered_body(): call(pack_kernel, jax.ShapeDtypeStruct((local_x * channels, local_y * loc...  1.04 us
  transfers between devices with their start and end apart: 5, of which 2 were waited for; matrix products, arithmetic and copies ran while one was open for 5% of the time, Pallas kernels for 27%

profile of v7, /device:TPU:0, one launch (start us, length us, event | category | flops | bytes accessed | tf_op | source)
XLA Modules:
  0.0 20.7 jit_solution(3474182168450212997)
XLA Ops:
  0.0 1.0 %shard_map.37 = bf16[64,128]{1,0:T(8,128)(2,1)S(1)} custom-call(bf16[2,16,2,8,16]{4,3,2,1,0:T(8,128)(2,1)} %measured_ref.1, s32[2,8,16]{2,1,0:T(8,128)} %mask_ref.1), custom_call_target="tpu_custom_call" | custom-call | bytes 4194304 | tf_op jit(solution)/shard_map/pallas_call | solution.py:313
  1.1 4.1 %collective-permute-start = (bf16[1,64,128]{2,1,0:T(8,128)(2,1)S(1)}, bf16[1,64,128]{2,1,0:T(8,128)(2,1)S(1)}, u32[]{:S(2)}, u32[]{:S(2)}) collective-permute-start(bf16[1,64,128]{2,1,0:T(8,128)(2,1)S(1)} %bitcast.2), channel_id=1, source_target_pairs={{0,8},{4,12},{8,0},{12,4},{1,9},{5,13},{9,1},{13,5},{2,10},{6,14},... | collective-permute-start | bytes 49160 | tf_op jit(solution)/shard_map/ppermute | solution.py:289
  5.2 1.0 %reshape.3 = bf16[250,512]{1,0:T(8,128)(2,1)S(1)} reshape(bf16[5,5,5,2,512]{4,3,2,1,0:T(2,128)(2,1)} %bitcast.5) | data formatting | bytes 512000 | tf_op jit(solution)/shard_map/reshape | solution.py:328
  6.3 0.7 %shard_map.38.flat = f32[2,4352,128]{2,1,0:T(8,128)S(1)} custom-call(bf16[256,512]{1,0:T(8,128)(2,1)S(1)} %pad.4.taps_ref), custom_call_target="tpu_custom_call" | custom-call | bytes 4194304 | tf_op jit(solution)/shard_map/pallas_call | solution.py:349
  7.0 0.0 collective-permute-done
  7.0 1.8 %collective-permute-start.1 = (bf16[2,64,128]{2,1,0:T(8,128)(2,1)S(1)}, bf16[2,64,128]{2,1,0:T(8,128)(2,1)S(1)}, u32[]{:S(2)}, u32[]{:S(2)}) collective-permute-start(bf16[2,64,128]{2,1,0:T(8,128)(2,1)S(1)} %pad_maximum_fusion.1), channel_id=1, source_target_pairs={{0,2},{2,0},{1,3},{3,1},{4,6},{6,4},{5,7},{7,5},{8,10},{10,8},{9,1... | collective-permute-start | bytes 98312 | tf_op jit(solution)/shard_map/ppermute | solution.py:289
  8.8 1.3 %shard_map.39.table = bf16[5,5,256,512]{3,2,1,0:T(8,128)(2,1)S(1)} custom-call(f32[2,4352,128]{2,1,0:T(8,128)S(1)} %shard_map.38.flat), custom_call_target="tpu_custom_call" | custom-call | bytes 4194304 | tf_op jit(solution)/shard_map/pallas_call | solution.py:354
  10.2 0.8 %collective-permute-done.1 = bf16[2,64,128]{2,1,0:T(8,128)(2,1)S(1)} collective-permute-done((bf16[2,64,128]{2,1,0:T(8,128)(2,1)S(1)}, bf16[2,64,128]{2,1,0:T(8,128)(2,1)S(1)}, u32[]{:S(2)}, u32[]{:S(2)}) %collective-permute-start.1) | collective-permute-done | bytes 32800 | tf_op jit(solution)/shard_map/ppermute | solution.py:289
  11.0 0.2 %shard_map.41.half.near_own = bf16[512,128]{1,0:T(8,128)(2,1)S(1)} custom-call(bf16[4,64,128]{2,1,0:T(8,128)(2,1)S(1)} %pad_maximum_fusion.blocks_ref, bf16[512,256]{1,0:T(8,128)(2,1)S(1)} %shard_map.40.order), custom_call_target="tpu_custom_call" | custom-call | bytes 4194304 | tf_op jit(solution)/shard_map/pallas_call | solution.py:359
  11.2 0.1 collective-permute-start.3
  11.3 1.8 %collective-permute-start.2 = (bf16[4,64,128]{2,1,0:T(8,128)(2,1)S(1)}, bf16[4,64,128]{2,1,0:T(8,128)(2,1)S(1)}, u32[]{:S(2)}, u32[]{:S(2)}) collective-permute-start(bf16[4,64,128]{2,1,0:T(8,128)(2,1)S(1)} %pad_maximum_fusion.blocks_ref), channel_id=1, source_target_pairs={{0,4},{4,0},{8,12},{12,8},{1,5},{5,1},{9,13},{13,9},{2,6},{6,2},{1... | collective-permute-start | bytes 196616 | tf_op jit(solution)/shard_map/ppermute | solution.py:289
  13.1 1.2 %shard_map.42.before = f32[2,5,256,256]{3,2,1,0:T(8,128)S(1)} custom-call(bf16[512,128]{1,0:T(8,128)(2,1)S(1)} %shard_map.41.half.near_own, bf16[5,5,256,512]{3,2,1,0:T(8,128)(2,1)S(1)} %shard_map.39.table), custom_call_target="tpu_custom_call" | custom-call | bytes 4194304 | tf_op jit(solution)/shard_map/pallas_call | solution.py:362
  14.4 0.0 collective-permute-done.3.half.far_own
  14.4 0.9 %shard_map.43.before = f32[2,5,256,256]{3,2,1,0:T(8,128)S(1)} custom-call(bf16[512,128]{1,0:T(8,128)(2,1)S(1)} %collective-permute-done.3.half.far_own, bf16[5,5,256,512]{3,2,1,0:T(8,128)(2,1)S(1)} %shard_map.39.table, f32[2,5,256,256]{3,2,1,0:T(8,128)S(1)} %shard_map.42.before), custom_call_target="tpu_custom_call" | custom-call | bytes 4194304 | tf_op jit(solution)/shard_map/pallas_call | solution.py:342
  15.3 0.5 %collective-permute-done.2.blocks_ref = bf16[4,64,128]{2,1,0:T(8,128)(2,1)S(1)} collective-permute-done((bf16[4,64,128]{2,1,0:T(8,128)(2,1)S(1)}, bf16[4,64,128]{2,1,0:T(8,128)(2,1)S(1)}, u32[]{:S(2)}, u32[]{:S(2)}) %collective-permute-start.2) | collective-permute-done | bytes 65568 | tf_op jit(solution)/shard_map/ppermute | solution.py:289
  15.8 0.2 %shard_map.44.half.near_other = bf16[512,128]{1,0:T(8,128)(2,1)S(1)} custom-call(bf16[4,64,128]{2,1,0:T(8,128)(2,1)S(1)} %collective-permute-done.2.blocks_ref, bf16[512,256]{1,0:T(8,128)(2,1)S(1)} %shard_map.40.order), custom_call_target="tpu_custom_call" | custom-call | bytes 4194304 | tf_op jit(solution)/shard_map/pallas_call | solution.py:366
  16.1 0.0 copy-start
  16.1 0.0 copy-start.1
  16.1 0.1 collective-permute-start.4
  16.2 1.3 %shard_map.45.partial = f32[2,5,256,256]{3,2,1,0:T(8,128)S(1)} custom-call(bf16[512,128]{1,0:T(8,128)(2,1)S(1)} %shard_map.44.half.near_other, bf16[5,5,256,512]{3,2,1,0:T(8,128)(2,1)S(1)} %shard_map.39.table, f32[2,5,256,256]{3,2,1,0:T(8,128)S(1)} %shard_map.43.before), custom_call_target="tpu_custom_call" | custom-call | bytes 4194304 | tf_op jit(solution)/shard_map/pallas_call | solution.py:342
  17.5 0.0 collective-permute-done.4.far_other
  17.5 0.0 copy-done
  17.5 0.0 copy-done.1
  17.5 3.2 %shard_map.46 = bf16[2,16,2,8,16]{4,3,2,1,0:T(8,128)(2,1)} custom-call(bf16[512,128]{1,0:T(8,128)(2,1)S(1)} %shard_map.41.half.near_own, bf16[512,128]{1,0:T(8,128)(2,1)S(1)} %shard_map.44.half.near_other, bf16[512,128]{1,0:T(8,128)(2,1)S(1)} %collective-permute-done.3.half.far_own, bf16[512,128]{1,0:T(8,128)(2,1)S(1)} %collective-permute-done.4.far_other, ...), custom_call_target="tpu_custom_call" | custom-call | bytes 4194304 | tf_op jit(solution)/shard_map/pallas_call | solution.py:375
  (4 shorter events, 0.1 us)
Async XLA Ops:
  1.1 5.9 %collective-permute-start = (bf16[1,64,128]{2,1,0:T(8,128)(2,1)S(1)}, bf16[1,64,128]{2,1,0:T(8,128)(2,1)S(1)}, u32[]{:S(2)}, u32[]{:S(2)}) collective-permute-start(bf16[1,64,128]{2,1,0:T(8,128)(2,1)S(1)} %bitcast.2), channel_id=1, source_target_pairs={{0,8},{4,12},{8,0},{12,4},{1,9},{5,13},{9,1},{13,5},{2,10},{6,14},... | collective-permute-start | bytes 49160 | tf_op jit(solution)/shard_map/ppermute | solution.py:289
  7.0 4.0 %collective-permute-start.1 = (bf16[2,64,128]{2,1,0:T(8,128)(2,1)S(1)}, bf16[2,64,128]{2,1,0:T(8,128)(2,1)S(1)}, u32[]{:S(2)}, u32[]{:S(2)}) collective-permute-start(bf16[2,64,128]{2,1,0:T(8,128)(2,1)S(1)} %pad_maximum_fusion.1), channel_id=1, source_target_pairs={{0,2},{2,0},{1,3},{3,1},{4,6},{6,4},{5,7},{7,5},{8,10},{10,8},{9,1... | collective-permute-start | bytes 98312 | tf_op jit(solution)/shard_map/ppermute | solution.py:289
  11.2 3.2 %collective-permute-start.3 = (bf16[512,128]{1,0:T(8,128)(2,1)S(1)}, bf16[512,128]{1,0:T(8,128)(2,1)S(1)}, u32[]{:S(2)}, u32[]{:S(2)}) collective-permute-start(bf16[512,128]{1,0:T(8,128)(2,1)S(1)} %shard_map.41.half.near_own), channel_id=1, source_target_pairs={{0,1},{1,0},{2,3},{3,2},{4,5},{5,4},{6,7},{7,6},{8,9},{9,8},{10,11... | collective-permute-start | bytes 393224 | tf_op jit(solution)/shard_map/ppermute | solution.py:289
  11.3 4.5 %collective-permute-start.2 = (bf16[4,64,128]{2,1,0:T(8,128)(2,1)S(1)}, bf16[4,64,128]{2,1,0:T(8,128)(2,1)S(1)}, u32[]{:S(2)}, u32[]{:S(2)}) collective-permute-start(bf16[4,64,128]{2,1,0:T(8,128)(2,1)S(1)} %pad_maximum_fusion.blocks_ref), channel_id=1, source_target_pairs={{0,4},{4,0},{8,12},{12,8},{1,5},{5,1},{9,13},{13,9},{2,6},{6,2},{1... | collective-permute-start | bytes 196616 | tf_op jit(solution)/shard_map/ppermute | solution.py:289
  16.1 1.4 %copy-start = (bf16[2,16,2,8,16]{4,3,2,1,0:T(8,128)(2,1)S(1)}, bf16[2,16,2,8,16]{4,3,2,1,0:T(8,128)(2,1)}, u32[]{:S(2)}) copy-start(bf16[2,16,2,8,16]{4,3,2,1,0:T(8,128)(2,1)} %measured_ref.1) | copy-start | bytes 49156
  16.1 1.4 %copy-start.1 = (s32[2,8,16]{2,1,0:T(8,128)S(1)}, s32[2,8,16]{2,1,0:T(8,128)}, u32[]{:S(2)}) copy-start(s32[2,8,16]{2,1,0:T(8,128)} %mask_ref.1) | copy-start | bytes 3076
  16.1 1.4 %collective-permute-start.4 = (bf16[512,128]{1,0:T(8,128)(2,1)S(1)}, bf16[512,128]{1,0:T(8,128)(2,1)S(1)}, u32[]{:S(2)}, u32[]{:S(2)}) collective-permute-start(bf16[512,128]{1,0:T(8,128)(2,1)S(1)} %shard_map.44.half.near_other), channel_id=1, source_target_pairs={{0,1},{1,0},{2,3},{3,2},{4,5},{5,4},{6,7},{7,6},{8,9},{9,8},{10,11... | collective-permute-start | bytes 393224 | tf_op jit(solution)/shard_map/ppermute | solution.py:289

commit v8 on v7

--- a/solution.py
+++ b/solution.py
@@ -233,7 +233,7 @@
     for ref in (near, far, near_mirrored, far_mirrored):
         ref[:edge] = jnp.zeros((edge, width), jnp.bfloat16)
         ref[edge + rows :] = jnp.zeros((edge, width), jnp.bfloat16)
-    for _ in range(ITERS - 1):
+    for iteration in range(ITERS - 1):
         totals = [None, None]
         for dz in sorted(range(KS), key=lambda dz: dz == REACH):
             shift = dz - REACH
@@ -292,14 +292,15 @@
 def gathered_body(measured, sample_mask, kernel):
     parts, coils, local_x, local_y, local_z = measured.shape
     sizes = tuple(lax.axis_size(axis) for axis in SPACE)
+    devices = sizes[0] * sizes[1] * sizes[2]
     channels = parts * coils
-    size_x, size_y = sizes[0] * local_x, sizes[1] * local_y
+    size_x, size_y, size_z = sizes[0] * local_x, sizes[1] * local_y, sizes[2] * local_z
     width = size_x * channels
     half_rows = size_y * local_z
     in_vmem = pl.BlockSpec(memory_space=pltpu.VMEM)
     in_hbm = pl.BlockSpec(memory_space=pltpu.HBM)
 
-    def call(kernel_fn, out_shape, in_specs, scratch=(), outs=1, cost=2 ** 22):
+    def call(kernel_fn, name, out_shape, in_specs, scratch=(), outs=1, cost=2 ** 22):
         return pl.pallas_call(
             kernel_fn,
             out_shape=out_shape,
@@ -308,10 +309,12 @@
             scratch_shapes=list(scratch),
             compiler_params=pltpu.CompilerParams(vmem_limit_bytes=VMEM_LIMIT),
             cost_estimate=pl.CostEstimate(flops=0, bytes_accessed=cost, transcendentals=0),
+            name=name,
         )
 
     packed = call(
         pack_kernel,
+        "pack",
         jax.ShapeDtypeStruct((local_x * channels, local_y * local_z), jnp.bfloat16),
         [in_hbm, in_hbm],
         [
@@ -339,31 +342,34 @@
 
     def more(own_z, own_parity, half, table, before):
         more_fn = functools.partial(more_kernel, local_z, own_z, own_parity)
-        return call(more_fn, partial_shape, [in_vmem] * 3, scratch)(half, table, before)
+        return call(more_fn, "more", partial_shape, [in_vmem] * 3, scratch)(half, table, before)
 
     blocks = packed[None]
     for number, (axis, bit) in enumerate(steps):
-        arrived = swap(blocks, axis, bit)
+        with jax.named_scope(f"step_{number}"):
+            arrived = swap(blocks, axis, bit)
         if number == 0:
+            arrived, taps = after(arrived, taps)
+        elif number == 1:
             flat_shape = jax.ShapeDtypeStruct((2, taps.shape[0] * STRIDE, 128), jnp.float32)
-            arrived, flat = after(arrived, call(flat_kernel, flat_shape, [in_vmem])(taps))
-        elif number == 1:
+            flat = call(flat_kernel, "flat", flat_shape, [in_vmem])(taps)
             order_shape = jax.ShapeDtypeStruct((2 * half_rows, half_rows), jnp.bfloat16)
-            order = call(write_orders, order_shape, [])()
+            order = call(write_orders, "order", order_shape, [])()
             table_shape = jax.ShapeDtypeStruct((KS, KS, width, 2 * width), jnp.bfloat16)
-            table = call(functools.partial(table_kernel, order_x), table_shape, [in_vmem])(flat)
+            table = call(functools.partial(table_kernel, order_x), "table", table_shape, [in_vmem])(flat)
             arrived, table, order = after(arrived, table, order)
         elif number == 2:
             turned_shape = jax.ShapeDtypeStruct((2 * half_rows, width // 2), jnp.bfloat16)
             turn_fn = functools.partial(turn_kernel, half_x, sizes[1])
-            turned = call(turn_fn, turned_shape, [in_vmem] * 2)(blocks, order)
+            with jax.named_scope("turn_own"):
+                turned = call(turn_fn, "turn", turned_shape, [in_vmem] * 2)(blocks, order)
             turned_far = swap(turned, SPACE[2], 1)
             near_fn = functools.partial(near_kernel, local_z)
-            partial = call(near_fn, partial_shape, [in_vmem] * 2, scratch)(turned, table)
+            partial = call(near_fn, "near", partial_shape, [in_vmem] * 2, scratch)(turned, table)
             turned_far, partial = after(turned_far, partial)
             partial = more(False, True, turned_far, table, partial)
             arrived, turned, turned_far, partial = after(arrived, turned, turned_far, partial)
-            blocks = call(turn_fn, turned_shape, [in_vmem] * 2)(arrived, order)
+            blocks = call(turn_fn, "turn_other", turned_shape, [in_vmem] * 2)(arrived, order)
             continue
         elif number == 3:
             partial = more(True, False, blocks, table, partial)
@@ -374,6 +380,7 @@
     lined = pltpu.VMEM((local_x * channels * (local_y + 1), 128), jnp.float32)
     return call(
         grid_kernel,
+        "grid",
         jax.ShapeDtypeStruct(measured.shape, jnp.bfloat16),
         [in_vmem] * 9,
         scratch * 2 + [pltpu.VMEM((2, half_rows, width), jnp.bfloat16)] + [padded] * 4 + [lined],
@@ -460,7 +467,7 @@
     sampled = (sample_mask == 1)[None, None]
     current = jnp.where(sampled, measured, jnp.zeros_like(measured))
     tap_table = tap_matrix(kernel)
-    for _ in range(ITERS):
+    for iteration in range(ITERS):
         joined = jnp.concatenate([current, conjugate(mirror_state(current))], axis=1)
         padded = padded_2(joined, (("gx", 2), ("gy", 3), ("gz", 4)), reach)
         convolved = convolve(padded, tap_table)

time: 20.8 us -> 20.8 us (level)
  no operation moved by 1% of the time
where the time goes in v8:
time: 20.8 us; the launch traced here: 20.7 us
  Pallas kernels  10.2 us (49%)
  starting transfers between devices  8.04 us (39%)
  waiting for transfers between devices  1.2 us (6%)
  local copies, waits for them, and re-layouts  1.08 us (5%)
    ppermute x5, starting transfers between devices, swap(): return lax.ppermute(block, axis, [(i, i ^ bit) for i in range(count)])  8.04 us
    pallas_call x1, Pallas kernels, gathered_body(): call(grid_kernel, 'grid', jax.ShapeDtypeStruct(measured.shape, jnp.bfloat...  3.16 us
    pallas_call x2, Pallas kernels, more(): call(more_fn, 'more', partial_shape, [in_vmem] * 3, scratch)  2.19 us
    pallas_call x1, Pallas kernels, gathered_body(): call(functools.partial(table_kernel, order_x), 'table', table_shape, [in_...  1.34 us
    pallas_call x1, Pallas kernels, gathered_body(): call(near_fn, 'near', partial_shape, [in_vmem] * 2, scratch)(turned, table)  1.24 us
    ppermute x5, waiting for transfers between devices, swap(): return lax.ppermute(block, axis, [(i, i ^ bit) for i in range(count)])  1.2 us
    reshape x1, local copies, waits for them, and re-layouts, gathered_body(): jnp.moveaxis(kernel, 0, 3).reshape(parts * KS ** 3, coils * 2 * coils)  1.05 us
    pallas_call x1, Pallas kernels, gathered_body(): call(pack_kernel, 'pack', jax.ShapeDtypeStruct((local_x * channels, local...  1.04 us
  transfers between devices with their start and end apart: 5, of which 2 were waited for; matrix products, arithmetic and copies ran while one was open for 5% of the time, Pallas kernels for 27%

profile of v8, /device:TPU:0, one launch (start us, length us, event | category | flops | bytes accessed | tf_op | source)
XLA Modules:
  0.0 20.7 jit_solution(3086671254389303103)
XLA Ops:
  0.0 1.0 %pack.1 = bf16[64,128]{1,0:T(8,128)(2,1)S(1)} custom-call(bf16[2,16,2,8,16]{4,3,2,1,0:T(8,128)(2,1)} %measured_ref.1, s32[2,8,16]{2,1,0:T(8,128)} %mask_ref.1), custom_call_target="tpu_custom_call" | custom-call | bytes 4194304 | tf_op jit(solution)/shard_map/pack/pallas_call | solution.py:315
  1.1 4.1 %collective-permute-start = (bf16[1,64,128]{2,1,0:T(8,128)(2,1)S(1)}, bf16[1,64,128]{2,1,0:T(8,128)(2,1)S(1)}, u32[]{:S(2)}, u32[]{:S(2)}) collective-permute-start(bf16[1,64,128]{2,1,0:T(8,128)(2,1)S(1)} %bitcast.2), channel_id=1, source_target_pairs={{0,8},{4,12},{8,0},{12,4},{1,9},{5,13},{9,1},{13,5},{2,10},{6,14},... | collective-permute-start | bytes 49160 | tf_op jit(solution)/shard_map/step_0/ppermute | solution.py:289
  5.2 1.0 %reshape.3 = bf16[250,512]{1,0:T(8,128)(2,1)S(1)} reshape(bf16[5,5,5,2,512]{4,3,2,1,0:T(2,128)(2,1)} %bitcast.5) | data formatting | bytes 512000 | tf_op jit(solution)/shard_map/reshape | solution.py:331
  6.3 0.6 %collective-permute-done = bf16[1,64,128]{2,1,0:T(8,128)(2,1)S(1)} collective-permute-done((bf16[1,64,128]{2,1,0:T(8,128)(2,1)S(1)}, bf16[1,64,128]{2,1,0:T(8,128)(2,1)S(1)}, u32[]{:S(2)}, u32[]{:S(2)}) %collective-permute-start) | collective-permute-done | bytes 16416 | tf_op jit(solution)/shard_map/step_0/ppermute | solution.py:289
  6.9 1.9 %collective-permute-start.1 = (bf16[2,64,128]{2,1,0:T(8,128)(2,1)S(1)}, bf16[2,64,128]{2,1,0:T(8,128)(2,1)S(1)}, u32[]{:S(2)}, u32[]{:S(2)}) collective-permute-start(bf16[2,64,128]{2,1,0:T(8,128)(2,1)S(1)} %pad_maximum_fusion.1), channel_id=1, source_target_pairs={{0,2},{2,0},{1,3},{3,1},{4,6},{6,4},{5,7},{7,5},{8,10},{10,8},{9,1... | collective-permute-start | bytes 98312 | tf_op jit(solution)/shard_map/step_1/ppermute | solution.py:289
  8.8 0.7 %flat.1 = f32[2,4352,128]{2,1,0:T(8,128)S(1)} custom-call(bf16[256,512]{1,0:T(8,128)(2,1)S(1)} %pad.4.taps_ref), custom_call_target="tpu_custom_call" | custom-call | bytes 4194304 | tf_op jit(solution)/shard_map/flat/pallas_call | solution.py:355
  9.5 1.3 %table.1 = bf16[5,5,256,512]{3,2,1,0:T(8,128)(2,1)S(1)} custom-call(f32[2,4352,128]{2,1,0:T(8,128)S(1)} %flat.1), custom_call_target="tpu_custom_call" | custom-call | bytes 4194304 | tf_op jit(solution)/shard_map/table/pallas_call | solution.py:359
  10.9 0.0 collective-permute-done.1
  10.9 0.2 %turn.1.half.near_own = bf16[512,128]{1,0:T(8,128)(2,1)S(1)} custom-call(bf16[4,64,128]{2,1,0:T(8,128)(2,1)S(1)} %pad_maximum_fusion.blocks_ref, bf16[512,256]{1,0:T(8,128)(2,1)S(1)} %order.1), custom_call_target="tpu_custom_call" | custom-call | bytes 4194304 | tf_op jit(solution)/shard_map/turn_own/turn/pallas_call | solution.py:365
  11.2 0.1 collective-permute-start.3
  11.2 1.9 %collective-permute-start.2 = (bf16[4,64,128]{2,1,0:T(8,128)(2,1)S(1)}, bf16[4,64,128]{2,1,0:T(8,128)(2,1)S(1)}, u32[]{:S(2)}, u32[]{:S(2)}) collective-permute-start(bf16[4,64,128]{2,1,0:T(8,128)(2,1)S(1)} %pad_maximum_fusion.blocks_ref), channel_id=1, source_target_pairs={{0,4},{4,0},{8,12},{12,8},{1,5},{5,1},{9,13},{13,9},{2,6},{6,2},{1... | collective-permute-start | bytes 196616 | tf_op jit(solution)/shard_map/step_2/ppermute | solution.py:289
  13.1 1.2 %near.1.before = f32[2,5,256,256]{3,2,1,0:T(8,128)S(1)} custom-call(bf16[512,128]{1,0:T(8,128)(2,1)S(1)} %turn.1.half.near_own, bf16[5,5,256,512]{3,2,1,0:T(8,128)(2,1)S(1)} %table.1), custom_call_target="tpu_custom_call" | custom-call | bytes 4194304 | tf_op jit(solution)/shard_map/near/pallas_call | solution.py:368
  14.4 0.0 collective-permute-done.3.half.far_own
  14.4 0.9 %more.2.before = f32[2,5,256,256]{3,2,1,0:T(8,128)S(1)} custom-call(bf16[512,128]{1,0:T(8,128)(2,1)S(1)} %collective-permute-done.3.half.far_own, bf16[5,5,256,512]{3,2,1,0:T(8,128)(2,1)S(1)} %table.1, f32[2,5,256,256]{3,2,1,0:T(8,128)S(1)} %near.1.before), custom_call_target="tpu_custom_call" | custom-call | bytes 4194304 | tf_op jit(solution)/shard_map/more/pallas_call | solution.py:345
  15.3 0.5 %collective-permute-done.2.blocks_ref = bf16[4,64,128]{2,1,0:T(8,128)(2,1)S(1)} collective-permute-done((bf16[4,64,128]{2,1,0:T(8,128)(2,1)S(1)}, bf16[4,64,128]{2,1,0:T(8,128)(2,1)S(1)}, u32[]{:S(2)}, u32[]{:S(2)}) %collective-permute-start.2) | collective-permute-done | bytes 65568 | tf_op jit(solution)/shard_map/step_2/ppermute | solution.py:289
  15.8 0.2 %turn_other.1.half.near_other = bf16[512,128]{1,0:T(8,128)(2,1)S(1)} custom-call(bf16[4,64,128]{2,1,0:T(8,128)(2,1)S(1)} %collective-permute-done.2.blocks_ref, bf16[512,256]{1,0:T(8,128)(2,1)S(1)} %order.1), custom_call_target="tpu_custom_call" | custom-call | bytes 4194304 | tf_op jit(solution)/shard_map/turn_other/pallas_call | solution.py:372
  16.1 0.0 copy-start
  16.1 0.0 copy-start.1
  16.1 0.1 collective-permute-start.4
  16.2 1.3 %more.3.partial = f32[2,5,256,256]{3,2,1,0:T(8,128)S(1)} custom-call(bf16[512,128]{1,0:T(8,128)(2,1)S(1)} %turn_other.1.half.near_other, bf16[5,5,256,512]{3,2,1,0:T(8,128)(2,1)S(1)} %table.1, f32[2,5,256,256]{3,2,1,0:T(8,128)S(1)} %more.2.before), custom_call_target="tpu_custom_call" | custom-call | bytes 4194304 | tf_op jit(solution)/shard_map/more/pallas_call | solution.py:345
  17.5 0.0 collective-permute-done.4.far_other
  17.5 0.0 copy-done
  17.5 0.0 copy-done.1
  17.5 3.2 %grid.1 = bf16[2,16,2,8,16]{4,3,2,1,0:T(8,128)(2,1)} custom-call(bf16[512,128]{1,0:T(8,128)(2,1)S(1)} %turn.1.half.near_own, bf16[512,128]{1,0:T(8,128)(2,1)S(1)} %turn_other.1.half.near_other, bf16[512,128]{1,0:T(8,128)(2,1)S(1)} %collective-permute-done.3.half.far_own, bf16[512,128]{1,0:T(8,128)(2,1)S(1)} %collective-permute-done.4.far_other, ...), custom_call_target="tpu_custom_call" | custom-call | bytes 4194304 | tf_op jit(solution)/shard_map/grid/pallas_call | solution.py:381
  (4 shorter events, 0.1 us)
Async XLA Ops:
  1.1 5.8 %collective-permute-start = (bf16[1,64,128]{2,1,0:T(8,128)(2,1)S(1)}, bf16[1,64,128]{2,1,0:T(8,128)(2,1)S(1)}, u32[]{:S(2)}, u32[]{:S(2)}) collective-permute-start(bf16[1,64,128]{2,1,0:T(8,128)(2,1)S(1)} %bitcast.2), channel_id=1, source_target_pairs={{0,8},{4,12},{8,0},{12,4},{1,9},{5,13},{9,1},{13,5},{2,10},{6,14},... | collective-permute-start | bytes 49160 | tf_op jit(solution)/shard_map/step_0/ppermute | solution.py:289
  6.9 4.0 %collective-permute-start.1 = (bf16[2,64,128]{2,1,0:T(8,128)(2,1)S(1)}, bf16[2,64,128]{2,1,0:T(8,128)(2,1)S(1)}, u32[]{:S(2)}, u32[]{:S(2)}) collective-permute-start(bf16[2,64,128]{2,1,0:T(8,128)(2,1)S(1)} %pad_maximum_fusion.1), channel_id=1, source_target_pairs={{0,2},{2,0},{1,3},{3,1},{4,6},{6,4},{5,7},{7,5},{8,10},{10,8},{9,1... | collective-permute-start | bytes 98312 | tf_op jit(solution)/shard_map/step_1/ppermute | solution.py:289
  11.2 3.2 %collective-permute-start.3 = (bf16[512,128]{1,0:T(8,128)(2,1)S(1)}, bf16[512,128]{1,0:T(8,128)(2,1)S(1)}, u32[]{:S(2)}, u32[]{:S(2)}) collective-permute-start(bf16[512,128]{1,0:T(8,128)(2,1)S(1)} %turn.1.half.near_own), channel_id=1, source_target_pairs={{0,1},{1,0},{2,3},{3,2},{4,5},{5,4},{6,7},{7,6},{8,9},{9,8},{10,11... | collective-permute-start | bytes 393224 | tf_op jit(solution)/shard_map/ppermute | solution.py:289
  11.2 4.6 %collective-permute-start.2 = (bf16[4,64,128]{2,1,0:T(8,128)(2,1)S(1)}, bf16[4,64,128]{2,1,0:T(8,128)(2,1)S(1)}, u32[]{:S(2)}, u32[]{:S(2)}) collective-permute-start(bf16[4,64,128]{2,1,0:T(8,128)(2,1)S(1)} %pad_maximum_fusion.blocks_ref), channel_id=1, source_target_pairs={{0,4},{4,0},{8,12},{12,8},{1,5},{5,1},{9,13},{13,9},{2,6},{6,2},{1... | collective-permute-start | bytes 196616 | tf_op jit(solution)/shard_map/step_2/ppermute | solution.py:289
  16.1 1.4 %copy-start = (bf16[2,16,2,8,16]{4,3,2,1,0:T(8,128)(2,1)S(1)}, bf16[2,16,2,8,16]{4,3,2,1,0:T(8,128)(2,1)}, u32[]{:S(2)}) copy-start(bf16[2,16,2,8,16]{4,3,2,1,0:T(8,128)(2,1)} %measured_ref.1) | copy-start | bytes 49156
  16.1 1.4 %copy-start.1 = (s32[2,8,16]{2,1,0:T(8,128)S(1)}, s32[2,8,16]{2,1,0:T(8,128)}, u32[]{:S(2)}) copy-start(s32[2,8,16]{2,1,0:T(8,128)} %mask_ref.1) | copy-start | bytes 3076
  16.1 1.4 %collective-permute-start.4 = (bf16[512,128]{1,0:T(8,128)(2,1)S(1)}, bf16[512,128]{1,0:T(8,128)(2,1)S(1)}, u32[]{:S(2)}, u32[]{:S(2)}) collective-permute-start(bf16[512,128]{1,0:T(8,128)(2,1)S(1)} %turn_other.1.half.near_other), channel_id=1, source_target_pairs={{0,1},{1,0},{2,3},{3,2},{4,5},{5,4},{6,7},{7,6},{8,9},{9,8},{10,11... | collective-permute-start | bytes 393224 | tf_op jit(solution)/shard_map/step_3/ppermute | solution.py:289
